TPU v7x, 256 devices: a whole 4x4x8 slice. The times are simulated.
256 devices in a mesh: seq: 32 (over x, z), head: 8 (over y, core).
Axes of the slice: x: 4, y: 4, z: 8, core: 2. Of those that a mesh axis runs over, the one named last changes fastest.
Arguments:
- queries: bfloat16 [4096, 8192], P('seq', 'head'), may hold values from -250 to 250
- key_vectors: bfloat16 [4096, 1024], P('seq', 'head'), may hold values from -250 to 250
- value_vectors: bfloat16 [4096, 1024], P('seq', 'head'), may hold values from -20 to 20
- positions: int32 [4096], P('seq'), may hold values from 0 to 2047, as said below
- query_map: float32 [64, 128, 128], P('head'), may hold values from -0.5 to 0.5
- key_map: float32 [8, 128, 128], P('head'), may hold values from -0.5 to 0.5
Outputs:
- grad_queries: float32 [4096, 8192], P('seq', 'head')
- grad_keys: float32 [4096, 1024], P('seq', 'head')
- grad_values: float32 [4096, 1024], P('seq', 'head')
- query_map_grad: float32 [64, 128, 128], P('head')
- key_map_grad: float32 [8, 128, 128], P('head')
Inputs may be any that keep to these rules, and one draw needn't show every extreme that they name: positions[0] is 0, and each later position is either 0 (a document begins) or one more than the position before it; the slab holds at most 4 documents, and one of them is exactly 2048 tokens long.
All inputs are finite; a program needn't handle non-finite values.
Results may differ from a plain program's by a relative error of at most 0.0025.
Values may be sent and summed in bfloat16 or wider, within the bound.
No kernel may reach another device: no remote copies, remote signals or barrier semaphores. Data moves between devices by JAX's collectives and lax.ppermute only.
A program may use at most 64 MiB of HBM per device.

v0:
```python
import math

import jax
import jax.numpy as jnp
from jax import lax
from jax.sharding import PartitionSpec as P

HIGHEST = lax.Precision.HIGHEST
NEGATIVE = -1e30
epsilon = 1e-06


def entering(value, axis, join, neutral, backward):
    count, mine = (lax.axis_size(axis), lax.axis_index(axis))
    pieces = jax.tree.map(lambda part: lax.all_gather(part, axis), value)
    if backward:
        pieces = jax.tree.map(lambda part: part[::-1], pieces)
        mine = count - 1 - mine
    running = jax.tree.map(
        lambda part, zero: jnp.full_like(part, 0) + jnp.asarray(zero, part.dtype), value, neutral
    )

    def lap(position, running):
        longer = join(running, jax.tree.map(lambda part: part[position], pieces))
        return jax.tree.map(lambda new, old: jnp.where(position < mine, new, old), longer, running)

    return lax.fori_loop(0, count - 1, lap, running)


def feature_map(logits):
    return jnp.concatenate(
        [jax.nn.softmax(logits, axis=-1), jax.nn.softmax(-logits, axis=-1)], axis=-1
    )


def feature_back(phi, grad_phi, half_width):
    upper = phi[..., :half_width]
    lower = phi[..., half_width:]
    grad_up = grad_phi[..., :half_width]
    grad_low = grad_phi[..., half_width:]
    upper_part = upper * (grad_up - jnp.sum(upper * grad_up, axis=-1, keepdims=True))
    lower_part = lower * (grad_low - jnp.sum(lower * grad_low, axis=-1, keepdims=True))
    return upper_part - lower_part


def chain_states(earlier, later):
    carried = 1.0 - later[2]
    return (
        later[0] + carried * earlier[0],
        later[1] + carried * earlier[1],
        jnp.maximum(earlier[2], later[2]),
    )


def on_device(queries, key_vectors, value_vectors, positions, query_map, key_map):
    tok_rows = queries.shape[0]
    n_group = query_map.shape[0]
    head_dim = key_vectors.shape[1]
    half_width = query_map.shape[2]
    feat_width = 2 * half_width
    my_index = lax.axis_index("seq")
    row_base = my_index * tok_rows
    row_index = row_base + jnp.arange(tok_rows, dtype=jnp.int32)
    starts = row_index - positions
    last_start = starts[-1]
    q_heads = queries.reshape(tok_rows, n_group, head_dim)
    scaling = 1.0 / math.sqrt(head_dim)
    key_float = key_vectors.astype(jnp.float32)
    value_float = value_vectors.astype(jnp.float32)
    key_logits = jnp.dot(key_float, key_map[0], precision=HIGHEST)
    key_phi = feature_map(key_logits)
    initial = (
        jnp.full((n_group, tok_rows), NEGATIVE, jnp.float32),
        jnp.zeros((n_group, tok_rows), jnp.float32),
        jnp.zeros((n_group, tok_rows, head_dim), jnp.float32),
        jnp.zeros((feat_width, head_dim), jnp.float32),
        jnp.zeros((feat_width,), jnp.float32),
    )
    key_block = lax.all_gather(key_vectors, "seq", axis=0, tiled=True)
    value_block = lax.all_gather(value_vectors, "seq", axis=0, tiled=True)
    block_len = key_block.shape[0]
    key_index = jnp.arange(block_len, dtype=jnp.int32)
    visible = (key_index[None, :] <= row_index[:, None]) & (key_index[None, :] >= starts[:, None])

    def update(current):
        run_max, row_sum, summed, state_sum, norm_sums = current
        scores = (
            jnp.einsum("tgd,nd->gtn", q_heads, key_block, preferred_element_type=jnp.float32)
            * scaling
        )
        scores = jnp.where(visible[None], scores, NEGATIVE)
        new_max = jnp.maximum(run_max, jnp.max(scores, axis=-1))
        weights = jnp.where(visible[None], jnp.exp(scores - new_max[..., None]), 0.0)
        row_sum = jnp.sum(weights, axis=-1)
        summed = jnp.einsum(
            "gtn,nd->gtd",
            weights.astype(jnp.bfloat16),
            value_block,
            preferred_element_type=jnp.float32,
        )
        return (new_max, row_sum, summed, state_sum, norm_sums)

    run_max, row_sum, summed, state_sum, norm_sums = lax.cond(
        jnp.any(visible), update, lambda current: current, initial
    )
    held_teacher = jnp.transpose(summed / row_sum[..., None], (1, 0, 2))
    query_float = q_heads.astype(jnp.float32)
    query_logits = jnp.einsum("tgd,gdf->tgf", query_float, query_map, precision=HIGHEST)
    query_phi = feature_map(query_logits)
    visible_rows = (
        (row_index[None, :] <= row_index[:, None]) & (row_index[None, :] >= starts[:, None])
    ).astype(jnp.float32)
    crossing = (starts < row_base).astype(jnp.float32)
    keeping = (starts == last_start).astype(jnp.float32)
    fresh_doc = (last_start >= row_base).astype(jnp.float32).reshape(1)
    kept_phi = key_phi * keeping[:, None]
    state_local = jnp.dot(kept_phi.T, value_float, precision=HIGHEST)
    norms_local = jnp.sum(kept_phi, axis=0)
    state_in, norms_in, unused = entering(
        (state_local, norms_local, fresh_doc),
        "seq",
        chain_states,
        (jnp.zeros_like(state_local), jnp.zeros_like(norms_local), jnp.zeros((1,), jnp.float32)),
        False,
    )
    inner = jnp.einsum("tgf,jf->gtj", query_phi, key_phi, precision=HIGHEST) * visible_rows[None]
    numer = jnp.einsum("gtj,jd->tgd", inner, value_float, precision=HIGHEST)
    numer = numer + crossing[:, None, None] * jnp.einsum(
        "tgf,fd->tgd", query_phi, state_in, precision=HIGHEST
    )
    denom = jnp.sum(inner, axis=-1).T + crossing[:, None] * jnp.einsum(
        "tgf,f->tg", query_phi, norms_in, precision=HIGHEST
    )
    outputs = numer / denom[..., None]
    error = outputs - held_teacher
    grad_numer = error / denom[..., None]
    grad_denom = -jnp.sum(error * outputs, axis=-1) / denom
    mixing = (
        jnp.einsum("tgd,jd->gtj", grad_numer, value_float, precision=HIGHEST)
        + grad_denom.T[:, :, None]
    ) * visible_rows[None]
    grad_qphi = jnp.einsum("gtj,jf->tgf", mixing, key_phi, precision=HIGHEST)
    grad_qphi = grad_qphi + crossing[:, None, None] * (
        jnp.einsum("tgd,fd->tgf", grad_numer, state_in, precision=HIGHEST)
        + grad_denom[..., None] * norms_in
    )
    crossing_phi = query_phi * crossing[:, None, None]
    back_local = jnp.einsum("tgf,tgd->fd", crossing_phi, grad_numer, precision=HIGHEST)
    back_norms = jnp.einsum("tgf,tg->f", crossing_phi, grad_denom, precision=HIGHEST)
    back_in, back_norms_in, unused_flag = entering(
        (back_local, back_norms, fresh_doc),
        "seq",
        chain_states,
        (jnp.zeros_like(back_local), jnp.zeros_like(back_norms), jnp.zeros((1,), jnp.float32)),
        True,
    )
    grad_kphi = jnp.einsum("gtj,tgf->jf", mixing, query_phi, precision=HIGHEST)
    grad_kphi = grad_kphi + keeping[:, None] * (
        jnp.dot(value_float, back_in.T, precision=HIGHEST) + back_norms_in[None, :]
    )
    grad_values = jnp.einsum("gtj,tgd->jd", inner, grad_numer, precision=HIGHEST)
    grad_values = grad_values + keeping[:, None] * jnp.dot(key_phi, back_in, precision=HIGHEST)
    query_dlogit = feature_back(query_phi, grad_qphi, half_width)
    key_dlogit = feature_back(key_phi, grad_kphi, half_width)
    grad_queries = jnp.einsum("tgf,gdf->tgd", query_dlogit, query_map, precision=HIGHEST).reshape(
        tok_rows, n_group * head_dim
    )
    grad_keys = jnp.dot(key_dlogit, key_map[0].T, precision=HIGHEST)
    local_qmap = jnp.einsum("tgd,tgf->gdf", query_float, query_dlogit, precision=HIGHEST)
    local_kmap = jnp.dot(key_float.T, key_dlogit, precision=HIGHEST)[None]
    clip_limit = 0.25 * math.sqrt((n_group + 1) * lax.axis_size("head") * head_dim * half_width)
    summed_qmap, summed_kmap = lax.psum((local_qmap, local_kmap), "seq")
    squared = lax.psum(
        jnp.sum(summed_qmap * summed_qmap) + jnp.sum(summed_kmap * summed_kmap), "head"
    )
    factor = jnp.minimum(1.0, clip_limit / (jnp.sqrt(squared) + epsilon))
    query_map_grad = factor * summed_qmap
    key_map_grad = factor * summed_kmap
    return (grad_queries, grad_keys, grad_values, query_map_grad, key_map_grad)


def solution(mesh):
    placed = (
        P("seq", "head"),
        P("seq", "head"),
        P("seq", "head"),
        P("seq"),
        P("head", None, None),
        P("head", None, None),
    )
    return jax.shard_map(
        on_device,
        mesh=mesh,
        in_specs=placed,
        out_specs=(
            P("seq", "head"),
            P("seq", "head"),
            P("seq", "head"),
            P("head", None, None),
            P("head", None, None),
        ),
        check_vma=False,
    )
```

profile of v0, /device:TPU:1, one launch (start us, length us, event | category | flops | bytes accessed | tf_op | source)
XLA Modules:
  0.0 715.1 jit_solution(13117342215060472636)
XLA Ops:
  14.3 39.5 %all-gather.4 = f32[32,1,256]{2,1,0:T(1,128)S(1)} all-gather(f32[1,1,256]{2,1,0:T(1,128)S(1)} %bitcast.184), channel_id=3, replica_groups=mesh['seq'=32,'head'=8] {'seq'}, dimensions={0}, use_global_device_ids=true | all-gather | bytes 33792 | tf_op jit(solution)/shard_map/all_gather | solution.py:15
  53.8 1.8 copy.60
  59.4 57.9 %all-reduce = f32[32]{0:T(128)S(1)} all-reduce(f32[32]{0:T(128)S(1)} %dynamic-update-slice), channel_id=1, replica_groups=mesh['seq'=32,'head'=8] {'seq'}, use_global_device_ids=true, to_apply=%add | all-reduce | flops 32 | bytes 256
  120.7 2.0 convolution_bitcast_fusion.3
  122.7 39.8 %all-gather.13.cloned.1.call-done = bf16[4096,128]{1,0:T(8,128)(2,1)} async-done(((bf16[128,128]{1,0:T(8,128)(2,1)}), bf16[4096,128]{1,0:T(8,128)(2,1)}) %all-gather.13.cloned.1.call-update) | async-done | bytes 1048592 | tf_op jit(solution)/shard_map/all_gather | solution.py:80
  162.5 12.8 %conditional.1 = (f32[8,128]{1,0:T(8,128)S(1)}, f32[8,128,128]{1,2,0:T(8,128)}) conditional(s32[]{:T(128)} %convert_element_type.26, () %tuple.45, (pred[128,4096]{0,1:T(8,128)(4,1)S(1)}, bf16[4096,128]{1,0:T(8,128)(2,1)}, bf16[128,8,128]{0,2,1:T(8,128)(2,1)}, bf16[4096,128]{1,0:T(8,128)(2,1)}) %tuple.46), branch_computations={%region_13.14_spmd, %region_14.17_spmd} | conditional | flops 2202008576 | bytes 59007020 | solution.py:103
  162.5 3.8 fusion
  166.4 4.8 fusion.3
  171.2 4.0 fusion.2
  175.4 70.9 %all-gather.15.cloned.1.call-done = f32[8192,128]{1,0:T(8,128)} async-done(((f32[256,128]{1,0:T(8,128)}), f32[8192,128]{1,0:T(8,128)}) %all-gather.15.cloned.1.call-update) | async-done | bytes 4194320 | tf_op jit(solution)/shard_map/all_gather | solution.py:15
  246.3 90.0 %while.32 = (s32[]{:T(128)}, f32[256,128]{1,0:T(8,128)S(1)}, f32[256]{0:T(256)S(1)}, s32[]{:T(128)}, f32[32,256,128]{2,1,0:T(8,128)}, /*index=5*/f32[32,1]{0,1:T...) while((s32[]{:T(128)}, f32[256,128]{1,0:T(8,128)S(1)}, f32[256]{0:T(256)S(1)}, s32[]{:T(128)}, ...), condition=%wide.region_10.11_spmd.clone, body=%wide.region_9.10_spmd.clone.sunk | while | flops 132101 | bytes 398487 | solution.py:27
  247.6 1.6 fusion.106
  250.5 1.6 fusion.106
  253.4 1.6 fusion.106
  256.3 1.6 fusion.106
  259.2 1.6 fusion.106
  262.1 1.6 fusion.106
  265.0 1.6 fusion.106
  267.9 1.6 fusion.106
  270.8 1.6 fusion.106
  273.7 1.6 fusion.106
  276.6 1.6 fusion.106
  279.5 1.6 fusion.106
  282.4 1.6 fusion.106
  285.3 1.6 fusion.106
  288.2 1.6 fusion.106
  291.1 1.6 fusion.106
  294.0 1.6 fusion.106
  296.9 1.6 fusion.106
  299.8 1.6 fusion.106
  302.7 1.6 fusion.106
  305.6 1.6 fusion.106
  317.2 1.6 fusion.106
  320.1 1.6 fusion.106
  323.1 1.6 fusion.106
  326.0 1.6 fusion.106
  337.0 2.1 multiply_reduce_fusion.3
  339.0 1.7 convolution_bitcast_fusion.6
  341.8 32.8 %all-gather.5 = f32[32,1,256]{2,1,0:T(1,128)S(1)} all-gather(f32[1,1,256]{2,1,0:T(1,128)S(1)} %convolution_bitcast_fusion.10), channel_id=5, replica_groups=mesh['seq'=32,'head'=8] {'seq'}, dimensions={0}, use_global_device_ids=true | all-gather | bytes 33792 | tf_op jit(solution)/shard_map/all_gather | solution.py:15
  375.7 1.6 convolution_bitcast_fusion.7
  379.7 2.4 convolution_bitcast_fusion.1
  382.1 37.8 %all-gather.17.cloned.1.call-done = f32[8192,128]{1,0:T(8,128)} async-done(((f32[256,128]{1,0:T(8,128)}), f32[8192,128]{1,0:T(8,128)}) %all-gather.17.cloned.1.call-update) | async-done | bytes 4194320 | tf_op jit(solution)/shard_map/all_gather | solution.py:15
  419.9 4.6 rev.9
  424.5 109.9 %while.33 = (s32[]{:T(128)}, f32[256,128]{1,0:T(8,128)S(1)}, f32[256]{0:T(256)S(1)}, s32[]{:T(128)}, f32[32,256,128]{2,1,0:T(8,128)}, /*index=5*/f32[32,1]{0,1:T(1,128)S(1)}, f32[32,256]{1,0:T(8,128)}, s32[]{:T(128)}, s32[]{:T(128)}) while((s32[]{:T(128)}, f32[256,128]{1,0:T(8,128)S(1)}, f32[256]{0:T(256)S(1)}, s32[]{:T(128)}, ...), condition=%wide.region_21.22_spmd.clone, body=%wide.region_20.21_spmd.clone.sunk | while | flops 132101 | bytes 398487 | solution.py:27
  540.4 139.9 %all-reduce.4.cloned.1.call-done = (f32[8,128,128]{1,2,0:T(8,128)}, f32[1,128,128]{1,2,0:T(8,128)}) async-done(((f32[8,128,128]{1,2,0:T(8,128)}, f32[1,128,128]{1,2,0:T(8,128)}), (f32[8,128,128]{1,2,0:T(8,128)}, f32[1,128,128]{1,2,0:T(8,128)})) %all-reduce.4.cloned.1.call-update) | async-done | bytes 589840 | tf_op jit(solution)/shard_map/psum | solution.py:172
  681.7 1.8 multiply_reduce_fusion
  684.8 1.8 fusion.44
  686.6 17.6 %psum.23 = f32[]{:T(128)} all-reduce(f32[]{:T(128)S(6)} %add.151), channel_id=1, replica_groups=mesh['seq'=32,'head'=8] {'head'}, use_global_device_ids=true, to_apply=%region_28.29 | all-reduce | flops 1 | bytes 8 | tf_op jit(solution)/shard_map/psum | solution.py:173
  (291 shorter events, 186.8 us)
Async XLA Ops:
  7.2 110.2 %copy-start = (f32[8,128,128]{2,1,0:T(8,128)S(1)}, f32[8,128,128]{2,1,0:T(8,128)}, u32[]{:S(2)}) copy-start(f32[8,128,128]{2,1,0:T(8,128)} %param.16) | copy-start | bytes 1572868
  7.2 115.5 %all-gather.11.cloned.1.call-start = ((), (), s32[]{:S(2)}) async-start(), calls=%async_computation | async-start | bytes 1081344 | tf_op jit(solution)/shard_map/all_gather | solution.py:79
  7.9 154.6 %all-gather.13.cloned.1.call-start = ((), (), s32[]{:S(2)}) async-start(), calls=%async_computation.1 | async-start | bytes 1081344 | tf_op jit(solution)/shard_map/all_gather | solution.py:80
  8.7 237.7 %all-gather.15.cloned.1.call-start = ((), (), s32[]{:S(2)}) async-start(), calls=%async_computation.2 | async-start | bytes 4325376 | tf_op jit(solution)/shard_map/all_gather | solution.py:15
  13.5 406.4 %all-gather.17.cloned.1.call-start = ((), (), s32[]{:S(2)}) async-start(), calls=%async_computation.3 | async-start | bytes 4325376 | tf_op jit(solution)/shard_map/all_gather | solution.py:15
  162.5 212.7 %copy-start.1 = (bf16[128,128]{1,0:T(8,128)(2,1)S(1)}, bf16[128,128]{1,0:T(8,128)(2,1)}, u32[]{:S(2)}) copy-start(bf16[128,128]{1,0:T(8,128)(2,1)} %param.14) | copy-start | bytes 98308
  162.5 3.8 copy-start.2
  340.7 339.6 %all-reduce.4.cloned.1.call-start = ((), (), s32[]{:S(2)}) async-start(), calls=%async_computation.4 | async-start | bytes 1179648 | tf_op jit(solution)/shard_map/psum | solution.py:172
Sparse Core Ops, SparseCore 0:
  10.6 75.4 all-gather.10
  88.7 73.7 all-gather.12
  165.1 81.1 all-gather.14
  340.8 79.0 all-gather.16
  537.3 142.9 all-reduce.3
where the time goes:
time: 720 us; the launch traced here: 715 us
  waiting for transfers between devices  290 us (40%)
  other arithmetic  190 us (26%)
  blocking collectives  148 us (21%)
  local copies, waits for them, and re-layouts  34.3 us (5%)
  matrix products  34.1 us (5%)
  between operations  17.4 us (2%)
    psum x1, waiting for transfers between devices, on_device(): summed_qmap, summed_kmap = lax.psum((local_qmap, local_kmap), 'seq')  140 us
    select_n x124, other arithmetic, lap(): jnp.where(position < mine, new, old)  140 us
    all_gather x2, waiting for transfers between devices, entering(): pieces = jax.tree.map(lambda part: lax.all_gather(part, axis), value)  109 us
    all_gather x2, blocking collectives, entering(): pieces = jax.tree.map(lambda part: lax.all_gather(part, axis), value)  72.3 us
    unnamed x1, blocking collectives  57.9 us
    all_gather x1, waiting for transfers between devices, on_device(): value_block = lax.all_gather(value_vectors, 'seq', axis=0, tiled=True)  39.8 us
    sub x62, other arithmetic, chain_states(): carried = 1.0 - later[2]  36.6 us
    dynamic_slice x62, local copies, waits for them, and re-layouts, lap(): longer = join(running, jax.tree.map(lambda part: part[position], pieces))  21.9 us
  transfers between devices with their start and end apart: 5, of which 4 were waited for; matrix products, arithmetic and copies ran while one was open for 6% of the time, Pallas kernels for 0%

commit v1 on v0

v1 whole, which is shorter than its diff:
```python
import functools
import math

import jax
import jax.numpy as jnp
from jax import lax
from jax.experimental import pallas as pl
from jax.experimental.pallas import tpu as pltpu
from jax.sharding import PartitionSpec as P

F32 = jnp.float32
BF16 = jnp.bfloat16
NEGATIVE = -1e30
EPSILON = 1e-06
T = 128
WINDOW = 16
KEYS = (WINDOW + 1) * T
PER_STEP = 2
ROWS = PER_STEP * T
PIECE = 48
STATE_ROW, KMAP_ROW, NORM_ROW, INFO_ROW = 32, 40, 44, 46


def nn(a, b):
    return lax.dot_general(a, b, (((1,), (0,)), ((), ())), preferred_element_type=F32)


def nt(a, b):
    return lax.dot_general(a, b, (((1,), (1,)), ((), ())), preferred_element_type=F32)


def tn(a, b):
    return lax.dot_general(a, b, (((0,), (0,)), ((), ())), preferred_element_type=F32)


def split2(x):
    high = x.astype(BF16)
    return high, (x - high.astype(F32)).astype(BF16)


def split3(x):
    high = x.astype(BF16)
    rest = x - high.astype(F32)
    middle = rest.astype(BF16)
    return high, middle, (rest - middle.astype(F32)).astype(BF16)


def product(form, a, b):
    return form(a[0], b[0]) + (form(a[0], b[1]) + form(a[1], b[0]))


def exact_left(form, a, parts):
    total = form(a, parts[-1])
    for part in parts[-2::-1]:
        total = total + form(a, part)
    return total


def exact_right(form, parts, b):
    return form(parts[0], b) + form(parts[1], b)


def feature_map(logits):
    upper = jnp.exp(logits - jnp.max(logits, axis=-1, keepdims=True))
    lower = jnp.exp(jnp.min(logits, axis=-1, keepdims=True) - logits)
    upper = upper * (1.0 / jnp.sum(upper, axis=-1, keepdims=True))
    lower = lower * (1.0 / jnp.sum(lower, axis=-1, keepdims=True))
    return upper, lower


def feature_back(phi, grad):
    upper, lower = phi[:, :T], phi[:, T:]
    up, low = grad[:, :T], grad[:, T:]
    up = upper * (up - jnp.sum(upper * up, axis=-1, keepdims=True))
    low = lower * (low - jnp.sum(lower * low, axis=-1, keepdims=True))
    return up - low


def column_of(row):
    i = lax.broadcasted_iota(jnp.int32, (T, T), 0)
    j = lax.broadcasted_iota(jnp.int32, (T, T), 1)
    return jnp.sum(jnp.where(i == j, row, 0.0), axis=1, keepdims=True)


def main_kernel(
    places,
    pos_ref,
    q_ref,
    qmap_ref,
    kmap_ref,
    *rest,
):
    count = len(places)
    blocks = rest[:count]
    gq_ref, payload_ref, phi_ref, gkphi_ref, gv_ref = rest[count : count + 5]
    k_s, v_s, phi_s, bias_s, s_s, n_s, back_s, backn_s = rest[count + 5 :]
    step = pl.program_id(0)
    last = pl.num_programs(0) - 1
    pos = column_of(pos_ref[...].astype(F32))
    row = lax.broadcasted_iota(jnp.int32, (T, 1), 0).astype(F32)
    start = row - pos
    crossing = (start < 0.0).astype(F32)
    entry = -pos_ref[0:1, 0:1].astype(F32)

    @pl.when(step == 0)
    def _():
        for ref, held in zip(blocks, places):
            for slot, block in enumerate(held):
                at = (WINDOW - block) * T
                k_s[at : at + T, :] = ref[slot * 2 * T : slot * 2 * T + T, :]
                v_s[at : at + T, :] = ref[slot * 2 * T + T : slot * 2 * T + 2 * T, :]
        key = lax.broadcasted_iota(jnp.int32, (T, KEYS), 1).astype(F32) - float(WINDOW * T)
        bias_s[...] = jnp.where((key <= row) & (key >= start), 0.0, NEGATIVE)
        map_parts = split3(kmap_ref[0])
        s_s[...] = jnp.zeros_like(s_s)
        n_s[...] = jnp.zeros_like(n_s)
        back_s[...] = jnp.zeros_like(back_s)
        backn_s[...] = jnp.zeros_like(backn_s)
        gkphi_ref[...] = jnp.zeros_like(gkphi_ref)
        gv_ref[...] = jnp.zeros_like(gv_ref)

        def features(at):
            logits = exact_left(nn, k_s[pl.ds(at, T), :], map_parts)
            return jnp.concatenate(feature_map(logits), axis=1)

        def lap(block, carry):
            at = pl.multiple_of(block * T, T)
            key_row = row + (at - WINDOW * T).astype(F32)
            phi = jnp.where(key_row >= entry, features(at), 0.0)
            phi_s[pl.ds(at, T), :] = phi
            s_s[...] += exact_right(tn, split2(phi), v_s[pl.ds(at, T), :])
            n_s[...] += jnp.sum(phi, axis=0, keepdims=True)
            return carry

        lax.fori_loop(0, WINDOW, lap, 0)
        own = features(WINDOW * T)
        phi_s[WINDOW * T :, :] = own
        phi_ref[...] = own

    both = lambda x: jnp.concatenate([x] * PER_STEP, axis=0)
    cross = both(crossing)
    own_v = v_s[WINDOW * T :, :]
    own_phi = split2(phi_s[WINDOW * T :, :])
    state = split2(s_s[...])
    norms = n_s[...]
    bias = bias_s[...]
    seen = both((bias[:, WINDOW * T :] == 0.0).astype(F32))

    heads = [q_ref[:, i * T : (i + 1) * T] for i in range(PER_STEP)]
    queries = jnp.concatenate(heads, axis=0)
    scores = nt(queries, k_s[...]) * (1.0 / math.sqrt(T)) + both(bias)
    weights = jnp.exp(scores - jnp.max(scores, axis=-1, keepdims=True))
    total = jnp.sum(weights, axis=-1, keepdims=True)
    teacher = nn(weights.astype(BF16), v_s[...]) / total
    logits = jnp.concatenate(
        [exact_left(nn, heads[i], split3(qmap_ref[i])) for i in range(PER_STEP)], axis=0
    )
    phi = jnp.concatenate(feature_map(logits), axis=1)
    phi_parts = split2(phi)
    inner = product(nt, phi_parts, own_phi) * seen
    inner_parts = split2(inner)
    numer = exact_right(nn, inner_parts, own_v) + cross * product(nn, phi_parts, state)
    denom = jnp.sum(inner, axis=-1, keepdims=True) + cross * jnp.sum(
        phi * norms, axis=-1, keepdims=True
    )
    outputs = numer / denom
    error = outputs - teacher
    grad_numer = error / denom
    grad_denom = -jnp.sum(error * outputs, axis=-1, keepdims=True) / denom
    numer_parts = split2(grad_numer)
    far_numer = cross * grad_numer
    far_parts = split2(far_numer)
    far_denom = cross * grad_denom
    mixing = (exact_right(nt, numer_parts, own_v) + grad_denom) * seen
    mixing_parts = split2(mixing)
    grad_phi = (
        product(nn, mixing_parts, own_phi) + product(nt, far_parts, state) + far_denom * norms
    )
    back_s[...] += product(tn, phi_parts, far_parts)
    backn_s[...] += jnp.sum(phi * far_denom, axis=0, keepdims=True)
    gkphi_ref[...] += product(tn, mixing_parts, phi_parts)
    gv_ref[...] += product(tn, inner_parts, numer_parts)
    dlogit = feature_back(phi, grad_phi)
    for i in range(PER_STEP):
        part = split2(dlogit[i * T : (i + 1) * T, :])
        gq_ref[:, i * T : (i + 1) * T] = product(nt, part, split2(qmap_ref[i]))
        grad_map = exact_left(tn, heads[i], part)
        for quarter in range(4):
            payload_ref[step * (4 * PER_STEP) + 4 * i + quarter, 0:STATE_ROW, :] = grad_map[
                quarter * 32 : quarter * 32 + 32, :
            ]

    @pl.when(step == last)
    def _():
        back = back_s[...]
        back_parts = split2(back)
        backn = backn_s[...]
        for piece in range(32):
            payload_ref[piece, STATE_ROW : STATE_ROW + 8, :] = back[piece * 8 : piece * 8 + 8, :]

        def lap(block, total):
            at = pl.multiple_of(block * T, T)
            grad = exact_left(nt, v_s[pl.ds(at, T), :], back_parts) + backn
            part = split2(feature_back(phi_s[pl.ds(at, T), :], grad))
            return total + exact_left(tn, k_s[pl.ds(at, T), :], part)

        own = split2(feature_back(phi_s[WINDOW * T :, :], gkphi_ref[...]))
        grad_map = lax.fori_loop(0, WINDOW, lap, exact_left(tn, k_s[WINDOW * T :, :], own))
        tail = jnp.concatenate(
            [
                backn[:, :T],
                backn[:, T:],
                jnp.broadcast_to(pos_ref[0:1, 0:1].astype(F32), (1, T)),
                jnp.zeros((1, T), F32),
            ],
            axis=0,
        )
        for piece in range(32):
            payload_ref[piece, KMAP_ROW:PIECE, :] = jnp.concatenate(
                [grad_map[piece * 4 : piece * 4 + 4, :], tail], axis=0
            )


def middle_kernel(me_ref, got_ref, out_ref, norms_ref):
    pieces = got_ref.shape[0]
    total = got_ref[0]
    for i in range(1, pieces):
        total = total + got_ref[i]
    squares = jnp.sum(total[0:STATE_ROW, :] * total[0:STATE_ROW, :]) + jnp.sum(
        total[KMAP_ROW:NORM_ROW, :] * total[KMAP_ROW:NORM_ROW, :]
    )
    tail = jnp.concatenate(
        [total[KMAP_ROW:INFO_ROW, :], jnp.full((2, T), squares, F32)], axis=0
    )
    for j in range(pieces):
        out_ref[j, 0:STATE_ROW, :] = total[0:STATE_ROW, :]
        out_ref[j, KMAP_ROW:PIECE, :] = tail
    sender = lax.broadcasted_iota(jnp.int32, (pieces, T), 0)
    target = lax.broadcasted_iota(jnp.int32, (pieces, T), 1)
    first = (sender * T).astype(F32) - got_ref[:, INFO_ROW, :]
    links = (sender > target) & (first <= (target * T + (T - 1)).astype(F32))
    reach = links.astype(F32)[:, :pieces].astype(BF16)
    for i in range(8):
        high, middle, low = split3(got_ref[:, STATE_ROW + i, :])
        out_ref[:, STATE_ROW + i, :] = tn(reach, high) + (tn(reach, middle) + tn(reach, low))
    me = me_ref[0]
    mine = (sender > me) & (first <= (me * T + (T - 1)).astype(F32))
    for half in range(2):
        norms_ref[0:1, half * T : half * T + T] = jnp.sum(
            jnp.where(mine, got_ref[:, NORM_ROW + half, :], 0.0), axis=0, keepdims=True
        )


def last_kernel(pos_ref, got_ref, norms_ref, kv_ref, kmap_ref, phi_ref, gkphi_ref, gv_ref, gk_ref, gvo_ref):
    pos = column_of(pos_ref[...].astype(F32))
    row = lax.broadcasted_iota(jnp.int32, (T, 1), 0).astype(F32)
    start = row - pos
    last_start = float(T - 1) - pos_ref[0:1, T - 1 : T].astype(F32)
    keeping = (start == last_start).astype(F32)
    pieces = got_ref.shape[0]
    back = split2(
        jnp.concatenate([got_ref[r, STATE_ROW : STATE_ROW + 8, :] for r in range(pieces)], axis=0)
    )
    phi = phi_ref[...]
    own_v = kv_ref[T:, :]
    grad = gkphi_ref[...] + keeping * (exact_left(nt, own_v, back) + norms_ref[...])
    gvo_ref[...] = gv_ref[...] + keeping * product(nn, split2(phi), back)
    gk_ref[...] = product(nt, split2(feature_back(phi, grad)), split2(kmap_ref[0]))


def vmem(count):
    return [pl.BlockSpec(memory_space=pltpu.VMEM)] * count


def window_of(kv):
    n = lax.axis_size("seq")

    def shift(x, k):
        return lax.ppermute(x, "seq", [(i, (i + k) % n) for i in range(n)])

    r8 = shift(kv, 8)
    r16 = shift(r8, 8)
    ahead = jnp.concatenate([kv, r8], axis=0)
    behind = jnp.concatenate([r8, r16], axis=0)
    f1, b1 = shift(ahead, 1), shift(behind, -1)
    f2, b2 = shift(f1, 1), shift(b1, -1)
    f3, b3 = shift(f2, 1), shift(b2, -1)
    f4, b4 = shift(f3[: 2 * T], 1), shift(b3[2 * T :], -1)
    arrays = [kv, r8, r16, f1, b1, f2, b2, f3, b3, f4, b4]
    places = [(0,), (8,), (16,), (1, 9), (7, 15), (2, 10), (6, 14), (3, 11), (5, 13), (4,), (12,)]
    return arrays, places


def on_device(queries, key_vectors, value_vectors, positions, query_map, key_map):
    group = query_map.shape[0]
    pieces = lax.axis_size("seq")
    me = lax.axis_index("seq").astype(jnp.int32).reshape(1)
    pos = positions.reshape(1, T)
    kv = jnp.concatenate([key_vectors, value_vectors], axis=0)
    arrays, places = window_of(kv)
    sds = jax.ShapeDtypeStruct
    whole = lambda *shape: pl.BlockSpec(shape, lambda h: (0,) * len(shape))
    grad_queries, payload, phi, gkphi, gv = pl.pallas_call(
        functools.partial(main_kernel, places),
        grid=(group // PER_STEP,),
        in_specs=[
            whole(1, T),
            pl.BlockSpec((T, ROWS), lambda h: (0, h)),
            pl.BlockSpec((PER_STEP, T, T), lambda h: (h, 0, 0)),
            whole(1, T, T),
        ]
        + [whole(*a.shape) for a in arrays],
        out_specs=[
            pl.BlockSpec((T, ROWS), lambda h: (0, h)),
            whole(pieces, PIECE, T),
            whole(T, 2 * T),
            whole(T, 2 * T),
            whole(T, T),
        ],
        out_shape=[
            sds((T, group * T), F32),
            sds((pieces, PIECE, T), F32),
            sds((T, 2 * T), F32),
            sds((T, 2 * T), F32),
            sds((T, T), F32),
        ],
        scratch_shapes=[
            pltpu.VMEM((KEYS, T), BF16),
            pltpu.VMEM((KEYS, T), BF16),
            pltpu.VMEM((KEYS, 2 * T), F32),
            pltpu.VMEM((T, KEYS), F32),
            pltpu.VMEM((2 * T, T), F32),
            pltpu.VMEM((1, 2 * T), F32),
            pltpu.VMEM((2 * T, T), F32),
            pltpu.VMEM((1, 2 * T), F32),
        ],
        compiler_params=pltpu.CompilerParams(vmem_limit_bytes=48 << 20),
        name="attention_transfer",
    )(pos, queries, query_map, key_map, *arrays)

    gathered = lax.all_to_all(payload, "seq", 0, 0)
    reduced, norms = pl.pallas_call(
        middle_kernel,
        in_specs=[pl.BlockSpec(memory_space=pltpu.SMEM)] + vmem(1),
        out_specs=vmem(2),
        out_shape=[sds((pieces, PIECE, T), F32), sds((1, 2 * T), F32)],
        compiler_params=pltpu.CompilerParams(vmem_limit_bytes=32 << 20),
        name="sum_pieces",
    )(me, gathered)
    back = lax.all_to_all(reduced, "seq", 0, 0)
    squares = jnp.sum(back[:, INFO_ROW, 0])
    heads = lax.axis_size("head")
    squared = jnp.sum(lax.all_to_all(jnp.broadcast_to(squares, (heads, 8, T)), "head", 0, 0)[:, 0, 0])
    grad_keys, grad_values = pl.pallas_call(
        last_kernel,
        in_specs=vmem(8),
        out_specs=vmem(2),
        out_shape=[sds((T, T), F32), sds((T, T), F32)],
        compiler_params=pltpu.CompilerParams(vmem_limit_bytes=32 << 20),
        name="key_gradients",
    )(pos, back, norms, kv, key_map, phi, gkphi, gv)
    clip_limit = 0.25 * math.sqrt((group + 1) * heads * T * T)
    factor = jnp.minimum(1.0, clip_limit / (jnp.sqrt(squared) + EPSILON))
    query_map_grad = factor * back[:, :STATE_ROW, :].reshape(group, T, T)
    key_map_grad = factor * back[:, KMAP_ROW:NORM_ROW, :].reshape(1, T, T)
    return (grad_queries, grad_keys, grad_values, query_map_grad, key_map_grad)


def solution(mesh):
    placed = (
        P("seq", "head"),
        P("seq", "head"),
        P("seq", "head"),
        P("seq"),
        P("head", None, None),
        P("head", None, None),
    )
    return jax.shard_map(
        on_device,
        mesh=mesh,
        in_specs=placed,
        out_specs=(
            P("seq", "head"),
            P("seq", "head"),
            P("seq", "head"),
            P("head", None, None),
            P("head", None, None),
        ),
        check_vma=False,
    )
```

time: 720 us -> 140 us (0.19)
  waiting for transfers between devices: 290 us -> 34.6 us
  other arithmetic: 190 us -> 3.54 us
  blocking collectives: 148 us -> 19.6 us
  starting transfers between devices: 0.2 us -> 43.9 us
  matrix products: 34.1 us -> 0 us
  Pallas kernels: 0 us -> 33.4 us
  local copies, waits for them, and re-layouts: 34.3 us -> 2.88 us
  between operations: 17.4 us -> 1.47 us
    all_gather x4 -> x0, waiting for transfers between devices: 149 us -> none  [the longest x2 109 us: entering(): pieces = jax.tree.map(lambda part: lax.all_gather(part, axis), value)]
    psum x1 -> x0, waiting for transfers between devices: 140 us -> none  [on_device(): summed_qmap, summed_kmap = lax.psum((local_qmap, local_kmap), 'seq')]
    select_n x124 -> x0, other arithmetic: 140 us -> none  [lap(): jnp.where(position < mine, new, old)]
    all_gather x2 -> x0, blocking collectives: 72.3 us -> none  [entering(): pieces = jax.tree.map(lambda part: lax.all_gather(part, axis), value)]
    unnamed x1 -> x0, blocking collectives: 57.9 us -> none
    sub x66 -> x0, other arithmetic: 37.7 us -> none  [the longest x62 36.6 us: chain_states(): carried = 1.0 - later[2]]
    pallas_call x0 -> x3, Pallas kernels: none -> 33.4 us  [the longest x1 31.6 us: on_device(): pl.pallas_call(functools.partial(main_kernel, places), grid=(group // PER...]
    dot_general x21 -> x0, matrix products: 29.3 us -> none  [the longest x1 3.83 us: update(): jnp.einsum('tgd,nd->gtn', q_heads, key_block, preferred_element_type=jnp....]
  transfers between devices with their start and end apart: 5 -> 12, of which waited for: 4 -> 8; matrix products, arithmetic and copies ran while one was open for 6% -> 0% of each run, Pallas kernels for 0% -> 1%
where the time goes in v1:
time: 140 us; the launch traced here: 139 us
  starting transfers between devices  43.9 us (31%)
  waiting for transfers between devices  34.6 us (25%)
  Pallas kernels  33.4 us (24%)
  blocking collectives  19.6 us (14%)
  other arithmetic  3.54 us (3%)
  local copies, waits for them, and re-layouts  2.88 us (2%)
  between operations  1.47 us (1%)
    pallas_call x1, Pallas kernels, on_device(): pl.pallas_call(functools.partial(main_kernel, places), grid=(group // PER...  31.6 us
    ppermute x10, starting transfers between devices, shift(): return lax.ppermute(x, 'seq', [(i, (i + k) % n) for i in range(n)])  22.8 us
    all_to_all x1, blocking collectives, on_device(): back = lax.all_to_all(reduced, 'seq', 0, 0)  19.6 us
    ppermute x10, waiting for transfers between devices, shift(): return lax.ppermute(x, 'seq', [(i, (i + k) % n) for i in range(n)])  16.2 us
    all_to_all x1, waiting for transfers between devices, on_device(): gathered = lax.all_to_all(payload, 'seq', 0, 0)  14.7 us
    all_to_all x1, starting transfers between devices, on_device(): lax.all_to_all(jnp.broadcast_to(squares, (heads, 8, T)), 'head', 0, 0)  14.4 us
    all_to_all x1, starting transfers between devices, on_device(): gathered = lax.all_to_all(payload, 'seq', 0, 0)  6.73 us
    all_to_all x1, waiting for transfers between devices, on_device(): lax.all_to_all(jnp.broadcast_to(squares, (heads, 8, T)), 'head', 0, 0)  3.65 us
  transfers between devices with their start and end apart: 12, of which 8 were waited for; matrix products, arithmetic and copies ran while one was open for 0% of the time, Pallas kernels for 1%

profile of v1, /device:TPU:1, one launch (start us, length us, event | category | flops | bytes accessed | tf_op | source)
XLA Modules:
  0.0 139.3 jit_solution(3697382297079725300)
XLA Ops:
  0.6 0.0 copy-start
  0.6 0.8 constant_dynamic-update-slice_fusion.1
  1.5 0.8 constant_dynamic-update-slice_fusion.rest_0_.kv_ref
  2.2 0.0 copy-start.1
  2.2 2.0 %collective-permute-start = (bf16[256,128]{1,0:T(8,128)(2,1)S(1)}, bf16[256,128]{1,0:T(8,128)(2,1)S(1)}, u32[]{:S(2)}, u32[]{:S(2)}) collective-permute-start(bf16[256,128]{1,0:T(8,128)(2,1)S(1)} %constant_dynamic-update-slice_fusion.rest_0_.kv_ref), channel_id=1, source_target_pairs={{0,64},{8,72},{16,80},{24,88},{32,96},{40,104},{48,112},{56,120},{... | collective-permute-start | bytes 196616 | tf_op jit(solution)/shard_map/ppermute | solution.py:279
  4.3 2.9 %collective-permute-done.rest_1_ = bf16[256,128]{1,0:T(8,128)(2,1)S(1)} collective-permute-done((bf16[256,128]{1,0:T(8,128)(2,1)S(1)}, bf16[256,128]{1,0:T(8,128)(2,1)S(1)}, u32[]{:S(2)}, u32[]{:S(2)}) %collective-permute-start) | collective-permute-done | bytes 65568 | tf_op jit(solution)/shard_map/ppermute | solution.py:279
  7.2 0.2 collective-permute-start.1
  7.4 4.1 %collective-permute-done.1.rest_2_ = bf16[256,128]{1,0:T(8,128)(2,1)S(1)} collective-permute-done((bf16[256,128]{1,0:T(8,128)(2,1)S(1)}, bf16[256,128]{1,0:T(8,128)(2,1)S(1)}, u32[]{:S(2)}, u32[]{:S(2)}) %collective-permute-start.1) | collective-permute-done | bytes 65568 | tf_op jit(solution)/shard_map/ppermute | solution.py:279
  11.5 0.8 pad_maximum_fusion.1
  12.3 1.9 %collective-permute-start.2 = (bf16[512,128]{1,0:T(8,128)(2,1)S(1)}, bf16[512,128]{1,0:T(8,128)(2,1)S(1)}, u32[]{:S(2)}, u32[]{:S(2)}) collective-permute-start(bf16[512,128]{1,0:T(8,128)(2,1)S(1)} %get-tuple-element.24), channel_id=1, source_target_pairs={{0,8},{8,16},{16,24},{24,32},{32,40},{40,48},{48,56},{56,64},{64,7... | collective-permute-start | bytes 393224 | tf_op jit(solution)/shard_map/ppermute | solution.py:279
  14.2 3.8 %collective-permute-start.3 = (bf16[512,128]{1,0:T(8,128)(2,1)S(1)}, bf16[512,128]{1,0:T(8,128)(2,1)S(1)}, u32[]{:S(2)}, u32[]{:S(2)}) collective-permute-start(bf16[512,128]{1,0:T(8,128)(2,1)S(1)} %get-tuple-element.23), channel_id=1, source_target_pairs={{0,248},{8,0},{16,8},{24,16},{32,24},{40,32},{48,40},{56,48},{64,5... | collective-permute-start | bytes 393224 | tf_op jit(solution)/shard_map/ppermute | solution.py:279
  18.0 2.3 %collective-permute-done.2.rest_3_ = bf16[512,128]{1,0:T(8,128)(2,1)S(1)} collective-permute-done((bf16[512,128]{1,0:T(8,128)(2,1)S(1)}, bf16[512,128]{1,0:T(8,128)(2,1)S(1)}, u32[]{:S(2)}, u32[]{:S(2)}) %collective-permute-start.2) | collective-permute-done | bytes 131104 | tf_op jit(solution)/shard_map/ppermute | solution.py:279
  20.3 0.0 collective-permute-start.4
  20.3 0.0 collective-permute-done.3.rest_4_
  20.3 4.9 %collective-permute-start.5 = (bf16[512,128]{1,0:T(8,128)(2,1)S(1)}, bf16[512,128]{1,0:T(8,128)(2,1)S(1)}, u32[]{:S(2)}, u32[]{:S(2)}) collective-permute-start(bf16[512,128]{1,0:T(8,128)(2,1)S(1)} %collective-permute-done.3.rest_4_), channel_id=1, source_target_pairs={{0,248},{8,0},{16,8},{24,16},{32,24},{40,32},{48,40},{56,48},{64,5... | collective-permute-start | bytes 393224 | tf_op jit(solution)/shard_map/ppermute | solution.py:279
  25.2 2.3 %collective-permute-done.4.rest_5_ = bf16[512,128]{1,0:T(8,128)(2,1)S(1)} collective-permute-done((bf16[512,128]{1,0:T(8,128)(2,1)S(1)}, bf16[512,128]{1,0:T(8,128)(2,1)S(1)}, u32[]{:S(2)}, u32[]{:S(2)}) %collective-permute-start.4) | collective-permute-done | bytes 131104 | tf_op jit(solution)/shard_map/ppermute | solution.py:279
  27.4 0.0 collective-permute-start.6
  27.4 0.0 collective-permute-done.5.rest_6_
  27.4 4.9 %collective-permute-start.7 = (bf16[512,128]{1,0:T(8,128)(2,1)S(1)}, bf16[512,128]{1,0:T(8,128)(2,1)S(1)}, u32[]{:S(2)}, u32[]{:S(2)}) collective-permute-start(bf16[512,128]{1,0:T(8,128)(2,1)S(1)} %collective-permute-done.5.rest_6_), channel_id=1, source_target_pairs={{0,248},{8,0},{16,8},{24,16},{32,24},{40,32},{48,40},{56,48},{64,5... | collective-permute-start | bytes 393224 | tf_op jit(solution)/shard_map/ppermute | solution.py:279
  32.3 2.3 %collective-permute-done.6.rest_7_ = bf16[512,128]{1,0:T(8,128)(2,1)S(1)} collective-permute-done((bf16[512,128]{1,0:T(8,128)(2,1)S(1)}, bf16[512,128]{1,0:T(8,128)(2,1)S(1)}, u32[]{:S(2)}, u32[]{:S(2)}) %collective-permute-start.6) | collective-permute-done | bytes 131104 | tf_op jit(solution)/shard_map/ppermute | solution.py:279
  34.6 0.0 copy-start.2
  34.6 0.1 collective-permute-start.8
  34.7 0.0 collective-permute-done.7.rest_8_
  34.7 0.0 copy-start.3
  34.7 5.0 %collective-permute-start.9 = (bf16[256,128]{1,0:T(8,128)(2,1)S(1)}, bf16[256,128]{1,0:T(8,128)(2,1)S(1)}, u32[]{:S(2)}, u32[]{:S(2)}) collective-permute-start(bf16[256,128]{1,0:T(8,128)(2,1)S(1)} %slice.25), channel_id=1, source_target_pairs={{0,248},{8,0},{16,8},{24,16},{32,24},{40,32},{48,40},{56,48},{64,5... | collective-permute-start | bytes 196616 | tf_op jit(solution)/shard_map/ppermute | solution.py:279
  39.8 2.4 %collective-permute-done.8.rest_9_ = bf16[256,128]{1,0:T(8,128)(2,1)S(1)} collective-permute-done((bf16[256,128]{1,0:T(8,128)(2,1)S(1)}, bf16[256,128]{1,0:T(8,128)(2,1)S(1)}, u32[]{:S(2)}, u32[]{:S(2)}) %collective-permute-start.8) | collective-permute-done | bytes 65568 | tf_op jit(solution)/shard_map/ppermute | solution.py:279
  42.1 0.0 collective-permute-done.9.rest_10_
  42.1 0.0 copy-done
  42.1 0.0 copy-done.1
  42.1 0.0 copy-done.2
  42.1 0.0 copy-done.3
  42.1 31.6 %attention_transfer.1 = (f32[128,1024]{1,0:T(8,128)}, f32[32,48,128]{2,1,0:T(8,128)}, f32[128,256]{1,0:T(8,128)S(1)}, f32[128,256]{1,0:T(8,128)S(1)}, f32[128,128]{1,0:T(8,128)S(1)}) custom-call(s32[1,128]{1,0:T(1,128)S(1)} %bitcast.4, bf16[128,1024]{1,0:T(8,128)(2,1)S(1)} %copy-done.1, f32[8,128,128]{2,1,0:T(8,128)S(1)} %copy-done, ...), custom_call_target="tpu_custom_call" | custom-call | tf_op jit(solution)/shard_map/attention_transfer/pallas_call | solution.py:303
  73.7 6.7 %all-to-all-start = ((f32[32,48,128]{2,1,0:T(8,128)}), f32[32,48,128]{2,1,0:T(8,128)S(1)}, u32[]{:S(2)}, u32[]{:S(2)}) async-start(f32[32,48,128]{2,1,0:T(8,128)} %get-tuple-element.15), calls=%async_computation | async-start | bytes 1572864 | tf_op jit(solution)/shard_map/all_to_all | solution.py:341
  80.5 14.7 %all-to-all-done.got_ref = f32[32,48,128]{2,1,0:T(8,128)S(1)} async-done(((f32[32,48,128]{2,1,0:T(8,128)}), f32[32,48,128]{2,1,0:T(8,128)S(1)}, u32[]{:S(2)}, u32[]{:S(2)}) %all-to-all-start) | async-done | bytes 786464 | tf_op jit(solution)/shard_map/all_to_all | solution.py:341
  95.1 0.7 sum_pieces.1
  95.9 19.6 %all_to_all.15.got_ref = f32[32,48,128]{2,1,0:T(8,128)S(1)} all-to-all(f32[32,48,128]{2,1,0:T(8,128)S(1)} %get-tuple-element.16), channel_id=1, replica_groups=mesh['seq'=32,'head'=8] {'seq'}, dimensions={0} | all-to-all | bytes 1572864 | tf_op jit(solution)/shard_map/all_to_all | solution.py:350
  115.4 0.6 slice_reduce_fusion
  116.1 1.3 broadcast_in_dim.3
  117.3 14.4 %all-to-all-start.2 = ((f32[8,8,128]{2,1,0:T(8,128)}), f32[8,8,128]{2,1,0:T(8,128)S(1)}, u32[]{:S(2)}, u32[]{:S(2)}) async-start(f32[8,8,128]{2,1,0:T(8,128)} %broadcast_in_dim.3), calls=%async_computation.2 | async-start | bytes 65536 | tf_op jit(solution)/shard_map/all_to_all | solution.py:353
  131.7 1.1 key_gradients.1
  132.8 3.6 %all-to-all-done.2 = f32[8,8,128]{2,1,0:T(8,128)S(1)} async-done(((f32[8,8,128]{2,1,0:T(8,128)}), f32[8,8,128]{2,1,0:T(8,128)S(1)}, u32[]{:S(2)}, u32[]{:S(2)}) %all-to-all-start.2) | async-done | bytes 32800 | tf_op jit(solution)/shard_map/all_to_all | solution.py:353
  136.4 0.6 slice_reduce_fusion.1
  137.8 0.6 slice_multiply_fusion.1
  138.4 0.9 slice_multiply_fusion
  (2 shorter events, 0.0 us)
Async XLA Ops:
  0.6 41.5 %copy-start = (f32[8,128,128]{2,1,0:T(8,128)S(1)}, f32[8,128,128]{2,1,0:T(8,128)}, u32[]{:S(2)}) copy-start(f32[8,128,128]{2,1,0:T(8,128)} %qmap_ref.1) | copy-start | bytes 1572868
  2.2 39.9 %copy-start.1 = (bf16[128,1024]{1,0:T(8,128)(2,1)S(1)}, bf16[128,1024]{1,0:T(8,128)(2,1)}, u32[]{:S(2)}) copy-start(bf16[128,1024]{1,0:T(8,128)(2,1)} %q_ref.1) | copy-start | bytes 786436
  2.2 5.0 %collective-permute-start = (bf16[256,128]{1,0:T(8,128)(2,1)S(1)}, bf16[256,128]{1,0:T(8,128)(2,1)S(1)}, u32[]{:S(2)}, u32[]{:S(2)}) collective-permute-start(bf16[256,128]{1,0:T(8,128)(2,1)S(1)} %constant_dynamic-update-slice_fusion.rest_0_.kv_ref), channel_id=1, source_target_pairs={{0,64},{8,72},{16,80},{24,88},{32,96},{40,104},{48,112},{56,120},{... | collective-permute-start | bytes 196616 | tf_op jit(solution)/shard_map/ppermute | solution.py:279
  7.2 4.3 %collective-permute-start.1 = (bf16[256,128]{1,0:T(8,128)(2,1)S(1)}, bf16[256,128]{1,0:T(8,128)(2,1)S(1)}, u32[]{:S(2)}, u32[]{:S(2)}) collective-permute-start(bf16[256,128]{1,0:T(8,128)(2,1)S(1)} %collective-permute-done.rest_1_), channel_id=1, source_target_pairs={{0,64},{8,72},{16,80},{24,88},{32,96},{40,104},{48,112},{56,120},{... | collective-permute-start | bytes 196616 | tf_op jit(solution)/shard_map/ppermute | solution.py:279
  12.3 8.0 %collective-permute-start.2 = (bf16[512,128]{1,0:T(8,128)(2,1)S(1)}, bf16[512,128]{1,0:T(8,128)(2,1)S(1)}, u32[]{:S(2)}, u32[]{:S(2)}) collective-permute-start(bf16[512,128]{1,0:T(8,128)(2,1)S(1)} %get-tuple-element.24), channel_id=1, source_target_pairs={{0,8},{8,16},{16,24},{24,32},{32,40},{40,48},{48,56},{56,64},{64,7... | collective-permute-start | bytes 393224 | tf_op jit(solution)/shard_map/ppermute | solution.py:279
  14.2 6.1 %collective-permute-start.3 = (bf16[512,128]{1,0:T(8,128)(2,1)S(1)}, bf16[512,128]{1,0:T(8,128)(2,1)S(1)}, u32[]{:S(2)}, u32[]{:S(2)}) collective-permute-start(bf16[512,128]{1,0:T(8,128)(2,1)S(1)} %get-tuple-element.23), channel_id=1, source_target_pairs={{0,248},{8,0},{16,8},{24,16},{32,24},{40,32},{48,40},{56,48},{64,5... | collective-permute-start | bytes 393224 | tf_op jit(solution)/shard_map/ppermute | solution.py:279
  20.3 7.1 %collective-permute-start.4 = (bf16[512,128]{1,0:T(8,128)(2,1)S(1)}, bf16[512,128]{1,0:T(8,128)(2,1)S(1)}, u32[]{:S(2)}, u32[]{:S(2)}) collective-permute-start(bf16[512,128]{1,0:T(8,128)(2,1)S(1)} %collective-permute-done.2.rest_3_), channel_id=1, source_target_pairs={{0,8},{8,16},{16,24},{24,32},{32,40},{40,48},{48,56},{56,64},{64,7... | collective-permute-start | bytes 393224 | tf_op jit(solution)/shard_map/ppermute | solution.py:279
  20.3 7.1 %collective-permute-start.5 = (bf16[512,128]{1,0:T(8,128)(2,1)S(1)}, bf16[512,128]{1,0:T(8,128)(2,1)S(1)}, u32[]{:S(2)}, u32[]{:S(2)}) collective-permute-start(bf16[512,128]{1,0:T(8,128)(2,1)S(1)} %collective-permute-done.3.rest_4_), channel_id=1, source_target_pairs={{0,248},{8,0},{16,8},{24,16},{32,24},{40,32},{48,40},{56,48},{64,5... | collective-permute-start | bytes 393224 | tf_op jit(solution)/shard_map/ppermute | solution.py:279
  27.4 7.2 %collective-permute-start.6 = (bf16[512,128]{1,0:T(8,128)(2,1)S(1)}, bf16[512,128]{1,0:T(8,128)(2,1)S(1)}, u32[]{:S(2)}, u32[]{:S(2)}) collective-permute-start(bf16[512,128]{1,0:T(8,128)(2,1)S(1)} %collective-permute-done.4.rest_5_), channel_id=1, source_target_pairs={{0,8},{8,16},{16,24},{24,32},{32,40},{40,48},{48,56},{56,64},{64,7... | collective-permute-start | bytes 393224 | tf_op jit(solution)/shard_map/ppermute | solution.py:279
  27.4 7.3 %collective-permute-start.7 = (bf16[512,128]{1,0:T(8,128)(2,1)S(1)}, bf16[512,128]{1,0:T(8,128)(2,1)S(1)}, u32[]{:S(2)}, u32[]{:S(2)}) collective-permute-start(bf16[512,128]{1,0:T(8,128)(2,1)S(1)} %collective-permute-done.5.rest_6_), channel_id=1, source_target_pairs={{0,248},{8,0},{16,8},{24,16},{32,24},{40,32},{48,40},{56,48},{64,5... | collective-permute-start | bytes 393224 | tf_op jit(solution)/shard_map/ppermute | solution.py:279
  34.6 7.5 %copy-start.2 = (f32[1,128,128]{2,1,0:T(8,128)S(1)}, f32[1,128,128]{2,1,0:T(8,128)}, u32[]{:S(2)}) copy-start(f32[1,128,128]{2,1,0:T(8,128)} %kmap_ref.3) | copy-start | bytes 196612
  34.6 7.5 %collective-permute-start.8 = (bf16[256,128]{1,0:T(8,128)(2,1)S(1)}, bf16[256,128]{1,0:T(8,128)(2,1)S(1)}, u32[]{:S(2)}, u32[]{:S(2)}) collective-permute-start(bf16[256,128]{1,0:T(8,128)(2,1)S(1)} %slice.24), channel_id=1, source_target_pairs={{0,8},{8,16},{16,24},{24,32},{32,40},{40,48},{48,56},{56,64},{64,7... | collective-permute-start | bytes 196616 | tf_op jit(solution)/shard_map/ppermute | solution.py:279
  34.7 7.4 %copy-start.3 = (s32[128]{0:T(128)S(1)}, s32[128]{0:T(128)}, u32[]{:S(2)}) copy-start(s32[128]{0:T(128)} %param.9) | copy-start | bytes 1540
  34.7 7.4 %collective-permute-start.9 = (bf16[256,128]{1,0:T(8,128)(2,1)S(1)}, bf16[256,128]{1,0:T(8,128)(2,1)S(1)}, u32[]{:S(2)}, u32[]{:S(2)}) collective-permute-start(bf16[256,128]{1,0:T(8,128)(2,1)S(1)} %slice.25), channel_id=1, source_target_pairs={{0,248},{8,0},{16,8},{24,16},{32,24},{40,32},{48,40},{56,48},{64,5... | collective-permute-start | bytes 196616 | tf_op jit(solution)/shard_map/ppermute | solution.py:279
  73.7 21.4 %all-to-all-start = ((f32[32,48,128]{2,1,0:T(8,128)}), f32[32,48,128]{2,1,0:T(8,128)S(1)}, u32[]{:S(2)}, u32[]{:S(2)}) async-start(f32[32,48,128]{2,1,0:T(8,128)} %get-tuple-element.15), calls=%async_computation | async-start | bytes 1572864 | tf_op jit(solution)/shard_map/all_to_all | solution.py:341
  117.3 19.1 %all-to-all-start.2 = ((f32[8,8,128]{2,1,0:T(8,128)}), f32[8,8,128]{2,1,0:T(8,128)S(1)}, u32[]{:S(2)}, u32[]{:S(2)}) async-start(f32[8,8,128]{2,1,0:T(8,128)} %broadcast_in_dim.3), calls=%async_computation.2 | async-start | bytes 65536 | tf_op jit(solution)/shard_map/all_to_all | solution.py:353

commit v2 on v1

v2 whole, which is shorter than its diff:
```python
import functools
import math

import jax
import jax.numpy as jnp
from jax import lax
from jax.experimental import pallas as pl
from jax.experimental.pallas import tpu as pltpu
from jax.sharding import PartitionSpec as P

F32 = jnp.float32
BF16 = jnp.bfloat16
NEGATIVE = -1e30
EPSILON = 1e-06
T = 128
WINDOW = 16
KEYS = (WINDOW + 1) * T
CHUNK = 1024
PIECE = 48
STATE_ROW, KMAP_ROW, NORM_ROW, INFO_ROW = 32, 40, 44, 46


def nn(a, b):
    return lax.dot_general(a, b, (((1,), (0,)), ((), ())), preferred_element_type=F32)


def nt(a, b):
    return lax.dot_general(a, b, (((1,), (1,)), ((), ())), preferred_element_type=F32)


def tn(a, b):
    return lax.dot_general(a, b, (((0,), (0,)), ((), ())), preferred_element_type=F32)


def split2(x):
    high = x.astype(BF16)
    return high, (x - high.astype(F32)).astype(BF16)


def split3(x):
    high = x.astype(BF16)
    rest = x - high.astype(F32)
    middle = rest.astype(BF16)
    return high, middle, (rest - middle.astype(F32)).astype(BF16)


def product(form, a, b):
    return form(a[0], b[0]) + (form(a[0], b[1]) + form(a[1], b[0]))


def exact_left(form, a, parts):
    total = form(a, parts[-1])
    for part in parts[-2::-1]:
        total = total + form(a, part)
    return total


def exact_right(form, parts, b):
    return form(parts[0], b) + form(parts[1], b)


def feature_map(logits):
    upper = jnp.exp(logits - jnp.max(logits, axis=-1, keepdims=True))
    lower = jnp.exp(jnp.min(logits, axis=-1, keepdims=True) - logits)
    upper = upper * (1.0 / jnp.sum(upper, axis=-1, keepdims=True))
    lower = lower * (1.0 / jnp.sum(lower, axis=-1, keepdims=True))
    return upper, lower


def feature_back(phi, grad):
    upper, lower = phi[:, :T], phi[:, T:]
    up, low = grad[:, :T], grad[:, T:]
    up = upper * (up - jnp.sum(upper * up, axis=-1, keepdims=True))
    low = lower * (low - jnp.sum(lower * low, axis=-1, keepdims=True))
    return up - low


def column_of(row):
    i = lax.broadcasted_iota(jnp.int32, (T, T), 0)
    j = lax.broadcasted_iota(jnp.int32, (T, T), 1)
    return jnp.sum(jnp.where(i == j, row, 0.0), axis=1, keepdims=True)


def stacked(ref):
    return jnp.concatenate([ref[:, h * T : h * T + T] for h in range(ref.shape[1] // T)], axis=0)


def every_head(x, heads):
    return jnp.concatenate([x] * heads, axis=0)


def positions_of(pos_ref):
    row = lax.broadcasted_iota(jnp.int32, (T, 1), 0).astype(F32)
    return row, row - column_of(pos_ref[...].astype(F32))


def local_kernel(pos_ref, q_ref, k_ref, qmap_ref, kmap_ref, phi_ref, inner_ref, own_ref):
    heads = qmap_ref.shape[0]
    row, start = positions_of(pos_ref)
    key = lax.broadcasted_iota(jnp.int32, (T, T), 1).astype(F32)
    seen = every_head(((key <= row) & (key >= start)).astype(F32), heads)
    own = jnp.concatenate(
        feature_map(exact_left(nn, k_ref[...], split3(kmap_ref[0]))), axis=1
    )
    own_ref[...] = own
    logits = jnp.concatenate(
        [exact_left(nn, q_ref[:, h * T : h * T + T], split3(qmap_ref[h])) for h in range(heads)],
        axis=0,
    )
    phi = jnp.concatenate(feature_map(logits), axis=1)
    phi_ref[...] = phi
    inner_ref[...] = product(nt, split2(phi), split2(own)) * seen


def main_kernel(places, pos_ref, q_ref, kmap_ref, phi_ref, inner_ref, own_ref, *rest):
    count = len(places)
    blocks = rest[:count]
    payload_ref, dlogit_ref, gn_ref, gkphi_ref = rest[count : count + 4]
    k_s, v_s, phi_s = rest[count + 4 :]
    heads = q_ref.shape[1] // T
    row, start = positions_of(pos_ref)
    entry = -pos_ref[0:1, 0:1].astype(F32)
    for ref, held in zip(blocks, places):
        for slot, block in enumerate(held):
            at = (WINDOW - block) * T
            k_s[at : at + T, :] = ref[slot * 2 * T : slot * 2 * T + T, :]
            v_s[at : at + T, :] = ref[slot * 2 * T + T : slot * 2 * T + 2 * T, :]

    map_parts = split3(kmap_ref[0])
    state = jnp.zeros((2 * T, T), F32)
    norms = jnp.zeros((1, 2 * T), F32)
    for at in range(0, WINDOW * T, CHUNK):
        key_row = lax.broadcasted_iota(jnp.int32, (CHUNK, 1), 0) + (at - WINDOW * T)
        features = jnp.concatenate(
            feature_map(exact_left(nn, k_s[at : at + CHUNK, :], map_parts)), axis=1
        )
        features = jnp.where(key_row.astype(F32) >= entry, features, 0.0)
        phi_s[at : at + CHUNK, :] = features
        state = state + exact_right(tn, split2(features), v_s[at : at + CHUNK, :])
        norms = norms + jnp.sum(features, axis=0, keepdims=True)
    state = split2(state)

    key = lax.broadcasted_iota(jnp.int32, (T, KEYS), 1).astype(F32) - float(WINDOW * T)
    visible = (key <= row) & (key >= start)
    bias = every_head(jnp.where(visible, 0.0, NEGATIVE), heads)
    seen = every_head(visible[:, WINDOW * T :].astype(F32), heads)
    cross = every_head((start < 0.0).astype(F32), heads)
    queries = stacked(q_ref)
    scores = nt(queries, k_s[...]) * (1.0 / math.sqrt(T)) + bias
    weights = jnp.exp(scores - jnp.max(scores, axis=-1, keepdims=True))
    total = jnp.sum(weights, axis=-1, keepdims=True)
    teacher = nn(weights.astype(BF16), v_s[...]) / total

    own = own_ref[...]
    own_v = v_s[WINDOW * T :, :]
    own_phi = split2(own)
    phi = phi_ref[...]
    phi_parts = split2(phi)
    inner = inner_ref[...]
    numer = exact_right(nn, split2(inner), own_v) + cross * product(nn, phi_parts, state)
    denom = jnp.sum(inner, axis=-1, keepdims=True) + cross * jnp.sum(
        phi * norms, axis=-1, keepdims=True
    )
    outputs = numer / denom
    error = outputs - teacher

    grad_numer = error / denom
    grad_denom = -jnp.sum(error * outputs, axis=-1, keepdims=True) / denom
    gn_ref[...] = grad_numer
    far_parts = split2(cross * grad_numer)
    far_denom = cross * grad_denom
    mixing_parts = split2((exact_right(nt, split2(grad_numer), own_v) + grad_denom) * seen)
    grad_phi = (
        product(nn, mixing_parts, own_phi) + product(nt, far_parts, state) + far_denom * norms
    )
    back = product(tn, phi_parts, far_parts)
    backn = jnp.sum(phi * far_denom, axis=0, keepdims=True)
    gkphi = product(tn, mixing_parts, phi_parts)
    gkphi_ref[...] = gkphi
    dlogit = feature_back(phi, grad_phi)
    dlogit_ref[...] = dlogit
    dlogit_parts = split2(dlogit)
    for h in range(heads):
        at = slice(h * T, h * T + T)
        grad_map = exact_left(tn, q_ref[:, at], [part[at, :] for part in dlogit_parts])
        for quarter in range(4):
            payload_ref[4 * h + quarter, 0:STATE_ROW, :] = grad_map[
                quarter * 32 : quarter * 32 + 32, :
            ]
    back_parts = split2(back)
    for piece in range(32):
        payload_ref[piece, STATE_ROW : STATE_ROW + 8, :] = back[piece * 8 : piece * 8 + 8, :]

    part = split2(feature_back(own, gkphi))
    grad_map = exact_left(tn, k_s[WINDOW * T :, :], part)
    for at in range(0, WINDOW * T, CHUNK):
        grad = exact_left(nt, v_s[at : at + CHUNK, :], back_parts) + backn
        part = split2(feature_back(phi_s[at : at + CHUNK, :], grad))
        grad_map = grad_map + exact_left(tn, k_s[at : at + CHUNK, :], part)
    tail = jnp.concatenate(
        [
            backn[:, :T],
            backn[:, T:],
            jnp.broadcast_to(pos_ref[0:1, 0:1].astype(F32), (1, T)),
            jnp.zeros((1, T), F32),
        ],
        axis=0,
    )
    for piece in range(32):
        payload_ref[piece, KMAP_ROW:PIECE, :] = jnp.concatenate(
            [grad_map[piece * 4 : piece * 4 + 4, :], tail], axis=0
        )


def query_kernel(dlogit_ref, inner_ref, gn_ref, qmap_ref, gq_ref, gv_ref):
    for h in range(qmap_ref.shape[0]):
        at = slice(h * T, h * T + T)
        gq_ref[:, at] = product(nt, split2(dlogit_ref[at, :]), split2(qmap_ref[h]))
    gv_ref[...] = product(tn, split2(inner_ref[...]), split2(gn_ref[...]))


def middle_kernel(me_ref, got_ref, out_ref, norms_ref):
    pieces = got_ref.shape[0]
    total = got_ref[0]
    for i in range(1, pieces):
        total = total + got_ref[i]
    squares = jnp.sum(total[0:STATE_ROW, :] * total[0:STATE_ROW, :]) + jnp.sum(
        total[KMAP_ROW:NORM_ROW, :] * total[KMAP_ROW:NORM_ROW, :]
    )
    tail = jnp.concatenate(
        [total[KMAP_ROW:INFO_ROW, :], jnp.full((2, T), squares, F32)], axis=0
    )
    for j in range(pieces):
        out_ref[j, 0:STATE_ROW, :] = total[0:STATE_ROW, :]
        out_ref[j, KMAP_ROW:PIECE, :] = tail
    sender = lax.broadcasted_iota(jnp.int32, (pieces, T), 0)
    target = lax.broadcasted_iota(jnp.int32, (pieces, T), 1)
    first = (sender * T).astype(F32) - got_ref[:, INFO_ROW, :]
    links = (sender > target) & (first <= (target * T + (T - 1)).astype(F32))
    reach = links.astype(F32)[:, :pieces].astype(BF16)
    for i in range(8):
        high, middle, low = split3(got_ref[:, STATE_ROW + i, :])
        out_ref[:, STATE_ROW + i, :] = tn(reach, high) + (tn(reach, middle) + tn(reach, low))
    me = me_ref[0]
    mine = (sender > me) & (first <= (me * T + (T - 1)).astype(F32))
    for half in range(2):
        norms_ref[0:1, half * T : half * T + T] = jnp.sum(
            jnp.where(mine, got_ref[:, NORM_ROW + half, :], 0.0), axis=0, keepdims=True
        )


def last_kernel(pos_ref, got_ref, norms_ref, v_ref, kmap_ref, phi_ref, gkphi_ref, gv_ref, gk_ref, gvo_ref):
    _, start = positions_of(pos_ref)
    last_start = float(T - 1) - pos_ref[0:1, T - 1 : T].astype(F32)
    keeping = (start == last_start).astype(F32)
    pieces = got_ref.shape[0]
    back = split2(
        jnp.concatenate([got_ref[r, STATE_ROW : STATE_ROW + 8, :] for r in range(pieces)], axis=0)
    )
    phi = phi_ref[...]
    own_v = v_ref[...]
    grad = gkphi_ref[...] + keeping * (exact_left(nt, own_v, back) + norms_ref[...])
    gvo_ref[...] = gv_ref[...] + keeping * product(nn, split2(phi), back)
    gk_ref[...] = product(nt, split2(feature_back(phi, grad)), split2(kmap_ref[0]))


def squares_kernel(tail_ref, out_ref):
    total = jnp.sum(tail_ref[:, INFO_ROW - KMAP_ROW, :], axis=0, keepdims=True)
    out_ref[...] = jnp.broadcast_to(total.reshape(1, 1, T), out_ref.shape)


def scale_kernel(limit, got_ref, squares_ref, qmap_ref, kmap_ref):
    pieces = got_ref.shape[0]
    squared = jnp.sum(squares_ref[:, 0, :], axis=0, keepdims=True)
    factor = jnp.minimum(1.0, limit / (jnp.sqrt(squared) + EPSILON))
    for piece in range(pieces):
        rows = slice(piece % 4 * 32, piece % 4 * 32 + 32)
        qmap_ref[piece // 4, rows, :] = factor * got_ref[piece, 0:STATE_ROW, :]
        kmap_ref[0, piece * 4 : piece * 4 + 4, :] = factor * got_ref[piece, KMAP_ROW:NORM_ROW, :]


def call(body, name, ins, outs, scratch=(), limit=32):
    return pl.pallas_call(
        body,
        in_specs=[pl.BlockSpec(memory_space=space) for space in ins],
        out_specs=[pl.BlockSpec(memory_space=pltpu.VMEM)] * len(outs),
        out_shape=[jax.ShapeDtypeStruct(shape, F32) for shape in outs],
        scratch_shapes=list(scratch),
        compiler_params=pltpu.CompilerParams(vmem_limit_bytes=limit << 20),
        name=name,
    )


def joined(a, b):
    return lax.pad(a, jnp.zeros((), a.dtype), ((0, b.shape[0], 0), (0, 0, 0))) + lax.pad(
        b, jnp.zeros((), b.dtype), ((a.shape[0], 0, 0), (0, 0, 0))
    )


def window_of(kv):
    n = lax.axis_size("seq")
    size = kv.shape[0]

    def shift(x, k):
        return lax.ppermute(x, "seq", [(i, (i + k) % n) for i in range(n)])

    b1, b4, b7, b8 = (shift(kv, k) for k in (1, 4, 7, 8))
    near = jnp.concatenate([b8, b1, b4, b7], axis=0)
    far = shift(near, 8)
    up, down = slice(size, 3 * size), slice(2 * size, 4 * size)
    n1, n2 = shift(near[up], 1), shift(near[down], -1)
    f1, f2 = shift(far[up], 1), shift(far[down], -1)
    arrays = [kv, near, far, n1, n2, f1, f2]
    places = [(0,), (8, 1, 4, 7), (16, 9, 12, 15), (2, 5), (3, 6), (10, 13), (11, 14)]
    return arrays, places


def on_device(queries, key_vectors, value_vectors, positions, query_map, key_map):
    group = query_map.shape[0]
    pieces = lax.axis_size("seq")
    heads = lax.axis_size("head")
    rows = group * T
    me = lax.axis_index("seq").astype(jnp.int32).reshape(1)
    pos = positions.reshape(1, T)
    kv = joined(key_vectors, value_vectors)
    arrays, places = window_of(kv)
    V = pltpu.VMEM
    phi, inner, own = call(
        local_kernel, "local_features", [V] * 5, [(rows, 2 * T), (rows, T), (T, 2 * T)]
    )(pos, queries, key_vectors, query_map, key_map)
    payload, dlogit, grad_numer, gkphi = call(
        functools.partial(main_kernel, places),
        "attention_transfer",
        [V] * (6 + len(arrays)),
        [(pieces, PIECE, T), (rows, T), (rows, T), (T, 2 * T)],
        [V((KEYS, T), BF16), V((KEYS, T), BF16), V((WINDOW * T, 2 * T), F32)],
        32,
    )(pos, queries, key_map, phi, inner, own, *arrays)
    gathered = lax.all_to_all(payload, "seq", 0, 0)
    grad_queries, near_values = call(
        query_kernel, "query_gradients", [V] * 4, [(T, rows), (T, T)]
    )(dlogit, inner, grad_numer, query_map)
    reduced, norms = call(
        middle_kernel, "sum_pieces", [pltpu.SMEM, V], [(pieces, PIECE, T), (1, 2 * T)]
    )(me, gathered)
    back = lax.all_to_all(reduced, "seq", 0, 0)
    squares = pl.pallas_call(
        squares_kernel,
        grid=(1,),
        in_specs=[pl.BlockSpec((pieces, PIECE - KMAP_ROW, T), lambda i: (0, KMAP_ROW // 8, 0))],
        out_specs=pl.BlockSpec((heads, 8, T), lambda i: (0, 0, 0)),
        out_shape=jax.ShapeDtypeStruct((heads, 8, T), F32),
        name="head_squares",
    )(back)
    squares = lax.all_to_all(squares, "head", 0, 0)
    grad_keys, grad_values = call(last_kernel, "key_gradients", [V] * 8, [(T, T), (T, T)])(
        pos, back, norms, value_vectors, key_map, own, gkphi, near_values
    )
    clip_limit = 0.25 * math.sqrt((group + 1) * heads * T * T)
    query_map_grad, key_map_grad = call(
        functools.partial(scale_kernel, clip_limit),
        "clip_maps",
        [V] * 2,
        [(group, T, T), (1, T, T)],
    )(back, squares)
    return (grad_queries, grad_keys, grad_values, query_map_grad, key_map_grad)


def solution(mesh):
    placed = (
        P("seq", "head"),
        P("seq", "head"),
        P("seq", "head"),
        P("seq"),
        P("head", None, None),
        P("head", None, None),
    )
    return jax.shard_map(
        on_device,
        mesh=mesh,
        in_specs=placed,
        out_specs=(
            P("seq", "head"),
            P("seq", "head"),
            P("seq", "head"),
            P("head", None, None),
            P("head", None, None),
        ),
        check_vma=False,
    )
```

time: 140 us -> 117 us (0.84)
  Pallas kernels: 33.4 us -> 20.9 us
  waiting for transfers between devices: 34.6 us -> 28.2 us
  blocking collectives: 19.6 us -> 23.9 us
  local copies, waits for them, and re-layouts: 2.88 us -> 0.09 us
  other arithmetic: 3.54 us -> 0.8 us
  starting transfers between devices: 43.9 us -> 41.7 us
    pallas_call x3 -> x7, Pallas kernels: 33.4 us -> 20.9 us  [the longest x1 13.8 us: on_device(): call(functools.partial(main_kernel, places), 'attention_transfer', [V] *...]
    ppermute x10 -> x9, waiting for transfers between devices: 16.2 us -> 10.2 us  [shift(): return lax.ppermute(x, 'seq', [(i, (i + k) % n) for i in range(n)])]
    all_to_all x1, blocking collectives: 19.6 us -> 23.9 us  [on_device(): back = lax.all_to_all(reduced, 'seq', 0, 0)]
    all_to_all x1, waiting for transfers between devices: 3.65 us -> 2.12 us  [on_device(): squares = lax.all_to_all(squares, 'head', 0, 0)]
    all_to_all x1, starting transfers between devices: 14.4 us -> 12.9 us  [on_device(): squares = lax.all_to_all(squares, 'head', 0, 0)]
    mul x2 -> x0, other arithmetic: 1.5 us -> none  [the longest x1 0.86 us: on_device(): query_map_grad = factor * back[:, :STATE_ROW, :].reshape(group, T, T)]
    ppermute x10 -> x9, starting transfers between devices: 22.8 us -> 22.3 us  [shift(): return lax.ppermute(x, 'seq', [(i, (i + k) % n) for i in range(n)])]
  transfers between devices with their start and end apart: 12 -> 11, of which waited for: 8 -> 6; matrix products, arithmetic and copies ran while one was open for 0% -> 0% of each run, Pallas kernels for 1% -> 3%
where the time goes in v2:
time: 117 us; the launch traced here: 116 us
  starting transfers between devices  41.7 us (36%)
  waiting for transfers between devices  28.2 us (24%)
  blocking collectives  23.9 us (20%)
  Pallas kernels  20.9 us (18%)
    all_to_all x1, blocking collectives, on_device(): back = lax.all_to_all(reduced, 'seq', 0, 0)  23.9 us
    ppermute x9, starting transfers between devices, shift(): return lax.ppermute(x, 'seq', [(i, (i + k) % n) for i in range(n)])  22.3 us
    all_to_all x1, waiting for transfers between devices, on_device(): gathered = lax.all_to_all(payload, 'seq', 0, 0)  15.9 us
    pallas_call x1, Pallas kernels, on_device(): call(functools.partial(main_kernel, places), 'attention_transfer', [V] *...  13.8 us
    all_to_all x1, starting transfers between devices, on_device(): squares = lax.all_to_all(squares, 'head', 0, 0)  12.9 us
    ppermute x9, waiting for transfers between devices, shift(): return lax.ppermute(x, 'seq', [(i, (i + k) % n) for i in range(n)])  10.2 us
    all_to_all x1, starting transfers between devices, on_device(): gathered = lax.all_to_all(payload, 'seq', 0, 0)  6.44 us
  transfers between devices with their start and end apart: 11, of which 6 were waited for; matrix products, arithmetic and copies ran while one was open for 0% of the time, Pallas kernels for 3%

profile of v2, /device:TPU:1, one launch (start us, length us, event | category | flops | bytes accessed | tf_op | source)
XLA Modules:
  0.0 116.3 jit_solution(12130525946147302905)
XLA Ops:
  0.6 0.8 pad_add_fusion.rest_0_
  1.4 2.0 %collective-permute-start = (bf16[256,128]{1,0:T(8,128)(2,1)S(1)}, bf16[256,128]{1,0:T(8,128)(2,1)S(1)}, u32[]{:S(2)}, u32[]{:S(2)}) collective-permute-start(bf16[256,128]{1,0:T(8,128)(2,1)S(1)} %pad_add_fusion.rest_0_), channel_id=1, source_target_pairs={{0,64},{8,72},{16,80},{24,88},{32,96},{40,104},{48,112},{56,120},{... | collective-permute-start | bytes 196616 | tf_op jit(solution)/shard_map/ppermute | solution.py:305
  3.5 1.6 %collective-permute-start.1 = (bf16[256,128]{1,0:T(8,128)(2,1)S(1)}, bf16[256,128]{1,0:T(8,128)(2,1)S(1)}, u32[]{:S(2)}, u32[]{:S(2)}) collective-permute-start(bf16[256,128]{1,0:T(8,128)(2,1)S(1)} %pad_add_fusion.rest_0_), channel_id=1, source_target_pairs={{0,8},{8,16},{16,24},{24,32},{32,40},{40,48},{48,56},{56,64},{64,7... | collective-permute-start | bytes 196616 | tf_op jit(solution)/shard_map/ppermute | solution.py:305
  5.1 6.0 %collective-permute-start.2 = (bf16[256,128]{1,0:T(8,128)(2,1)S(1)}, bf16[256,128]{1,0:T(8,128)(2,1)S(1)}, u32[]{:S(2)}, u32[]{:S(2)}) collective-permute-start(bf16[256,128]{1,0:T(8,128)(2,1)S(1)} %pad_add_fusion.rest_0_), channel_id=1, source_target_pairs={{0,32},{8,40},{16,48},{24,56},{32,64},{40,72},{48,80},{56,88},{64,... | collective-permute-start | bytes 196616 | tf_op jit(solution)/shard_map/ppermute | solution.py:305
  11.1 2.9 %collective-permute-start.3 = (bf16[256,128]{1,0:T(8,128)(2,1)S(1)}, bf16[256,128]{1,0:T(8,128)(2,1)S(1)}, u32[]{:S(2)}, u32[]{:S(2)}) collective-permute-start(bf16[256,128]{1,0:T(8,128)(2,1)S(1)} %pad_add_fusion.rest_0_), channel_id=1, source_target_pairs={{0,56},{8,64},{16,72},{24,80},{32,88},{40,96},{48,104},{56,112},{6... | collective-permute-start | bytes 196616 | tf_op jit(solution)/shard_map/ppermute | solution.py:305
  14.0 0.0 collective-permute-done
  14.0 0.0 collective-permute-done.1
  14.0 0.7 collective-permute-done.2
  14.7 2.9 %collective-permute-done.3 = bf16[256,128]{1,0:T(8,128)(2,1)S(1)} collective-permute-done((bf16[256,128]{1,0:T(8,128)(2,1)S(1)}, bf16[256,128]{1,0:T(8,128)(2,1)S(1)}, u32[]{:S(2)}, u32[]{:S(2)}) %collective-permute-start.3) | collective-permute-done | bytes 65568 | tf_op jit(solution)/shard_map/ppermute | solution.py:305
  17.7 0.0 copy-start.1
  17.7 0.1 collective-permute-start.4
  17.8 0.4 collective-permute-start.5
  18.2 0.0 copy-start.2
  18.2 0.0 copy-start.3
  18.2 0.0 copy-start.4
  18.2 4.5 %collective-permute-start.6 = (bf16[512,128]{1,0:T(8,128)(2,1)S(1)}, bf16[512,128]{1,0:T(8,128)(2,1)S(1)}, u32[]{:S(2)}, u32[]{:S(2)}) collective-permute-start(bf16[512,128]{1,0:T(8,128)(2,1)S(1)} %get-tuple-element.37), channel_id=1, source_target_pairs={{0,248},{8,0},{16,8},{24,16},{32,24},{40,32},{48,40},{56,48},{64,5... | collective-permute-start | bytes 393224 | tf_op jit(solution)/shard_map/ppermute | solution.py:305
  22.7 5.5 %collective-permute-done.4.rest_2_ = bf16[1024,128]{1,0:T(8,128)(2,1)S(1)} collective-permute-done((bf16[1024,128]{1,0:T(8,128)(2,1)S(1)}, bf16[1024,128]{1,0:T(8,128)(2,1)S(1)}, u32[]{:S(2)}, u32[]{:S(2)}) %collective-permute-start.4) | collective-permute-done | bytes 262176 | tf_op jit(solution)/shard_map/ppermute | solution.py:305
  28.2 0.1 collective-permute-start.7
  28.3 0.0 copy-start.6
  28.3 4.8 %collective-permute-start.8 = (bf16[512,128]{1,0:T(8,128)(2,1)S(1)}, bf16[512,128]{1,0:T(8,128)(2,1)S(1)}, u32[]{:S(2)}, u32[]{:S(2)}) collective-permute-start(bf16[512,128]{1,0:T(8,128)(2,1)S(1)} %get-tuple-element.35), channel_id=1, source_target_pairs={{0,248},{8,0},{16,8},{24,16},{32,24},{40,32},{48,40},{56,48},{64,5... | collective-permute-start | bytes 393224 | tf_op jit(solution)/shard_map/ppermute | solution.py:305
  33.1 0.0 copy-done.1
  33.1 0.0 copy-done.2
  33.1 0.0 copy-done.3
  33.1 0.0 copy-done.4
  33.1 0.0 copy-done.6
  33.1 1.3 %local_features.1 = (f32[1024,256]{1,0:T(8,128)S(1)}, f32[1024,128]{1,0:T(8,128)S(1)}, f32[128,256]{1,0:T(8,128)S(1)}) custom-call(s32[1,128]{1,0:T(1,128)S(1)} %bitcast.2, bf16[128,1024]{1,0:T(8,128)(2,1)S(1)} %copy-done.2, bf16[128,128]{1,0:T(8,128)(2,1)S(1)} %copy-done.4, f32[8,128,128]{2,1,0:T(8,128)S(1)} %copy-done.1, f32[1,128,128]{2,1,0:T(8,128)S(1)} %copy-done.3), custom_call_target="tpu_custom_call" | custom-call | tf_op jit(solution)/shard_map/local_features/pallas_call | solution.py:328
  34.4 0.0 collective-permute-done.5.rest_3_
  34.4 0.0 collective-permute-done.6.rest_4_
  34.4 1.0 collective-permute-done.7.rest_5_
  35.5 0.0 collective-permute-done.8.rest_6_
  35.5 13.8 %attention_transfer.1 = (f32[32,48,128]{2,1,0:T(8,128)}, f32[1024,128]{1,0:T(8,128)S(1)}, f32[1024,128]{1,0:T(8,128)S(1)}, f32[128,256]{1,0:T(8,128)S(1)}) custom-call(s32[1,128]{1,0:T(1,128)S(1)} %bitcast.3, bf16[128,1024]{1,0:T(8,128)(2,1)S(1)} %copy-done.2, f32[1,128,128]{2,1,0:T(8,128)S(1)} %copy-done.3, f32[1024,256]{1,0:T(8,128)S(1)} %get-tuple-element.20.phi_ref, ...), custom_call_target="tpu_custom_call" | custom-call | tf_op jit(solution)/shard_map/attention_transfer/pallas_call | solution.py:331
  49.3 6.4 %all-to-all-start = ((f32[32,48,128]{2,1,0:T(8,128)}), f32[32,48,128]{2,1,0:T(8,128)S(1)}, u32[]{:S(2)}, u32[]{:S(2)}) async-start(f32[32,48,128]{2,1,0:T(8,128)} %get-tuple-element.26), calls=%async_computation | async-start | bytes 1572864 | tf_op jit(solution)/shard_map/all_to_all | solution.py:339
  55.8 15.9 %all-to-all-done.got_ref = f32[32,48,128]{2,1,0:T(8,128)S(1)} async-done(((f32[32,48,128]{2,1,0:T(8,128)}), f32[32,48,128]{2,1,0:T(8,128)S(1)}, u32[]{:S(2)}, u32[]{:S(2)}) %all-to-all-start) | async-done | bytes 786464 | tf_op jit(solution)/shard_map/all_to_all | solution.py:339
  71.7 0.7 sum_pieces.1
  72.4 23.9 %all_to_all.15.got_ref.tail_ref = f32[32,48,128]{2,1,0:T(8,128)} all-to-all(f32[32,48,128]{2,1,0:T(8,128)S(1)} %get-tuple-element.27), channel_id=1, replica_groups=mesh['seq'=32,'head'=8] {'seq'}, dimensions={0} | all-to-all | bytes 1572864 | tf_op jit(solution)/shard_map/all_to_all | solution.py:346
  96.3 1.5 %head_squares.1 = f32[8,8,128]{2,1,0:T(8,128)} custom-call(f32[32,48,128]{2,1,0:T(8,128)} %all_to_all.15.got_ref.tail_ref), custom_call_target="tpu_custom_call" | custom-call | tf_op jit(solution)/shard_map/head_squares/pallas_call | solution.py:347
  97.8 12.9 %all-to-all-start.2 = ((f32[8,8,128]{2,1,0:T(8,128)}), f32[8,8,128]{2,1,0:T(8,128)S(1)}, u32[]{:S(2)}, u32[]{:S(2)}) async-start(f32[8,8,128]{2,1,0:T(8,128)} %head_squares.1), calls=%async_computation.2 | async-start | bytes 65536 | tf_op jit(solution)/shard_map/all_to_all | solution.py:355
  110.7 0.0 copy-start
  110.7 0.0 copy-start.5
  110.7 1.5 %query_gradients.1 = (f32[128,1024]{1,0:T(8,128)}, f32[128,128]{1,0:T(8,128)S(1)}) custom-call(f32[1024,128]{1,0:T(8,128)S(1)} %get-tuple-element.23.dlogit_ref, f32[1024,128]{1,0:T(8,128)S(1)} %get-tuple-element.21.inner_ref, f32[1024,128]{1,0:T(8,128)S(1)} %get-tuple-element.24.gn_ref, f32[8,128,128]{2,1,0:T(8,128)S(1)} %copy-done.1), custom_call_target="tpu_custom_call" | custom-call | tf_op jit(solution)/shard_map/query_gradients/pallas_call | solution.py:340
  112.2 0.0 copy-done
  112.2 0.0 copy-done.5
  112.2 1.1 key_gradients.1
  113.3 2.1 %all-to-all-done.2.squares_ref = f32[8,8,128]{2,1,0:T(8,128)S(1)} async-done(((f32[8,8,128]{2,1,0:T(8,128)}), f32[8,8,128]{2,1,0:T(8,128)S(1)}, u32[]{:S(2)}, u32[]{:S(2)}) %all-to-all-start.2) | async-done | bytes 32800 | tf_op jit(solution)/shard_map/all_to_all | solution.py:355
  115.4 0.9 clip_maps.1
  (6 shorter events, 0.1 us)
Async XLA Ops:
  1.4 12.6 %collective-permute-start = (bf16[256,128]{1,0:T(8,128)(2,1)S(1)}, bf16[256,128]{1,0:T(8,128)(2,1)S(1)}, u32[]{:S(2)}, u32[]{:S(2)}) collective-permute-start(bf16[256,128]{1,0:T(8,128)(2,1)S(1)} %pad_add_fusion.rest_0_), channel_id=1, source_target_pairs={{0,64},{8,72},{16,80},{24,88},{32,96},{40,104},{48,112},{56,120},{... | collective-permute-start | bytes 196616 | tf_op jit(solution)/shard_map/ppermute | solution.py:305
  3.5 10.5 %collective-permute-start.1 = (bf16[256,128]{1,0:T(8,128)(2,1)S(1)}, bf16[256,128]{1,0:T(8,128)(2,1)S(1)}, u32[]{:S(2)}, u32[]{:S(2)}) collective-permute-start(bf16[256,128]{1,0:T(8,128)(2,1)S(1)} %pad_add_fusion.rest_0_), channel_id=1, source_target_pairs={{0,8},{8,16},{16,24},{24,32},{32,40},{40,48},{48,56},{56,64},{64,7... | collective-permute-start | bytes 196616 | tf_op jit(solution)/shard_map/ppermute | solution.py:305
  5.1 9.6 %collective-permute-start.2 = (bf16[256,128]{1,0:T(8,128)(2,1)S(1)}, bf16[256,128]{1,0:T(8,128)(2,1)S(1)}, u32[]{:S(2)}, u32[]{:S(2)}) collective-permute-start(bf16[256,128]{1,0:T(8,128)(2,1)S(1)} %pad_add_fusion.rest_0_), channel_id=1, source_target_pairs={{0,32},{8,40},{16,48},{24,56},{32,64},{40,72},{48,80},{56,88},{64,... | collective-permute-start | bytes 196616 | tf_op jit(solution)/shard_map/ppermute | solution.py:305
  11.1 6.6 %collective-permute-start.3 = (bf16[256,128]{1,0:T(8,128)(2,1)S(1)}, bf16[256,128]{1,0:T(8,128)(2,1)S(1)}, u32[]{:S(2)}, u32[]{:S(2)}) collective-permute-start(bf16[256,128]{1,0:T(8,128)(2,1)S(1)} %pad_add_fusion.rest_0_), channel_id=1, source_target_pairs={{0,56},{8,64},{16,72},{24,80},{32,88},{40,96},{48,104},{56,112},{6... | collective-permute-start | bytes 196616 | tf_op jit(solution)/shard_map/ppermute | solution.py:305
  17.7 15.4 %copy-start.1 = (f32[8,128,128]{2,1,0:T(8,128)S(1)}, f32[8,128,128]{2,1,0:T(8,128)}, u32[]{:S(2)}) copy-start(f32[8,128,128]{2,1,0:T(8,128)} %qmap_ref.3) | copy-start | bytes 1572868
  17.7 10.5 %collective-permute-start.4 = (bf16[1024,128]{1,0:T(8,128)(2,1)S(1)}, bf16[1024,128]{1,0:T(8,128)(2,1)S(1)}, u32[]{:S(2)}, u32[]{:S(2)}) collective-permute-start(bf16[1024,128]{1,0:T(8,128)(2,1)S(1)} %constant_dynamic-update-slice_fusion.rest_1_), channel_id=1, source_target_pairs={{0,64},{8,72},{16,80},{24,88},{32,96},{40,104},{48,112},{56,120},{... | collective-permute-start | bytes 786440 | tf_op jit(solution)/shard_map/ppermute | solution.py:305
  17.8 16.6 %collective-permute-start.5 = (bf16[512,128]{1,0:T(8,128)(2,1)S(1)}, bf16[512,128]{1,0:T(8,128)(2,1)S(1)}, u32[]{:S(2)}, u32[]{:S(2)}) collective-permute-start(bf16[512,128]{1,0:T(8,128)(2,1)S(1)} %get-tuple-element.38), channel_id=1, source_target_pairs={{0,8},{8,16},{16,24},{24,32},{32,40},{40,48},{48,56},{56,64},{64,7... | collective-permute-start | bytes 393224 | tf_op jit(solution)/shard_map/ppermute | solution.py:305
  18.2 14.9 %copy-start.2 = (bf16[128,1024]{1,0:T(8,128)(2,1)S(1)}, bf16[128,1024]{1,0:T(8,128)(2,1)}, u32[]{:S(2)}) copy-start(bf16[128,1024]{1,0:T(8,128)(2,1)} %q_ref.3) | copy-start | bytes 786436
  18.2 14.9 %copy-start.3 = (f32[1,128,128]{2,1,0:T(8,128)S(1)}, f32[1,128,128]{2,1,0:T(8,128)}, u32[]{:S(2)}) copy-start(f32[1,128,128]{2,1,0:T(8,128)} %kmap_ref.5) | copy-start | bytes 196612
  18.2 14.9 %copy-start.4 = (bf16[128,128]{1,0:T(8,128)(2,1)S(1)}, bf16[128,128]{1,0:T(8,128)(2,1)}, u32[]{:S(2)}) copy-start(bf16[128,128]{1,0:T(8,128)(2,1)} %k_ref.1) | copy-start | bytes 98308
  18.2 16.2 %collective-permute-start.6 = (bf16[512,128]{1,0:T(8,128)(2,1)S(1)}, bf16[512,128]{1,0:T(8,128)(2,1)S(1)}, u32[]{:S(2)}, u32[]{:S(2)}) collective-permute-start(bf16[512,128]{1,0:T(8,128)(2,1)S(1)} %get-tuple-element.37), channel_id=1, source_target_pairs={{0,248},{8,0},{16,8},{24,16},{32,24},{40,32},{48,40},{56,48},{64,5... | collective-permute-start | bytes 393224 | tf_op jit(solution)/shard_map/ppermute | solution.py:305
  28.2 7.2 %collective-permute-start.7 = (bf16[512,128]{1,0:T(8,128)(2,1)S(1)}, bf16[512,128]{1,0:T(8,128)(2,1)S(1)}, u32[]{:S(2)}, u32[]{:S(2)}) collective-permute-start(bf16[512,128]{1,0:T(8,128)(2,1)S(1)} %get-tuple-element.36), channel_id=1, source_target_pairs={{0,8},{8,16},{16,24},{24,32},{32,40},{40,48},{48,56},{56,64},{64,7... | collective-permute-start | bytes 393224 | tf_op jit(solution)/shard_map/ppermute | solution.py:305
  28.3 4.8 %copy-start.6 = (s32[128]{0:T(128)S(1)}, s32[128]{0:T(128)}, u32[]{:S(2)}) copy-start(s32[128]{0:T(128)} %param.9) | copy-start | bytes 1540
  28.3 7.1 %collective-permute-start.8 = (bf16[512,128]{1,0:T(8,128)(2,1)S(1)}, bf16[512,128]{1,0:T(8,128)(2,1)S(1)}, u32[]{:S(2)}, u32[]{:S(2)}) collective-permute-start(bf16[512,128]{1,0:T(8,128)(2,1)S(1)} %get-tuple-element.35), channel_id=1, source_target_pairs={{0,248},{8,0},{16,8},{24,16},{32,24},{40,32},{48,40},{56,48},{64,5... | collective-permute-start | bytes 393224 | tf_op jit(solution)/shard_map/ppermute | solution.py:305
  49.3 22.4 %all-to-all-start = ((f32[32,48,128]{2,1,0:T(8,128)}), f32[32,48,128]{2,1,0:T(8,128)S(1)}, u32[]{:S(2)}, u32[]{:S(2)}) async-start(f32[32,48,128]{2,1,0:T(8,128)} %get-tuple-element.26), calls=%async_computation | async-start | bytes 1572864 | tf_op jit(solution)/shard_map/all_to_all | solution.py:339
  97.8 17.6 %all-to-all-start.2 = ((f32[8,8,128]{2,1,0:T(8,128)}), f32[8,8,128]{2,1,0:T(8,128)S(1)}, u32[]{:S(2)}, u32[]{:S(2)}) async-start(f32[8,8,128]{2,1,0:T(8,128)} %head_squares.1), calls=%async_computation.2 | async-start | bytes 65536 | tf_op jit(solution)/shard_map/all_to_all | solution.py:355
  110.7 1.5 %copy-start = (f32[32,48,128]{2,1,0:T(8,128)S(1)}, f32[32,48,128]{2,1,0:T(8,128)}, u32[]{:S(2)}) copy-start(f32[32,48,128]{2,1,0:T(8,128)} %all_to_all.15.got_ref.tail_ref) | copy-start | bytes 2359300
  110.7 1.5 %copy-start.5 = (bf16[128,128]{1,0:T(8,128)(2,1)S(1)}, bf16[128,128]{1,0:T(8,128)(2,1)}, u32[]{:S(2)}) copy-start(bf16[128,128]{1,0:T(8,128)(2,1)} %v_ref.1) | copy-start | bytes 98308

commit v3 on v2

--- a/solution.py
+++ b/solution.py
@@ -15,9 +15,11 @@
 T = 128
 WINDOW = 16
 KEYS = (WINDOW + 1) * T
-CHUNK = 1024
+CHUNK = 2048
 PIECE = 48
 STATE_ROW, KMAP_ROW, NORM_ROW, INFO_ROW = 32, 40, 44, 46
+REPLY = 56
+HIGH_ROW, LOW_ROW, KEY_ROW, SQUARE_ROW = 32, 40, 48, 52
 
 
 def nn(a, b):
@@ -59,20 +61,20 @@
     return form(parts[0], b) + form(parts[1], b)
 
 
+def row_sums(x):
+    return exact_right(nn, split2(x), jnp.ones((T, T), BF16))
+
+
 def feature_map(logits):
     upper = jnp.exp(logits - jnp.max(logits, axis=-1, keepdims=True))
     lower = jnp.exp(jnp.min(logits, axis=-1, keepdims=True) - logits)
-    upper = upper * (1.0 / jnp.sum(upper, axis=-1, keepdims=True))
-    lower = lower * (1.0 / jnp.sum(lower, axis=-1, keepdims=True))
-    return upper, lower
+    return jnp.concatenate([upper / row_sums(upper), lower / row_sums(lower)], axis=1)
 
 
 def feature_back(phi, grad):
     upper, lower = phi[:, :T], phi[:, T:]
     up, low = grad[:, :T], grad[:, T:]
-    up = upper * (up - jnp.sum(upper * up, axis=-1, keepdims=True))
-    low = lower * (low - jnp.sum(lower * low, axis=-1, keepdims=True))
-    return up - low
+    return upper * (up - row_sums(upper * up)) - lower * (low - row_sums(lower * low))
 
 
 def column_of(row):
@@ -99,15 +101,13 @@
     row, start = positions_of(pos_ref)
     key = lax.broadcasted_iota(jnp.int32, (T, T), 1).astype(F32)
     seen = every_head(((key <= row) & (key >= start)).astype(F32), heads)
-    own = jnp.concatenate(
-        feature_map(exact_left(nn, k_ref[...], split3(kmap_ref[0]))), axis=1
-    )
+    own = feature_map(exact_left(nn, k_ref[...], split3(kmap_ref[0])))
     own_ref[...] = own
     logits = jnp.concatenate(
         [exact_left(nn, q_ref[:, h * T : h * T + T], split3(qmap_ref[h])) for h in range(heads)],
         axis=0,
     )
-    phi = jnp.concatenate(feature_map(logits), axis=1)
+    phi = feature_map(logits)
     phi_ref[...] = phi
     inner_ref[...] = product(nt, split2(phi), split2(own)) * seen
 
@@ -120,61 +120,78 @@
     heads = q_ref.shape[1] // T
     row, start = positions_of(pos_ref)
     entry = -pos_ref[0:1, 0:1].astype(F32)
+    crossing = (start < 0.0).astype(F32)
+    lane = lax.broadcasted_iota(jnp.int32, (T, T), 1)
     for ref, held in zip(blocks, places):
         for slot, block in enumerate(held):
             at = (WINDOW - block) * T
-            k_s[at : at + T, :] = ref[slot * 2 * T : slot * 2 * T + T, :]
-            v_s[at : at + T, :] = ref[slot * 2 * T + T : slot * 2 * T + 2 * T, :]
+            k_s[at : at + T, :T] = ref[slot * 2 * T : slot * 2 * T + T, :]
+            v_s[at : at + T, :T] = ref[slot * 2 * T + T : slot * 2 * T + 2 * T, :]
+            hidden = jnp.where(row - float(block * T) >= entry, 0.0, NEGATIVE)
+            hidden = jnp.where(lane == 0, NEGATIVE, jnp.where(lane == 1, hidden, 0.0))
+            k_s[at : at + T, T:] = (hidden if block else jnp.zeros((T, T), F32)).astype(BF16)
+    v_s[:, T:] = jnp.ones((KEYS, T), BF16)
 
     map_parts = split3(kmap_ref[0])
-    state = jnp.zeros((2 * T, T), F32)
-    norms = jnp.zeros((1, 2 * T), F32)
+    state = jnp.zeros((2 * T, 2 * T), F32)
     for at in range(0, WINDOW * T, CHUNK):
         key_row = lax.broadcasted_iota(jnp.int32, (CHUNK, 1), 0) + (at - WINDOW * T)
-        features = jnp.concatenate(
-            feature_map(exact_left(nn, k_s[at : at + CHUNK, :], map_parts)), axis=1
-        )
+        features = feature_map(exact_left(nn, k_s[at : at + CHUNK, :T], map_parts))
         features = jnp.where(key_row.astype(F32) >= entry, features, 0.0)
         phi_s[at : at + CHUNK, :] = features
         state = state + exact_right(tn, split2(features), v_s[at : at + CHUNK, :])
-        norms = norms + jnp.sum(features, axis=0, keepdims=True)
+    norms = jnp.transpose(state[:, T:])[0:1, :]
     state = split2(state)
 
-    key = lax.broadcasted_iota(jnp.int32, (T, KEYS), 1).astype(F32) - float(WINDOW * T)
-    visible = (key <= row) & (key >= start)
+    own_key = lane.astype(F32)
+    visible = (own_key <= row) & (own_key >= start)
+    seen = every_head(visible.astype(F32), heads)
     bias = every_head(jnp.where(visible, 0.0, NEGATIVE), heads)
-    seen = every_head(visible[:, WINDOW * T :].astype(F32), heads)
-    cross = every_head((start < 0.0).astype(F32), heads)
-    queries = stacked(q_ref)
-    scores = nt(queries, k_s[...]) * (1.0 / math.sqrt(T)) + bias
-    weights = jnp.exp(scores - jnp.max(scores, axis=-1, keepdims=True))
-    total = jnp.sum(weights, axis=-1, keepdims=True)
-    teacher = nn(weights.astype(BF16), v_s[...]) / total
+    cross = every_head(jnp.broadcast_to(crossing, (T, T)), heads)
+    hider = jnp.where(lane == 0, 1.0 - crossing, jnp.where(lane == 1, 1.0, 0.0)).astype(BF16)
+    queries = jnp.concatenate([stacked(q_ref), every_head(hider, heads)], axis=1)
+    scores = nt(queries, k_s[...])
+    near = scores[:, WINDOW * T :] + bias
+    far = scores[:, : WINDOW * T]
+    highest = jnp.maximum(
+        jnp.max(near, axis=-1, keepdims=True), jnp.max(far, axis=-1, keepdims=True)
+    )
+    rate = math.log2(math.e) / math.sqrt(T)
+    near = jnp.exp2((near - highest) * rate)
+    far = jnp.exp2((far - highest) * rate)
+    total = jnp.sum(near, axis=-1, keepdims=True) + jnp.sum(far, axis=-1, keepdims=True)
+    own_v = v_s[WINDOW * T :, :]
+    teacher = nn(near.astype(BF16), own_v[:, :T]) + nn(far.astype(BF16), v_s[: WINDOW * T, :T])
+    teacher = teacher / total
 
     own = own_ref[...]
-    own_v = v_s[WINDOW * T :, :]
     own_phi = split2(own)
     phi = phi_ref[...]
     phi_parts = split2(phi)
-    inner = inner_ref[...]
-    numer = exact_right(nn, split2(inner), own_v) + cross * product(nn, phi_parts, state)
-    denom = jnp.sum(inner, axis=-1, keepdims=True) + cross * jnp.sum(
-        phi * norms, axis=-1, keepdims=True
-    )
-    outputs = numer / denom
+    near = exact_right(nn, split2(inner_ref[...]), own_v)
+    far = product(nn, phi_parts, state)
+    inverse = 1.0 / (near[:, T:] + cross * far[:, T:])
+    outputs = (near[:, :T] + cross * far[:, :T]) * inverse
     error = outputs - teacher
 
-    grad_numer = error / denom
-    grad_denom = -jnp.sum(error * outputs, axis=-1, keepdims=True) / denom
+    grad_numer = error * inverse
+    grad_denom = -row_sums(error * outputs) * inverse
     gn_ref[...] = grad_numer
-    far_parts = split2(cross * grad_numer)
+    far_numer = cross * grad_numer
     far_denom = cross * grad_denom
-    mixing_parts = split2((exact_right(nt, split2(grad_numer), own_v) + grad_denom) * seen)
-    grad_phi = (
-        product(nn, mixing_parts, own_phi) + product(nt, far_parts, state) + far_denom * norms
-    )
-    back = product(tn, phi_parts, far_parts)
-    backn = jnp.sum(phi * far_denom, axis=0, keepdims=True)
+    mixing = (exact_right(nt, split2(grad_numer), own_v[:, :T]) + grad_denom) * seen
+    mixing_parts = split2(mixing)
+    near = product(nn, mixing_parts, own_phi)
+    far = product(nt, split2(far_numer), [part[:, :T] for part in state])
+    grad_phi = jnp.concatenate(
+        [
+            near[:, :T] + far[:, :T] + far_denom * norms[:, :T],
+            near[:, T:] + far[:, T:] + far_denom * norms[:, T:],
+        ],
+        axis=1,
+    )
+    back = product(tn, phi_parts, split2(jnp.concatenate([far_numer, far_denom], axis=1)))
+    backn = jnp.transpose(back[:, T:])[0:1, :]
     gkphi = product(tn, mixing_parts, phi_parts)
     gkphi_ref[...] = gkphi
     dlogit = feature_back(phi, grad_phi)
@@ -187,16 +204,16 @@
             payload_ref[4 * h + quarter, 0:STATE_ROW, :] = grad_map[
                 quarter * 32 : quarter * 32 + 32, :
             ]
-    back_parts = split2(back)
     for piece in range(32):
-        payload_ref[piece, STATE_ROW : STATE_ROW + 8, :] = back[piece * 8 : piece * 8 + 8, :]
+        payload_ref[piece, STATE_ROW : STATE_ROW + 8, :] = back[piece * 8 : piece * 8 + 8, :T]
 
     part = split2(feature_back(own, gkphi))
-    grad_map = exact_left(tn, k_s[WINDOW * T :, :], part)
+    grad_map = exact_left(tn, k_s[WINDOW * T :, :T], part)
+    back_parts = split2(jnp.concatenate([back[:, :T], back[:, T:] * (1.0 / T)], axis=1))
     for at in range(0, WINDOW * T, CHUNK):
-        grad = exact_left(nt, v_s[at : at + CHUNK, :], back_parts) + backn
+        grad = exact_left(nt, v_s[at : at + CHUNK, :], back_parts)
         part = split2(feature_back(phi_s[at : at + CHUNK, :], grad))
-        grad_map = grad_map + exact_left(tn, k_s[at : at + CHUNK, :], part)
+        grad_map = grad_map + exact_left(tn, k_s[at : at + CHUNK, :T], part)
     tail = jnp.concatenate(
         [
             backn[:, :T],
@@ -219,28 +236,29 @@
     gv_ref[...] = product(tn, split2(inner_ref[...]), split2(gn_ref[...]))
 
 
-def middle_kernel(me_ref, got_ref, out_ref, norms_ref):
+def middle_kernel(me_ref, got_ref, out_ref, norms_ref, state_s):
     pieces = got_ref.shape[0]
     total = got_ref[0]
     for i in range(1, pieces):
         total = total + got_ref[i]
-    squares = jnp.sum(total[0:STATE_ROW, :] * total[0:STATE_ROW, :]) + jnp.sum(
-        total[KMAP_ROW:NORM_ROW, :] * total[KMAP_ROW:NORM_ROW, :]
-    )
-    tail = jnp.concatenate(
-        [total[KMAP_ROW:INFO_ROW, :], jnp.full((2, T), squares, F32)], axis=0
-    )
+    qmap, kmap = total[0:STATE_ROW, :], total[KMAP_ROW:NORM_ROW, :]
+    squares = jnp.sum(qmap * qmap) + jnp.sum(kmap * kmap)
+    parts = [part.astype(F32) for part in split3(jnp.full((1, T), squares, F32))]
+    tail = jnp.concatenate([kmap] + parts + [jnp.zeros((1, T), F32)], axis=0).astype(BF16)
+    qmap = qmap.astype(BF16)
     for j in range(pieces):
-        out_ref[j, 0:STATE_ROW, :] = total[0:STATE_ROW, :]
-        out_ref[j, KMAP_ROW:PIECE, :] = tail
+        out_ref[j, 0:HIGH_ROW, :] = qmap
+        out_ref[j, KEY_ROW:REPLY, :] = tail
     sender = lax.broadcasted_iota(jnp.int32, (pieces, T), 0)
     target = lax.broadcasted_iota(jnp.int32, (pieces, T), 1)
     first = (sender * T).astype(F32) - got_ref[:, INFO_ROW, :]
     links = (sender > target) & (first <= (target * T + (T - 1)).astype(F32))
     reach = links.astype(F32)[:, :pieces].astype(BF16)
     for i in range(8):
-        high, middle, low = split3(got_ref[:, STATE_ROW + i, :])
-        out_ref[:, STATE_ROW + i, :] = tn(reach, high) + (tn(reach, middle) + tn(reach, low))
+        state_s[:, i, :] = exact_left(tn, reach, split3(got_ref[:, STATE_ROW + i, :]))
+    high, low = split2(state_s[...])
+    out_ref[:, HIGH_ROW:LOW_ROW, :] = high
+    out_ref[:, LOW_ROW:KEY_ROW, :] = low
     me = me_ref[0]
     mine = (sender > me) & (first <= (me * T + (T - 1)).astype(F32))
     for half in range(2):
@@ -254,9 +272,10 @@
     last_start = float(T - 1) - pos_ref[0:1, T - 1 : T].astype(F32)
     keeping = (start == last_start).astype(F32)
     pieces = got_ref.shape[0]
-    back = split2(
-        jnp.concatenate([got_ref[r, STATE_ROW : STATE_ROW + 8, :] for r in range(pieces)], axis=0)
-    )
+    back = [
+        jnp.concatenate([got_ref[r, at : at + 8, :] for r in range(pieces)], axis=0)
+        for at in (HIGH_ROW, LOW_ROW)
+    ]
     phi = phi_ref[...]
     own_v = v_ref[...]
     grad = gkphi_ref[...] + keeping * (exact_left(nt, own_v, back) + norms_ref[...])
@@ -265,7 +284,8 @@
 
 
 def squares_kernel(tail_ref, out_ref):
-    total = jnp.sum(tail_ref[:, INFO_ROW - KMAP_ROW, :], axis=0, keepdims=True)
+    total = jnp.sum(tail_ref[:, KEY_ROW:REPLY, :].astype(F32), axis=0)
+    total = jnp.sum(total[SQUARE_ROW - KEY_ROW : SQUARE_ROW - KEY_ROW + 3, :], axis=0)
     out_ref[...] = jnp.broadcast_to(total.reshape(1, 1, T), out_ref.shape)
 
 
@@ -275,8 +295,9 @@
     factor = jnp.minimum(1.0, limit / (jnp.sqrt(squared) + EPSILON))
     for piece in range(pieces):
         rows = slice(piece % 4 * 32, piece % 4 * 32 + 32)
-        qmap_ref[piece // 4, rows, :] = factor * got_ref[piece, 0:STATE_ROW, :]
-        kmap_ref[0, piece * 4 : piece * 4 + 4, :] = factor * got_ref[piece, KMAP_ROW:NORM_ROW, :]
+        qmap_ref[piece // 4, rows, :] = factor * got_ref[piece, 0:HIGH_ROW, :].astype(F32)
+        tail = got_ref[piece, KEY_ROW:REPLY, :].astype(F32)
+        kmap_ref[0, piece * 4 : piece * 4 + 4, :] = factor * tail[0 : SQUARE_ROW - KEY_ROW, :]
 
 
 def call(body, name, ins, outs, scratch=(), limit=32):
@@ -284,7 +305,10 @@
         body,
         in_specs=[pl.BlockSpec(memory_space=space) for space in ins],
         out_specs=[pl.BlockSpec(memory_space=pltpu.VMEM)] * len(outs),
-        out_shape=[jax.ShapeDtypeStruct(shape, F32) for shape in outs],
+        out_shape=[
+            out if isinstance(out, jax.ShapeDtypeStruct) else jax.ShapeDtypeStruct(out, F32)
+            for out in outs
+        ],
         scratch_shapes=list(scratch),
         compiler_params=pltpu.CompilerParams(vmem_limit_bytes=limit << 20),
         name=name,
@@ -333,7 +357,7 @@
         "attention_transfer",
         [V] * (6 + len(arrays)),
         [(pieces, PIECE, T), (rows, T), (rows, T), (T, 2 * T)],
-        [V((KEYS, T), BF16), V((KEYS, T), BF16), V((WINDOW * T, 2 * T), F32)],
+        [V((KEYS, 2 * T), BF16), V((KEYS, 2 * T), BF16), V((WINDOW * T, 2 * T), F32)],
         32,
     )(pos, queries, key_map, phi, inner, own, *arrays)
     gathered = lax.all_to_all(payload, "seq", 0, 0)
@@ -341,17 +365,14 @@
         query_kernel, "query_gradients", [V] * 4, [(T, rows), (T, T)]
     )(dlogit, inner, grad_numer, query_map)
     reduced, norms = call(
-        middle_kernel, "sum_pieces", [pltpu.SMEM, V], [(pieces, PIECE, T), (1, 2 * T)]
+        middle_kernel,
+        "sum_pieces",
+        [pltpu.SMEM, V],
+        [jax.ShapeDtypeStruct((pieces, REPLY, T), BF16), (1, 2 * T)],
+        [V((pieces, 8, T), F32)],
     )(me, gathered)
     back = lax.all_to_all(reduced, "seq", 0, 0)
-    squares = pl.pallas_call(
-        squares_kernel,
-        grid=(1,),
-        in_specs=[pl.BlockSpec((pieces, PIECE - KMAP_ROW, T), lambda i: (0, KMAP_ROW // 8, 0))],
-        out_specs=pl.BlockSpec((heads, 8, T), lambda i: (0, 0, 0)),
-        out_shape=jax.ShapeDtypeStruct((heads, 8, T), F32),
-        name="head_squares",
-    )(back)
+    squares = call(squares_kernel, "head_squares", [V], [(heads, 8, T)])(back)[0]
     squares = lax.all_to_all(squares, "head", 0, 0)
     grad_keys, grad_values = call(last_kernel, "key_gradients", [V] * 8, [(T, T), (T, T)])(
         pos, back, norms, value_vectors, key_map, own, gkphi, near_values

time: 117 us -> 110 us (0.940)
  blocking collectives: 23.9 us -> 19 us
    all_to_all x1, blocking collectives: 23.9 us -> 19 us  [on_device(): back = lax.all_to_all(reduced, 'seq', 0, 0)]
  transfers between devices with their start and end apart: 11 -> 11, of which waited for: 6 -> 6; matrix products, arithmetic and copies ran while one was open for 0% -> 0% of each run, Pallas kernels for 3% -> 4%
where the time goes in v3:
time: 110 us
  starting transfers between devices  40.7 us (37%)
  waiting for transfers between devices  28 us (25%)
  Pallas kernels  20.2 us (18%)
  blocking collectives  19 us (17%)
    ppermute x9, starting transfers between devices, shift(): return lax.ppermute(x, 'seq', [(i, (i + k) % n) for i in range(n)])  22.3 us
    all_to_all x1, blocking collectives, on_device(): back = lax.all_to_all(reduced, 'seq', 0, 0)  19 us
    all_to_all x1, waiting for transfers between devices, on_device(): gathered = lax.all_to_all(payload, 'seq', 0, 0)  15.9 us
    pallas_call x1, Pallas kernels, on_device(): call(functools.partial(main_kernel, places), 'attention_transfer', [V] *...  13.8 us
    all_to_all x1, starting transfers between devices, on_device(): squares = lax.all_to_all(squares, 'head', 0, 0)  11.9 us
    ppermute x9, waiting for transfers between devices, shift(): return lax.ppermute(x, 'seq', [(i, (i + k) % n) for i in range(n)])  10 us
    all_to_all x1, starting transfers between devices, on_device(): gathered = lax.all_to_all(payload, 'seq', 0, 0)  6.45 us
  transfers between devices with their start and end apart: 11, of which 6 were waited for; matrix products, arithmetic and copies ran while one was open for 0% of the time, Pallas kernels for 4%

profile of v3, /device:TPU:1, one launch (start us, length us, event | category | flops | bytes accessed | tf_op | source)
XLA Modules:
  0.0 109.6 jit_solution(7365056333080567585)
XLA Ops:
  0.6 0.8 pad_add_fusion.rest_0_
  1.4 2.0 %collective-permute-start = (bf16[256,128]{1,0:T(8,128)(2,1)S(1)}, bf16[256,128]{1,0:T(8,128)(2,1)S(1)}, u32[]{:S(2)}, u32[]{:S(2)}) collective-permute-start(bf16[256,128]{1,0:T(8,128)(2,1)S(1)} %pad_add_fusion.rest_0_), channel_id=1, source_target_pairs={{0,64},{8,72},{16,80},{24,88},{32,96},{40,104},{48,112},{56,120},{... | collective-permute-start | bytes 196616 | tf_op jit(solution)/shard_map/ppermute | solution.py:329
  3.5 1.6 %collective-permute-start.1 = (bf16[256,128]{1,0:T(8,128)(2,1)S(1)}, bf16[256,128]{1,0:T(8,128)(2,1)S(1)}, u32[]{:S(2)}, u32[]{:S(2)}) collective-permute-start(bf16[256,128]{1,0:T(8,128)(2,1)S(1)} %pad_add_fusion.rest_0_), channel_id=1, source_target_pairs={{0,8},{8,16},{16,24},{24,32},{32,40},{40,48},{48,56},{56,64},{64,7... | collective-permute-start | bytes 196616 | tf_op jit(solution)/shard_map/ppermute | solution.py:329
  5.1 6.0 %collective-permute-start.2 = (bf16[256,128]{1,0:T(8,128)(2,1)S(1)}, bf16[256,128]{1,0:T(8,128)(2,1)S(1)}, u32[]{:S(2)}, u32[]{:S(2)}) collective-permute-start(bf16[256,128]{1,0:T(8,128)(2,1)S(1)} %pad_add_fusion.rest_0_), channel_id=1, source_target_pairs={{0,32},{8,40},{16,48},{24,56},{32,64},{40,72},{48,80},{56,88},{64,... | collective-permute-start | bytes 196616 | tf_op jit(solution)/shard_map/ppermute | solution.py:329
  11.1 2.9 %collective-permute-start.3 = (bf16[256,128]{1,0:T(8,128)(2,1)S(1)}, bf16[256,128]{1,0:T(8,128)(2,1)S(1)}, u32[]{:S(2)}, u32[]{:S(2)}) collective-permute-start(bf16[256,128]{1,0:T(8,128)(2,1)S(1)} %pad_add_fusion.rest_0_), channel_id=1, source_target_pairs={{0,56},{8,64},{16,72},{24,80},{32,88},{40,96},{48,104},{56,112},{6... | collective-permute-start | bytes 196616 | tf_op jit(solution)/shard_map/ppermute | solution.py:329
  14.0 0.0 collective-permute-done
  14.0 0.0 collective-permute-done.1
  14.0 0.7 collective-permute-done.2
  14.7 2.9 %collective-permute-done.3 = bf16[256,128]{1,0:T(8,128)(2,1)S(1)} collective-permute-done((bf16[256,128]{1,0:T(8,128)(2,1)S(1)}, bf16[256,128]{1,0:T(8,128)(2,1)S(1)}, u32[]{:S(2)}, u32[]{:S(2)}) %collective-permute-start.3) | collective-permute-done | bytes 65568 | tf_op jit(solution)/shard_map/ppermute | solution.py:329
  17.7 0.0 copy-start
  17.7 0.1 collective-permute-start.4
  17.8 0.4 collective-permute-start.5
  18.2 0.0 copy-start.1
  18.2 0.0 copy-start.2
  18.2 0.0 copy-start.3
  18.2 4.5 %collective-permute-start.6 = (bf16[512,128]{1,0:T(8,128)(2,1)S(1)}, bf16[512,128]{1,0:T(8,128)(2,1)S(1)}, u32[]{:S(2)}, u32[]{:S(2)}) collective-permute-start(bf16[512,128]{1,0:T(8,128)(2,1)S(1)} %get-tuple-element.37), channel_id=1, source_target_pairs={{0,248},{8,0},{16,8},{24,16},{32,24},{40,32},{48,40},{56,48},{64,5... | collective-permute-start | bytes 393224 | tf_op jit(solution)/shard_map/ppermute | solution.py:329
  22.7 5.5 %collective-permute-done.4.rest_2_ = bf16[1024,128]{1,0:T(8,128)(2,1)S(1)} collective-permute-done((bf16[1024,128]{1,0:T(8,128)(2,1)S(1)}, bf16[1024,128]{1,0:T(8,128)(2,1)S(1)}, u32[]{:S(2)}, u32[]{:S(2)}) %collective-permute-start.4) | collective-permute-done | bytes 262176 | tf_op jit(solution)/shard_map/ppermute | solution.py:329
  28.2 0.1 collective-permute-start.7
  28.3 0.0 copy-start.5
  28.3 4.8 %collective-permute-start.8 = (bf16[512,128]{1,0:T(8,128)(2,1)S(1)}, bf16[512,128]{1,0:T(8,128)(2,1)S(1)}, u32[]{:S(2)}, u32[]{:S(2)}) collective-permute-start(bf16[512,128]{1,0:T(8,128)(2,1)S(1)} %get-tuple-element.35), channel_id=1, source_target_pairs={{0,248},{8,0},{16,8},{24,16},{32,24},{40,32},{48,40},{56,48},{64,5... | collective-permute-start | bytes 393224 | tf_op jit(solution)/shard_map/ppermute | solution.py:329
  33.1 0.0 copy-done
  33.1 0.0 copy-done.1
  33.1 0.0 copy-done.2
  33.1 0.0 copy-done.3
  33.1 0.0 copy-done.5
  33.1 1.4 %local_features.1 = (f32[1024,256]{1,0:T(8,128)S(1)}, f32[1024,128]{1,0:T(8,128)S(1)}, f32[128,256]{1,0:T(8,128)S(1)}) custom-call(s32[1,128]{1,0:T(1,128)S(1)} %bitcast.2, bf16[128,1024]{1,0:T(8,128)(2,1)S(1)} %copy-done.1, bf16[128,128]{1,0:T(8,128)(2,1)S(1)} %copy-done.3, f32[8,128,128]{2,1,0:T(8,128)S(1)} %copy-done, f32[1,128,128]{2,1,0:T(8,128)S(1)} %copy-done.2), custom_call_target="tpu_custom_call" | custom-call | tf_op jit(solution)/shard_map/local_features/pallas_call | solution.py:352
  34.6 0.0 collective-permute-done.5.rest_3_
  34.6 0.0 collective-permute-done.6.rest_4_
  34.6 0.9 collective-permute-done.7.rest_5_
  35.5 0.0 collective-permute-done.8.rest_6_
  35.5 13.8 %attention_transfer.1 = (f32[32,48,128]{2,1,0:T(8,128)}, f32[1024,128]{1,0:T(8,128)S(1)}, f32[1024,128]{1,0:T(8,128)S(1)}, f32[128,256]{1,0:T(8,128)S(1)}) custom-call(s32[1,128]{1,0:T(1,128)S(1)} %bitcast.3, bf16[128,1024]{1,0:T(8,128)(2,1)S(1)} %copy-done.1, f32[1,128,128]{2,1,0:T(8,128)S(1)} %copy-done.2, f32[1024,256]{1,0:T(8,128)S(1)} %get-tuple-element.20.phi_ref, ...), custom_call_target="tpu_custom_call" | custom-call | tf_op jit(solution)/shard_map/attention_transfer/pallas_call | solution.py:355
  49.3 6.4 %all-to-all-start = ((f32[32,48,128]{2,1,0:T(8,128)}), f32[32,48,128]{2,1,0:T(8,128)S(1)}, u32[]{:S(2)}, u32[]{:S(2)}) async-start(f32[32,48,128]{2,1,0:T(8,128)} %get-tuple-element.26), calls=%async_computation | async-start | bytes 1572864 | tf_op jit(solution)/shard_map/all_to_all | solution.py:363
  55.7 15.9 %all-to-all-done.got_ref = f32[32,48,128]{2,1,0:T(8,128)S(1)} async-done(((f32[32,48,128]{2,1,0:T(8,128)}), f32[32,48,128]{2,1,0:T(8,128)S(1)}, u32[]{:S(2)}, u32[]{:S(2)}) %all-to-all-start) | async-done | bytes 786464 | tf_op jit(solution)/shard_map/all_to_all | solution.py:363
  71.7 0.7 sum_pieces.1
  72.4 19.0 %all_to_all.15.got_ref.tail_ref = bf16[32,56,128]{2,1,0:T(8,128)(2,1)S(1)} all-to-all(bf16[32,56,128]{2,1,0:T(8,128)(2,1)S(1)} %get-tuple-element.27), channel_id=1, replica_groups=mesh['seq'=32,'head'=8] {'seq'}, dimensions={0} | all-to-all | bytes 917504 | tf_op jit(solution)/shard_map/all_to_all | solution.py:374
  91.4 0.7 head_squares.1
  92.1 11.9 %all-to-all-start.2 = ((f32[8,8,128]{2,1,0:T(8,128)}), f32[8,8,128]{2,1,0:T(8,128)S(1)}, u32[]{:S(2)}, u32[]{:S(2)}) async-start(f32[8,8,128]{2,1,0:T(8,128)} %head_squares.1), calls=%async_computation.2 | async-start | bytes 65536 | tf_op jit(solution)/shard_map/all_to_all | solution.py:376
  104.0 0.0 copy-start.4
  104.0 1.5 %query_gradients.1 = (f32[128,1024]{1,0:T(8,128)}, f32[128,128]{1,0:T(8,128)S(1)}) custom-call(f32[1024,128]{1,0:T(8,128)S(1)} %get-tuple-element.23.dlogit_ref, f32[1024,128]{1,0:T(8,128)S(1)} %get-tuple-element.21.inner_ref, f32[1024,128]{1,0:T(8,128)S(1)} %get-tuple-element.24.gn_ref, f32[8,128,128]{2,1,0:T(8,128)S(1)} %copy-done), custom_call_target="tpu_custom_call" | custom-call | tf_op jit(solution)/shard_map/query_gradients/pallas_call | solution.py:364
  105.5 0.0 copy-done.4
  105.5 1.2 %key_gradients.1 = (f32[128,128]{1,0:T(8,128)}, f32[128,128]{1,0:T(8,128)}) custom-call(s32[1,128]{1,0:T(1,128)S(1)} %bitcast.4, bf16[32,56,128]{2,1,0:T(8,128)(2,1)S(1)} %all_to_all.15.got_ref.tail_ref, f32[1,256]{1,0:T(1,128)S(1)} %get-tuple-element.28.norms_ref, bf16[128,128]{1,0:T(8,128)(2,1)S(1)} %copy-done.4, f32[1,128,128]{2,1,0:T(8,128)S(1)} %copy-done.2, ...), custom_call_target="tpu_custom_call" | custom-call | tf_op jit(solution)/shard_map/key_gradients/pallas_call | solution.py:377
  106.7 2.0 %all-to-all-done.2.squares_ref = f32[8,8,128]{2,1,0:T(8,128)S(1)} async-done(((f32[8,8,128]{2,1,0:T(8,128)}), f32[8,8,128]{2,1,0:T(8,128)S(1)}, u32[]{:S(2)}, u32[]{:S(2)}) %all-to-all-start.2) | async-done | bytes 32800 | tf_op jit(solution)/shard_map/all_to_all | solution.py:376
  108.7 0.9 clip_maps.1
  (6 shorter events, 0.1 us)
Async XLA Ops:
  1.4 12.6 %collective-permute-start = (bf16[256,128]{1,0:T(8,128)(2,1)S(1)}, bf16[256,128]{1,0:T(8,128)(2,1)S(1)}, u32[]{:S(2)}, u32[]{:S(2)}) collective-permute-start(bf16[256,128]{1,0:T(8,128)(2,1)S(1)} %pad_add_fusion.rest_0_), channel_id=1, source_target_pairs={{0,64},{8,72},{16,80},{24,88},{32,96},{40,104},{48,112},{56,120},{... | collective-permute-start | bytes 196616 | tf_op jit(solution)/shard_map/ppermute | solution.py:329
  3.5 10.5 %collective-permute-start.1 = (bf16[256,128]{1,0:T(8,128)(2,1)S(1)}, bf16[256,128]{1,0:T(8,128)(2,1)S(1)}, u32[]{:S(2)}, u32[]{:S(2)}) collective-permute-start(bf16[256,128]{1,0:T(8,128)(2,1)S(1)} %pad_add_fusion.rest_0_), channel_id=1, source_target_pairs={{0,8},{8,16},{16,24},{24,32},{32,40},{40,48},{48,56},{56,64},{64,7... | collective-permute-start | bytes 196616 | tf_op jit(solution)/shard_map/ppermute | solution.py:329
  5.1 9.6 %collective-permute-start.2 = (bf16[256,128]{1,0:T(8,128)(2,1)S(1)}, bf16[256,128]{1,0:T(8,128)(2,1)S(1)}, u32[]{:S(2)}, u32[]{:S(2)}) collective-permute-start(bf16[256,128]{1,0:T(8,128)(2,1)S(1)} %pad_add_fusion.rest_0_), channel_id=1, source_target_pairs={{0,32},{8,40},{16,48},{24,56},{32,64},{40,72},{48,80},{56,88},{64,... | collective-permute-start | bytes 196616 | tf_op jit(solution)/shard_map/ppermute | solution.py:329
  11.1 6.6 %collective-permute-start.3 = (bf16[256,128]{1,0:T(8,128)(2,1)S(1)}, bf16[256,128]{1,0:T(8,128)(2,1)S(1)}, u32[]{:S(2)}, u32[]{:S(2)}) collective-permute-start(bf16[256,128]{1,0:T(8,128)(2,1)S(1)} %pad_add_fusion.rest_0_), channel_id=1, source_target_pairs={{0,56},{8,64},{16,72},{24,80},{32,88},{40,96},{48,104},{56,112},{6... | collective-permute-start | bytes 196616 | tf_op jit(solution)/shard_map/ppermute | solution.py:329
  17.7 15.4 %copy-start = (f32[8,128,128]{2,1,0:T(8,128)S(1)}, f32[8,128,128]{2,1,0:T(8,128)}, u32[]{:S(2)}) copy-start(f32[8,128,128]{2,1,0:T(8,128)} %qmap_ref.3) | copy-start | bytes 1572868
  17.7 10.5 %collective-permute-start.4 = (bf16[1024,128]{1,0:T(8,128)(2,1)S(1)}, bf16[1024,128]{1,0:T(8,128)(2,1)S(1)}, u32[]{:S(2)}, u32[]{:S(2)}) collective-permute-start(bf16[1024,128]{1,0:T(8,128)(2,1)S(1)} %constant_dynamic-update-slice_fusion.rest_1_), channel_id=1, source_target_pairs={{0,64},{8,72},{16,80},{24,88},{32,96},{40,104},{48,112},{56,120},{... | collective-permute-start | bytes 786440 | tf_op jit(solution)/shard_map/ppermute | solution.py:329
  17.8 16.7 %collective-permute-start.5 = (bf16[512,128]{1,0:T(8,128)(2,1)S(1)}, bf16[512,128]{1,0:T(8,128)(2,1)S(1)}, u32[]{:S(2)}, u32[]{:S(2)}) collective-permute-start(bf16[512,128]{1,0:T(8,128)(2,1)S(1)} %get-tuple-element.38), channel_id=1, source_target_pairs={{0,8},{8,16},{16,24},{24,32},{32,40},{40,48},{48,56},{56,64},{64,7... | collective-permute-start | bytes 393224 | tf_op jit(solution)/shard_map/ppermute | solution.py:329
  18.2 14.9 %copy-start.1 = (bf16[128,1024]{1,0:T(8,128)(2,1)S(1)}, bf16[128,1024]{1,0:T(8,128)(2,1)}, u32[]{:S(2)}) copy-start(bf16[128,1024]{1,0:T(8,128)(2,1)} %q_ref.3) | copy-start | bytes 786436
  18.2 14.9 %copy-start.2 = (f32[1,128,128]{2,1,0:T(8,128)S(1)}, f32[1,128,128]{2,1,0:T(8,128)}, u32[]{:S(2)}) copy-start(f32[1,128,128]{2,1,0:T(8,128)} %kmap_ref.5) | copy-start | bytes 196612
  18.2 14.9 %copy-start.3 = (bf16[128,128]{1,0:T(8,128)(2,1)S(1)}, bf16[128,128]{1,0:T(8,128)(2,1)}, u32[]{:S(2)}) copy-start(bf16[128,128]{1,0:T(8,128)(2,1)} %k_ref.1) | copy-start | bytes 98308
  18.2 16.4 %collective-permute-start.6 = (bf16[512,128]{1,0:T(8,128)(2,1)S(1)}, bf16[512,128]{1,0:T(8,128)(2,1)S(1)}, u32[]{:S(2)}, u32[]{:S(2)}) collective-permute-start(bf16[512,128]{1,0:T(8,128)(2,1)S(1)} %get-tuple-element.37), channel_id=1, source_target_pairs={{0,248},{8,0},{16,8},{24,16},{32,24},{40,32},{48,40},{56,48},{64,5... | collective-permute-start | bytes 393224 | tf_op jit(solution)/shard_map/ppermute | solution.py:329
  28.2 7.2 %collective-permute-start.7 = (bf16[512,128]{1,0:T(8,128)(2,1)S(1)}, bf16[512,128]{1,0:T(8,128)(2,1)S(1)}, u32[]{:S(2)}, u32[]{:S(2)}) collective-permute-start(bf16[512,128]{1,0:T(8,128)(2,1)S(1)} %get-tuple-element.36), channel_id=1, source_target_pairs={{0,8},{8,16},{16,24},{24,32},{32,40},{40,48},{48,56},{56,64},{64,7... | collective-permute-start | bytes 393224 | tf_op jit(solution)/shard_map/ppermute | solution.py:329
  28.3 4.8 %copy-start.5 = (s32[128]{0:T(128)S(1)}, s32[128]{0:T(128)}, u32[]{:S(2)}) copy-start(s32[128]{0:T(128)} %param.9) | copy-start | bytes 1540
  28.3 7.1 %collective-permute-start.8 = (bf16[512,128]{1,0:T(8,128)(2,1)S(1)}, bf16[512,128]{1,0:T(8,128)(2,1)S(1)}, u32[]{:S(2)}, u32[]{:S(2)}) collective-permute-start(bf16[512,128]{1,0:T(8,128)(2,1)S(1)} %get-tuple-element.35), channel_id=1, source_target_pairs={{0,248},{8,0},{16,8},{24,16},{32,24},{40,32},{48,40},{56,48},{64,5... | collective-permute-start | bytes 393224 | tf_op jit(solution)/shard_map/ppermute | solution.py:329
  49.3 22.4 %all-to-all-start = ((f32[32,48,128]{2,1,0:T(8,128)}), f32[32,48,128]{2,1,0:T(8,128)S(1)}, u32[]{:S(2)}, u32[]{:S(2)}) async-start(f32[32,48,128]{2,1,0:T(8,128)} %get-tuple-element.26), calls=%async_computation | async-start | bytes 1572864 | tf_op jit(solution)/shard_map/all_to_all | solution.py:363
  92.1 16.6 %all-to-all-start.2 = ((f32[8,8,128]{2,1,0:T(8,128)}), f32[8,8,128]{2,1,0:T(8,128)S(1)}, u32[]{:S(2)}, u32[]{:S(2)}) async-start(f32[8,8,128]{2,1,0:T(8,128)} %head_squares.1), calls=%async_computation.2 | async-start | bytes 65536 | tf_op jit(solution)/shard_map/all_to_all | solution.py:376
  104.0 1.5 %copy-start.4 = (bf16[128,128]{1,0:T(8,128)(2,1)S(1)}, bf16[128,128]{1,0:T(8,128)(2,1)}, u32[]{:S(2)}) copy-start(bf16[128,128]{1,0:T(8,128)(2,1)} %v_ref.1) | copy-start | bytes 98308

commit v4 on v3

--- a/solution.py
+++ b/solution.py
@@ -325,15 +325,16 @@
     n = lax.axis_size("seq")
     size = kv.shape[0]
 
-    def shift(x, k):
-        return lax.ppermute(x, "seq", [(i, (i + k) % n) for i in range(n)])
-
-    b1, b4, b7, b8 = (shift(kv, k) for k in (1, 4, 7, 8))
+    def shift(x, k, ends=()):
+        pairs = [(i, (i + k) % n) for i in range(n) if 0 <= i + k < n or i in ends]
+        return lax.ppermute(x, "seq", pairs)
+
+    b8, b1, b4, b7 = shift(kv, 8), shift(kv, 1), shift(kv, 4, (n - 4,)), shift(kv, 7, (n - 7,))
     near = jnp.concatenate([b8, b1, b4, b7], axis=0)
-    far = shift(near, 8)
+    far = shift(near, 8, (n - 8,))
     up, down = slice(size, 3 * size), slice(2 * size, 4 * size)
-    n1, n2 = shift(near[up], 1), shift(near[down], -1)
-    f1, f2 = shift(far[up], 1), shift(far[down], -1)
+    n1, n2 = shift(near[up], 1), shift(near[down], -1, (0,))
+    f1, f2 = shift(far[up], 1), shift(far[down], -1, (0,))
     arrays = [kv, near, far, n1, n2, f1, f2]
     places = [(0,), (8, 1, 4, 7), (16, 9, 12, 15), (2, 5), (3, 6), (10, 13), (11, 14)]
     return arrays, places

time: 110 us -> 114 us (1.036)
  starting transfers between devices: 40.7 us -> 49.5 us
  waiting for transfers between devices: 28 us -> 24.9 us
  blocking collectives: 19 us -> 17 us
    ppermute x9, starting transfers between devices: 22.3 us -> 27.9 us  [shift(): return lax.ppermute(x, 'seq', pairs)]
    ppermute x9, waiting for transfers between devices: 10 us -> 6.65 us  [shift(): return lax.ppermute(x, 'seq', pairs)]
    all_to_all x1, starting transfers between devices: 6.45 us -> 9.5 us  [on_device(): gathered = lax.all_to_all(payload, 'seq', 0, 0)]
    all_to_all x1, blocking collectives: 19 us -> 17 us  [on_device(): back = lax.all_to_all(reduced, 'seq', 0, 0)]
  transfers between devices with their start and end apart: 11 -> 11, of which waited for: 6 -> 5; matrix products, arithmetic and copies ran while one was open for 0% -> 0% of each run, Pallas kernels for 4% -> 4%
where the time goes in v4:
time: 114 us; the launch traced here: 113 us
  starting transfers between devices  49.5 us (43%)
  waiting for transfers between devices  24.9 us (22%)
  Pallas kernels  20.2 us (18%)
  blocking collectives  17 us (15%)
    ppermute x9, starting transfers between devices, shift(): return lax.ppermute(x, 'seq', pairs)  27.9 us
    all_to_all x1, blocking collectives, on_device(): back = lax.all_to_all(reduced, 'seq', 0, 0)  17 us
    all_to_all x1, waiting for transfers between devices, on_device(): gathered = lax.all_to_all(payload, 'seq', 0, 0)  16.2 us
    pallas_call x1, Pallas kernels, on_device(): call(functools.partial(main_kernel, places), 'attention_transfer', [V] *...  13.8 us
    all_to_all x1, starting transfers between devices, on_device(): squares = lax.all_to_all(squares, 'head', 0, 0)  12 us
    all_to_all x1, starting transfers between devices, on_device(): gathered = lax.all_to_all(payload, 'seq', 0, 0)  9.5 us
    ppermute x9, waiting for transfers between devices, shift(): return lax.ppermute(x, 'seq', pairs)  6.65 us
  transfers between devices with their start and end apart: 11, of which 5 were waited for; matrix products, arithmetic and copies ran while one was open for 0% of the time, Pallas kernels for 4%

profile of v4, /device:TPU:1, one launch (start us, length us, event | category | flops | bytes accessed | tf_op | source)
XLA Modules:
  0.0 113.3 jit_solution(15334901379821395334)
XLA Ops:
  0.6 0.8 pad_add_fusion.rest_0_
  1.4 3.9 %collective-permute-start = (bf16[256,128]{1,0:T(8,128)(2,1)S(1)}, bf16[256,128]{1,0:T(8,128)(2,1)S(1)}, u32[]{:S(2)}, u32[]{:S(2)}) collective-permute-start(bf16[256,128]{1,0:T(8,128)(2,1)S(1)} %pad_add_fusion.rest_0_), channel_id=1, source_target_pairs={{0,64},{8,72},{16,80},{24,88},{32,96},{40,104},{48,112},{56,120},{... | collective-permute-start | bytes 196616 | tf_op jit(solution)/shard_map/ppermute | solution.py:330
  5.4 3.5 %collective-permute-start.1 = (bf16[256,128]{1,0:T(8,128)(2,1)S(1)}, bf16[256,128]{1,0:T(8,128)(2,1)S(1)}, u32[]{:S(2)}, u32[]{:S(2)}) collective-permute-start(bf16[256,128]{1,0:T(8,128)(2,1)S(1)} %pad_add_fusion.rest_0_), channel_id=1, source_target_pairs={{0,8},{8,16},{16,24},{24,32},{32,40},{40,48},{48,56},{56,64},{64,7... | collective-permute-start | bytes 196616 | tf_op jit(solution)/shard_map/ppermute | solution.py:330
  8.9 7.9 %collective-permute-start.2 = (bf16[256,128]{1,0:T(8,128)(2,1)S(1)}, bf16[256,128]{1,0:T(8,128)(2,1)S(1)}, u32[]{:S(2)}, u32[]{:S(2)}) collective-permute-start(bf16[256,128]{1,0:T(8,128)(2,1)S(1)} %pad_add_fusion.rest_0_), channel_id=1, source_target_pairs={{0,32},{8,40},{16,48},{24,56},{32,64},{40,72},{48,80},{56,88},{64,... | collective-permute-start | bytes 196616 | tf_op jit(solution)/shard_map/ppermute | solution.py:330
  16.8 4.8 %collective-permute-start.3 = (bf16[256,128]{1,0:T(8,128)(2,1)S(1)}, bf16[256,128]{1,0:T(8,128)(2,1)S(1)}, u32[]{:S(2)}, u32[]{:S(2)}) collective-permute-start(bf16[256,128]{1,0:T(8,128)(2,1)S(1)} %pad_add_fusion.rest_0_), channel_id=1, source_target_pairs={{0,56},{8,64},{16,72},{24,80},{32,88},{40,96},{48,104},{56,112},{6... | collective-permute-start | bytes 196616 | tf_op jit(solution)/shard_map/ppermute | solution.py:330
  21.6 0.0 collective-permute-done
  21.6 0.0 collective-permute-done.1
  21.7 0.0 collective-permute-done.2
  21.7 2.3 %collective-permute-done.3 = bf16[256,128]{1,0:T(8,128)(2,1)S(1)} collective-permute-done((bf16[256,128]{1,0:T(8,128)(2,1)S(1)}, bf16[256,128]{1,0:T(8,128)(2,1)S(1)}, u32[]{:S(2)}, u32[]{:S(2)}) %collective-permute-start.3) | collective-permute-done | bytes 65568 | tf_op jit(solution)/shard_map/ppermute | solution.py:330
  24.0 0.0 copy-start
  24.0 2.1 %collective-permute-start.4 = (bf16[1024,128]{1,0:T(8,128)(2,1)S(1)}, bf16[1024,128]{1,0:T(8,128)(2,1)S(1)}, u32[]{:S(2)}, u32[]{:S(2)}) collective-permute-start(bf16[1024,128]{1,0:T(8,128)(2,1)S(1)} %constant_dynamic-update-slice_fusion.rest_1_), channel_id=1, source_target_pairs={{0,64},{8,72},{16,80},{24,88},{32,96},{40,104},{48,112},{56,120},{... | collective-permute-start | bytes 786440 | tf_op jit(solution)/shard_map/ppermute | solution.py:330
  26.1 2.7 %collective-permute-start.5 = (bf16[512,128]{1,0:T(8,128)(2,1)S(1)}, bf16[512,128]{1,0:T(8,128)(2,1)S(1)}, u32[]{:S(2)}, u32[]{:S(2)}) collective-permute-start(bf16[512,128]{1,0:T(8,128)(2,1)S(1)} %get-tuple-element.38), channel_id=1, source_target_pairs={{0,8},{8,16},{16,24},{24,32},{32,40},{40,48},{48,56},{56,64},{64,7... | collective-permute-start | bytes 393224 | tf_op jit(solution)/shard_map/ppermute | solution.py:330
  28.7 0.0 copy-start.1
  28.7 0.0 copy-start.2
  28.8 0.0 copy-start.3
  28.8 0.1 collective-permute-start.6
  28.9 3.6 %collective-permute-done.4.rest_2_ = bf16[1024,128]{1,0:T(8,128)(2,1)S(1)} collective-permute-done((bf16[1024,128]{1,0:T(8,128)(2,1)S(1)}, bf16[1024,128]{1,0:T(8,128)(2,1)S(1)}, u32[]{:S(2)}, u32[]{:S(2)}) %collective-permute-start.4) | collective-permute-done | bytes 262176 | tf_op jit(solution)/shard_map/ppermute | solution.py:330
  32.5 1.3 %collective-permute-start.7 = (bf16[512,128]{1,0:T(8,128)(2,1)S(1)}, bf16[512,128]{1,0:T(8,128)(2,1)S(1)}, u32[]{:S(2)}, u32[]{:S(2)}) collective-permute-start(bf16[512,128]{1,0:T(8,128)(2,1)S(1)} %get-tuple-element.36), channel_id=1, source_target_pairs={{0,8},{8,16},{16,24},{24,32},{32,40},{40,48},{48,56},{56,64},{64,7... | collective-permute-start | bytes 393224 | tf_op jit(solution)/shard_map/ppermute | solution.py:330
  33.8 0.0 copy-start.5
  33.8 1.7 %collective-permute-start.8 = (bf16[512,128]{1,0:T(8,128)(2,1)S(1)}, bf16[512,128]{1,0:T(8,128)(2,1)S(1)}, u32[]{:S(2)}, u32[]{:S(2)}) collective-permute-start(bf16[512,128]{1,0:T(8,128)(2,1)S(1)} %get-tuple-element.35), channel_id=1, source_target_pairs={{0,248},{8,0},{16,8},{24,16},{32,24},{40,32},{48,40},{56,48},{64,5... | collective-permute-start | bytes 393224 | tf_op jit(solution)/shard_map/ppermute | solution.py:330
  35.4 0.0 copy-done
  35.4 0.0 copy-done.1
  35.5 0.0 copy-done.2
  35.5 0.0 copy-done.3
  35.5 0.0 copy-done.5
  35.5 1.4 %local_features.1 = (f32[1024,256]{1,0:T(8,128)S(1)}, f32[1024,128]{1,0:T(8,128)S(1)}, f32[128,256]{1,0:T(8,128)S(1)}) custom-call(s32[1,128]{1,0:T(1,128)S(1)} %bitcast.2, bf16[128,1024]{1,0:T(8,128)(2,1)S(1)} %copy-done.1, bf16[128,128]{1,0:T(8,128)(2,1)S(1)} %copy-done.3, f32[8,128,128]{2,1,0:T(8,128)S(1)} %copy-done, f32[1,128,128]{2,1,0:T(8,128)S(1)} %copy-done.2), custom_call_target="tpu_custom_call" | custom-call | tf_op jit(solution)/shard_map/local_features/pallas_call | solution.py:353
  36.9 0.0 collective-permute-done.5.rest_3_
  36.9 0.0 collective-permute-done.6.rest_4_
  36.9 0.0 collective-permute-done.7.rest_5_
  36.9 0.8 collective-permute-done.8.rest_6_
  37.8 13.8 %attention_transfer.1 = (f32[32,48,128]{2,1,0:T(8,128)}, f32[1024,128]{1,0:T(8,128)S(1)}, f32[1024,128]{1,0:T(8,128)S(1)}, f32[128,256]{1,0:T(8,128)S(1)}) custom-call(s32[1,128]{1,0:T(1,128)S(1)} %bitcast.3, bf16[128,1024]{1,0:T(8,128)(2,1)S(1)} %copy-done.1, f32[1,128,128]{2,1,0:T(8,128)S(1)} %copy-done.2, f32[1024,256]{1,0:T(8,128)S(1)} %get-tuple-element.20.phi_ref, ...), custom_call_target="tpu_custom_call" | custom-call | tf_op jit(solution)/shard_map/attention_transfer/pallas_call | solution.py:356
  51.5 9.5 %all-to-all-start = ((f32[32,48,128]{2,1,0:T(8,128)}), f32[32,48,128]{2,1,0:T(8,128)S(1)}, u32[]{:S(2)}, u32[]{:S(2)}) async-start(f32[32,48,128]{2,1,0:T(8,128)} %get-tuple-element.26), calls=%async_computation | async-start | bytes 1572864 | tf_op jit(solution)/shard_map/all_to_all | solution.py:364
  61.0 16.2 %all-to-all-done.got_ref = f32[32,48,128]{2,1,0:T(8,128)S(1)} async-done(((f32[32,48,128]{2,1,0:T(8,128)}), f32[32,48,128]{2,1,0:T(8,128)S(1)}, u32[]{:S(2)}, u32[]{:S(2)}) %all-to-all-start) | async-done | bytes 786464 | tf_op jit(solution)/shard_map/all_to_all | solution.py:364
  77.2 0.7 sum_pieces.1
  78.0 17.0 %all_to_all.15.got_ref.tail_ref = bf16[32,56,128]{2,1,0:T(8,128)(2,1)S(1)} all-to-all(bf16[32,56,128]{2,1,0:T(8,128)(2,1)S(1)} %get-tuple-element.27), channel_id=1, replica_groups=mesh['seq'=32,'head'=8] {'seq'}, dimensions={0} | all-to-all | bytes 917504 | tf_op jit(solution)/shard_map/all_to_all | solution.py:375
  95.0 0.7 head_squares.1
  95.7 12.0 %all-to-all-start.2 = ((f32[8,8,128]{2,1,0:T(8,128)}), f32[8,8,128]{2,1,0:T(8,128)S(1)}, u32[]{:S(2)}, u32[]{:S(2)}) async-start(f32[8,8,128]{2,1,0:T(8,128)} %head_squares.1), calls=%async_computation.2 | async-start | bytes 65536 | tf_op jit(solution)/shard_map/all_to_all | solution.py:377
  107.7 0.0 copy-start.4
  107.7 1.5 %query_gradients.1 = (f32[128,1024]{1,0:T(8,128)}, f32[128,128]{1,0:T(8,128)S(1)}) custom-call(f32[1024,128]{1,0:T(8,128)S(1)} %get-tuple-element.23.dlogit_ref, f32[1024,128]{1,0:T(8,128)S(1)} %get-tuple-element.21.inner_ref, f32[1024,128]{1,0:T(8,128)S(1)} %get-tuple-element.24.gn_ref, f32[8,128,128]{2,1,0:T(8,128)S(1)} %copy-done), custom_call_target="tpu_custom_call" | custom-call | tf_op jit(solution)/shard_map/query_gradients/pallas_call | solution.py:365
  109.2 0.0 copy-done.4
  109.2 1.2 %key_gradients.1 = (f32[128,128]{1,0:T(8,128)}, f32[128,128]{1,0:T(8,128)}) custom-call(s32[1,128]{1,0:T(1,128)S(1)} %bitcast.4, bf16[32,56,128]{2,1,0:T(8,128)(2,1)S(1)} %all_to_all.15.got_ref.tail_ref, f32[1,256]{1,0:T(1,128)S(1)} %get-tuple-element.28.norms_ref, bf16[128,128]{1,0:T(8,128)(2,1)S(1)} %copy-done.4, f32[1,128,128]{2,1,0:T(8,128)S(1)} %copy-done.2, ...), custom_call_target="tpu_custom_call" | custom-call | tf_op jit(solution)/shard_map/key_gradients/pallas_call | solution.py:378
  110.4 2.0 %all-to-all-done.2.squares_ref = f32[8,8,128]{2,1,0:T(8,128)S(1)} async-done(((f32[8,8,128]{2,1,0:T(8,128)}), f32[8,8,128]{2,1,0:T(8,128)S(1)}, u32[]{:S(2)}, u32[]{:S(2)}) %all-to-all-start.2) | async-done | bytes 32800 | tf_op jit(solution)/shard_map/all_to_all | solution.py:377
  112.4 0.9 clip_maps.1
  (6 shorter events, 0.1 us)
Async XLA Ops:
  1.4 20.2 %collective-permute-start = (bf16[256,128]{1,0:T(8,128)(2,1)S(1)}, bf16[256,128]{1,0:T(8,128)(2,1)S(1)}, u32[]{:S(2)}, u32[]{:S(2)}) collective-permute-start(bf16[256,128]{1,0:T(8,128)(2,1)S(1)} %pad_add_fusion.rest_0_), channel_id=1, source_target_pairs={{0,64},{8,72},{16,80},{24,88},{32,96},{40,104},{48,112},{56,120},{... | collective-permute-start | bytes 196616 | tf_op jit(solution)/shard_map/ppermute | solution.py:330
  5.4 16.3 %collective-permute-start.1 = (bf16[256,128]{1,0:T(8,128)(2,1)S(1)}, bf16[256,128]{1,0:T(8,128)(2,1)S(1)}, u32[]{:S(2)}, u32[]{:S(2)}) collective-permute-start(bf16[256,128]{1,0:T(8,128)(2,1)S(1)} %pad_add_fusion.rest_0_), channel_id=1, source_target_pairs={{0,8},{8,16},{16,24},{24,32},{32,40},{40,48},{48,56},{56,64},{64,7... | collective-permute-start | bytes 196616 | tf_op jit(solution)/shard_map/ppermute | solution.py:330
  8.9 12.8 %collective-permute-start.2 = (bf16[256,128]{1,0:T(8,128)(2,1)S(1)}, bf16[256,128]{1,0:T(8,128)(2,1)S(1)}, u32[]{:S(2)}, u32[]{:S(2)}) collective-permute-start(bf16[256,128]{1,0:T(8,128)(2,1)S(1)} %pad_add_fusion.rest_0_), channel_id=1, source_target_pairs={{0,32},{8,40},{16,48},{24,56},{32,64},{40,72},{48,80},{56,88},{64,... | collective-permute-start | bytes 196616 | tf_op jit(solution)/shard_map/ppermute | solution.py:330
  16.8 7.1 %collective-permute-start.3 = (bf16[256,128]{1,0:T(8,128)(2,1)S(1)}, bf16[256,128]{1,0:T(8,128)(2,1)S(1)}, u32[]{:S(2)}, u32[]{:S(2)}) collective-permute-start(bf16[256,128]{1,0:T(8,128)(2,1)S(1)} %pad_add_fusion.rest_0_), channel_id=1, source_target_pairs={{0,56},{8,64},{16,72},{24,80},{32,88},{40,96},{48,104},{56,112},{6... | collective-permute-start | bytes 196616 | tf_op jit(solution)/shard_map/ppermute | solution.py:330
  24.0 11.5 %copy-start = (f32[8,128,128]{2,1,0:T(8,128)S(1)}, f32[8,128,128]{2,1,0:T(8,128)}, u32[]{:S(2)}) copy-start(f32[8,128,128]{2,1,0:T(8,128)} %qmap_ref.3) | copy-start | bytes 1572868
  24.0 8.5 %collective-permute-start.4 = (bf16[1024,128]{1,0:T(8,128)(2,1)S(1)}, bf16[1024,128]{1,0:T(8,128)(2,1)S(1)}, u32[]{:S(2)}, u32[]{:S(2)}) collective-permute-start(bf16[1024,128]{1,0:T(8,128)(2,1)S(1)} %constant_dynamic-update-slice_fusion.rest_1_), channel_id=1, source_target_pairs={{0,64},{8,72},{16,80},{24,88},{32,96},{40,104},{48,112},{56,120},{... | collective-permute-start | bytes 786440 | tf_op jit(solution)/shard_map/ppermute | solution.py:330
  26.1 10.8 %collective-permute-start.5 = (bf16[512,128]{1,0:T(8,128)(2,1)S(1)}, bf16[512,128]{1,0:T(8,128)(2,1)S(1)}, u32[]{:S(2)}, u32[]{:S(2)}) collective-permute-start(bf16[512,128]{1,0:T(8,128)(2,1)S(1)} %get-tuple-element.38), channel_id=1, source_target_pairs={{0,8},{8,16},{16,24},{24,32},{32,40},{40,48},{48,56},{56,64},{64,7... | collective-permute-start | bytes 393224 | tf_op jit(solution)/shard_map/ppermute | solution.py:330
  28.7 6.7 %copy-start.1 = (bf16[128,1024]{1,0:T(8,128)(2,1)S(1)}, bf16[128,1024]{1,0:T(8,128)(2,1)}, u32[]{:S(2)}) copy-start(bf16[128,1024]{1,0:T(8,128)(2,1)} %q_ref.3) | copy-start | bytes 786436
  28.7 6.7 %copy-start.2 = (f32[1,128,128]{2,1,0:T(8,128)S(1)}, f32[1,128,128]{2,1,0:T(8,128)}, u32[]{:S(2)}) copy-start(f32[1,128,128]{2,1,0:T(8,128)} %kmap_ref.5) | copy-start | bytes 196612
  28.8 6.7 %copy-start.3 = (bf16[128,128]{1,0:T(8,128)(2,1)S(1)}, bf16[128,128]{1,0:T(8,128)(2,1)}, u32[]{:S(2)}) copy-start(bf16[128,128]{1,0:T(8,128)(2,1)} %k_ref.1) | copy-start | bytes 98308
  28.8 8.2 %collective-permute-start.6 = (bf16[512,128]{1,0:T(8,128)(2,1)S(1)}, bf16[512,128]{1,0:T(8,128)(2,1)S(1)}, u32[]{:S(2)}, u32[]{:S(2)}) collective-permute-start(bf16[512,128]{1,0:T(8,128)(2,1)S(1)} %get-tuple-element.37), channel_id=1, source_target_pairs={{0,248},{8,0},{16,8},{24,16},{32,24},{40,32},{48,40},{56,48},{64,5... | collective-permute-start | bytes 393224 | tf_op jit(solution)/shard_map/ppermute | solution.py:330
  32.5 4.5 %collective-permute-start.7 = (bf16[512,128]{1,0:T(8,128)(2,1)S(1)}, bf16[512,128]{1,0:T(8,128)(2,1)S(1)}, u32[]{:S(2)}, u32[]{:S(2)}) collective-permute-start(bf16[512,128]{1,0:T(8,128)(2,1)S(1)} %get-tuple-element.36), channel_id=1, source_target_pairs={{0,8},{8,16},{16,24},{24,32},{32,40},{40,48},{48,56},{56,64},{64,7... | collective-permute-start | bytes 393224 | tf_op jit(solution)/shard_map/ppermute | solution.py:330
  33.8 1.7 %copy-start.5 = (s32[128]{0:T(128)S(1)}, s32[128]{0:T(128)}, u32[]{:S(2)}) copy-start(s32[128]{0:T(128)} %param.9) | copy-start | bytes 1540
  33.8 4.0 %collective-permute-start.8 = (bf16[512,128]{1,0:T(8,128)(2,1)S(1)}, bf16[512,128]{1,0:T(8,128)(2,1)S(1)}, u32[]{:S(2)}, u32[]{:S(2)}) collective-permute-start(bf16[512,128]{1,0:T(8,128)(2,1)S(1)} %get-tuple-element.35), channel_id=1, source_target_pairs={{0,248},{8,0},{16,8},{24,16},{32,24},{40,32},{48,40},{56,48},{64,5... | collective-permute-start | bytes 393224 | tf_op jit(solution)/shard_map/ppermute | solution.py:330
  51.5 25.7 %all-to-all-start = ((f32[32,48,128]{2,1,0:T(8,128)}), f32[32,48,128]{2,1,0:T(8,128)S(1)}, u32[]{:S(2)}, u32[]{:S(2)}) async-start(f32[32,48,128]{2,1,0:T(8,128)} %get-tuple-element.26), calls=%async_computation | async-start | bytes 1572864 | tf_op jit(solution)/shard_map/all_to_all | solution.py:364
  95.7 16.8 %all-to-all-start.2 = ((f32[8,8,128]{2,1,0:T(8,128)}), f32[8,8,128]{2,1,0:T(8,128)S(1)}, u32[]{:S(2)}, u32[]{:S(2)}) async-start(f32[8,8,128]{2,1,0:T(8,128)} %head_squares.1), calls=%async_computation.2 | async-start | bytes 65536 | tf_op jit(solution)/shard_map/all_to_all | solution.py:377
  107.7 1.5 %copy-start.4 = (bf16[128,128]{1,0:T(8,128)(2,1)S(1)}, bf16[128,128]{1,0:T(8,128)(2,1)}, u32[]{:S(2)}) copy-start(bf16[128,128]{1,0:T(8,128)(2,1)} %v_ref.1) | copy-start | bytes 98308

commit v5 on v3

--- a/solution.py
+++ b/solution.py
@@ -15,7 +15,8 @@
 T = 128
 WINDOW = 16
 KEYS = (WINDOW + 1) * T
-CHUNK = 2048
+TEACHER = 512
+CHUNK = 1024
 PIECE = 48
 STATE_ROW, KMAP_ROW, NORM_ROW, INFO_ROW = 32, 40, 44, 46
 REPLY = 56
@@ -61,20 +62,54 @@
     return form(parts[0], b) + form(parts[1], b)
 
 
+def deep(parts):
+    return jnp.concatenate(parts, axis=1)
+
+
+def deep_exact_right(form, parts, b):
+    return form(deep(parts), jnp.concatenate([b, b], axis=0 if form is nn else 1))
+
+
+def deep_product(form, a, b):
+    return deep_exact_right(form, a, b[0]) + form(a[0], b[1])
+
+
+def wide_exact_left(form, a, parts):
+    both = form(a, deep(parts))
+    return both[:, :T] + both[:, T:]
+
+
 def row_sums(x):
-    return exact_right(nn, split2(x), jnp.ones((T, T), BF16))
+    return nn(deep(split2(x)), jnp.ones((2 * T, T), BF16))
+
+
+def half_sums(x):
+    i = lax.broadcasted_iota(jnp.int32, (2 * T, 2 * T), 0) < T
+    j = lax.broadcasted_iota(jnp.int32, (2 * T, 2 * T), 1) < T
+    return exact_right(nn, split2(x), (i == j).astype(F32).astype(BF16))
+
+
+def map_of(weights):
+    high, middle, low = split3(weights)
+    rest = jnp.concatenate([middle, jnp.zeros_like(middle)], axis=1)
+    return jnp.concatenate([deep([high, low]), rest], axis=0)
+
+
+def logits_of(x, matrix):
+    both = nn(deep([x, x]), matrix)
+    return both[:, :T] + both[:, T:]
 
 
 def feature_map(logits):
     upper = jnp.exp(logits - jnp.max(logits, axis=-1, keepdims=True))
     lower = jnp.exp(jnp.min(logits, axis=-1, keepdims=True) - logits)
-    return jnp.concatenate([upper / row_sums(upper), lower / row_sums(lower)], axis=1)
+    both = deep([upper, lower])
+    return both / half_sums(both)
 
 
 def feature_back(phi, grad):
-    upper, lower = phi[:, :T], phi[:, T:]
-    up, low = grad[:, :T], grad[:, T:]
-    return upper * (up - row_sums(upper * up)) - lower * (low - row_sums(lower * low))
+    both = phi * (grad - half_sums(phi * grad))
+    return both[:, :T] - both[:, T:]
 
 
 def column_of(row):
@@ -101,10 +136,10 @@
     row, start = positions_of(pos_ref)
     key = lax.broadcasted_iota(jnp.int32, (T, T), 1).astype(F32)
     seen = every_head(((key <= row) & (key >= start)).astype(F32), heads)
-    own = feature_map(exact_left(nn, k_ref[...], split3(kmap_ref[0])))
+    own = feature_map(logits_of(k_ref[...], map_of(kmap_ref[0])))
     own_ref[...] = own
     logits = jnp.concatenate(
-        [exact_left(nn, q_ref[:, h * T : h * T + T], split3(qmap_ref[h])) for h in range(heads)],
+        [logits_of(q_ref[:, h * T : h * T + T], map_of(qmap_ref[h])) for h in range(heads)],
         axis=0,
     )
     phi = feature_map(logits)
@@ -132,11 +167,11 @@
             k_s[at : at + T, T:] = (hidden if block else jnp.zeros((T, T), F32)).astype(BF16)
     v_s[:, T:] = jnp.ones((KEYS, T), BF16)
 
-    map_parts = split3(kmap_ref[0])
+    matrix = map_of(kmap_ref[0])
     state = jnp.zeros((2 * T, 2 * T), F32)
     for at in range(0, WINDOW * T, CHUNK):
         key_row = lax.broadcasted_iota(jnp.int32, (CHUNK, 1), 0) + (at - WINDOW * T)
-        features = feature_map(exact_left(nn, k_s[at : at + CHUNK, :T], map_parts))
+        features = feature_map(logits_of(k_s[at : at + CHUNK, :T], matrix))
         features = jnp.where(key_row.astype(F32) >= entry, features, 0.0)
         phi_s[at : at + CHUNK, :] = features
         state = state + exact_right(tn, split2(features), v_s[at : at + CHUNK, :])
@@ -150,25 +185,29 @@
     cross = every_head(jnp.broadcast_to(crossing, (T, T)), heads)
     hider = jnp.where(lane == 0, 1.0 - crossing, jnp.where(lane == 1, 1.0, 0.0)).astype(BF16)
     queries = jnp.concatenate([stacked(q_ref), every_head(hider, heads)], axis=1)
-    scores = nt(queries, k_s[...])
-    near = scores[:, WINDOW * T :] + bias
-    far = scores[:, : WINDOW * T]
-    highest = jnp.maximum(
-        jnp.max(near, axis=-1, keepdims=True), jnp.max(far, axis=-1, keepdims=True)
-    )
+    own_v = v_s[WINDOW * T :, :]
     rate = math.log2(math.e) / math.sqrt(T)
-    near = jnp.exp2((near - highest) * rate)
-    far = jnp.exp2((far - highest) * rate)
-    total = jnp.sum(near, axis=-1, keepdims=True) + jnp.sum(far, axis=-1, keepdims=True)
-    own_v = v_s[WINDOW * T :, :]
-    teacher = nn(near.astype(BF16), own_v[:, :T]) + nn(far.astype(BF16), v_s[: WINDOW * T, :T])
-    teacher = teacher / total
+    teachers = []
+    for at in range(0, heads * T, TEACHER):
+        rows = slice(at, at + TEACHER)
+        scores = nt(queries[rows, :], k_s[...])
+        near = scores[:, WINDOW * T :] + bias[rows, :]
+        far = scores[:, : WINDOW * T]
+        highest = jnp.maximum(
+            jnp.max(near, axis=-1, keepdims=True), jnp.max(far, axis=-1, keepdims=True)
+        )
+        near = jnp.exp2((near - highest) * rate)
+        far = jnp.exp2((far - highest) * rate)
+        total = jnp.sum(near, axis=-1, keepdims=True) + jnp.sum(far, axis=-1, keepdims=True)
+        summed = nn(near.astype(BF16), own_v[:, :T]) + nn(far.astype(BF16), v_s[: WINDOW * T, :T])
+        teachers.append(summed / total)
+    teacher = jnp.concatenate(teachers, axis=0)
 
     own = own_ref[...]
     own_phi = split2(own)
     phi = phi_ref[...]
     phi_parts = split2(phi)
-    near = exact_right(nn, split2(inner_ref[...]), own_v)
+    near = deep_exact_right(nn, split2(inner_ref[...]), own_v)
     far = product(nn, phi_parts, state)
     inverse = 1.0 / (near[:, T:] + cross * far[:, T:])
     outputs = (near[:, :T] + cross * far[:, :T]) * inverse
@@ -179,10 +218,10 @@
     gn_ref[...] = grad_numer
     far_numer = cross * grad_numer
     far_denom = cross * grad_denom
-    mixing = (exact_right(nt, split2(grad_numer), own_v[:, :T]) + grad_denom) * seen
+    mixing = (deep_exact_right(nt, split2(grad_numer), own_v[:, :T]) + grad_denom) * seen
     mixing_parts = split2(mixing)
-    near = product(nn, mixing_parts, own_phi)
-    far = product(nt, split2(far_numer), [part[:, :T] for part in state])
+    near = deep_product(nn, mixing_parts, own_phi)
+    far = deep_product(nt, split2(far_numer), [part[:, :T] for part in state])
     grad_phi = jnp.concatenate(
         [
             near[:, :T] + far[:, :T] + far_denom * norms[:, :T],
@@ -199,7 +238,7 @@
     dlogit_parts = split2(dlogit)
     for h in range(heads):
         at = slice(h * T, h * T + T)
-        grad_map = exact_left(tn, q_ref[:, at], [part[at, :] for part in dlogit_parts])
+        grad_map = wide_exact_left(tn, q_ref[:, at], [part[at, :] for part in dlogit_parts])
         for quarter in range(4):
             payload_ref[4 * h + quarter, 0:STATE_ROW, :] = grad_map[
                 quarter * 32 : quarter * 32 + 32, :
@@ -208,12 +247,12 @@
         payload_ref[piece, STATE_ROW : STATE_ROW + 8, :] = back[piece * 8 : piece * 8 + 8, :T]
 
     part = split2(feature_back(own, gkphi))
-    grad_map = exact_left(tn, k_s[WINDOW * T :, :T], part)
+    grad_map = wide_exact_left(tn, k_s[WINDOW * T :, :T], part)
     back_parts = split2(jnp.concatenate([back[:, :T], back[:, T:] * (1.0 / T)], axis=1))
     for at in range(0, WINDOW * T, CHUNK):
         grad = exact_left(nt, v_s[at : at + CHUNK, :], back_parts)
         part = split2(feature_back(phi_s[at : at + CHUNK, :], grad))
-        grad_map = grad_map + exact_left(tn, k_s[at : at + CHUNK, :T], part)
+        grad_map = grad_map + wide_exact_left(tn, k_s[at : at + CHUNK, :T], part)
     tail = jnp.concatenate(
         [
             backn[:, :T],

time: 110 us -> 107 us (0.973)
  Pallas kernels: 20.2 us -> 17.8 us
    pallas_call x1, Pallas kernels: 13.8 us -> 11.2 us  [on_device(): call(functools.partial(main_kernel, places), 'attention_transfer', [V] *...]
where the time goes in v5:
time: 107 us
  starting transfers between devices  40.7 us (38%)
  waiting for transfers between devices  27.8 us (26%)
  blocking collectives  19 us (18%)
  Pallas kernels  17.8 us (17%)
    ppermute x9, starting transfers between devices, shift(): return lax.ppermute(x, 'seq', [(i, (i + k) % n) for i in range(n)])  22.3 us
    all_to_all x1, blocking collectives, on_device(): back = lax.all_to_all(reduced, 'seq', 0, 0)  19 us
    all_to_all x1, waiting for transfers between devices, on_device(): gathered = lax.all_to_all(payload, 'seq', 0, 0)  15.9 us
    all_to_all x1, starting transfers between devices, on_device(): squares = lax.all_to_all(squares, 'head', 0, 0)  11.9 us
    pallas_call x1, Pallas kernels, on_device(): call(functools.partial(main_kernel, places), 'attention_transfer', [V] *...  11.2 us
    ppermute x9, waiting for transfers between devices, shift(): return lax.ppermute(x, 'seq', [(i, (i + k) % n) for i in range(n)])  9.84 us
    all_to_all x1, starting transfers between devices, on_device(): gathered = lax.all_to_all(payload, 'seq', 0, 0)  6.45 us
  transfers between devices with their start and end apart: 11, of which 6 were waited for; matrix products, arithmetic and copies ran while one was open for 0% of the time, Pallas kernels for 4%

profile of v5, /device:TPU:1, one launch (start us, length us, event | category | flops | bytes accessed | tf_op | source)
XLA Modules:
  0.0 106.9 jit_solution(15623989042254814541)
XLA Ops:
  0.6 0.8 pad_add_fusion.rest_0_
  1.4 2.0 %collective-permute-start = (bf16[256,128]{1,0:T(8,128)(2,1)S(1)}, bf16[256,128]{1,0:T(8,128)(2,1)S(1)}, u32[]{:S(2)}, u32[]{:S(2)}) collective-permute-start(bf16[256,128]{1,0:T(8,128)(2,1)S(1)} %pad_add_fusion.rest_0_), channel_id=1, source_target_pairs={{0,64},{8,72},{16,80},{24,88},{32,96},{40,104},{48,112},{56,120},{... | collective-permute-start | bytes 196616 | tf_op jit(solution)/shard_map/ppermute | solution.py:368
  3.5 1.6 %collective-permute-start.1 = (bf16[256,128]{1,0:T(8,128)(2,1)S(1)}, bf16[256,128]{1,0:T(8,128)(2,1)S(1)}, u32[]{:S(2)}, u32[]{:S(2)}) collective-permute-start(bf16[256,128]{1,0:T(8,128)(2,1)S(1)} %pad_add_fusion.rest_0_), channel_id=1, source_target_pairs={{0,8},{8,16},{16,24},{24,32},{32,40},{40,48},{48,56},{56,64},{64,7... | collective-permute-start | bytes 196616 | tf_op jit(solution)/shard_map/ppermute | solution.py:368
  5.1 6.0 %collective-permute-start.2 = (bf16[256,128]{1,0:T(8,128)(2,1)S(1)}, bf16[256,128]{1,0:T(8,128)(2,1)S(1)}, u32[]{:S(2)}, u32[]{:S(2)}) collective-permute-start(bf16[256,128]{1,0:T(8,128)(2,1)S(1)} %pad_add_fusion.rest_0_), channel_id=1, source_target_pairs={{0,32},{8,40},{16,48},{24,56},{32,64},{40,72},{48,80},{56,88},{64,... | collective-permute-start | bytes 196616 | tf_op jit(solution)/shard_map/ppermute | solution.py:368
  11.1 2.9 %collective-permute-start.3 = (bf16[256,128]{1,0:T(8,128)(2,1)S(1)}, bf16[256,128]{1,0:T(8,128)(2,1)S(1)}, u32[]{:S(2)}, u32[]{:S(2)}) collective-permute-start(bf16[256,128]{1,0:T(8,128)(2,1)S(1)} %pad_add_fusion.rest_0_), channel_id=1, source_target_pairs={{0,56},{8,64},{16,72},{24,80},{32,88},{40,96},{48,104},{56,112},{6... | collective-permute-start | bytes 196616 | tf_op jit(solution)/shard_map/ppermute | solution.py:368
  14.0 0.0 collective-permute-done
  14.0 0.0 collective-permute-done.1
  14.0 0.7 collective-permute-done.2
  14.7 2.9 %collective-permute-done.3 = bf16[256,128]{1,0:T(8,128)(2,1)S(1)} collective-permute-done((bf16[256,128]{1,0:T(8,128)(2,1)S(1)}, bf16[256,128]{1,0:T(8,128)(2,1)S(1)}, u32[]{:S(2)}, u32[]{:S(2)}) %collective-permute-start.3) | collective-permute-done | bytes 65568 | tf_op jit(solution)/shard_map/ppermute | solution.py:368
  17.7 0.0 copy-start
  17.7 0.1 collective-permute-start.4
  17.8 0.4 collective-permute-start.5
  18.2 0.0 copy-start.1
  18.2 0.0 copy-start.2
  18.2 0.0 copy-start.3
  18.2 4.5 %collective-permute-start.6 = (bf16[512,128]{1,0:T(8,128)(2,1)S(1)}, bf16[512,128]{1,0:T(8,128)(2,1)S(1)}, u32[]{:S(2)}, u32[]{:S(2)}) collective-permute-start(bf16[512,128]{1,0:T(8,128)(2,1)S(1)} %get-tuple-element.37), channel_id=1, source_target_pairs={{0,248},{8,0},{16,8},{24,16},{32,24},{40,32},{48,40},{56,48},{64,5... | collective-permute-start | bytes 393224 | tf_op jit(solution)/shard_map/ppermute | solution.py:368
  22.7 5.5 %collective-permute-done.4.rest_2_ = bf16[1024,128]{1,0:T(8,128)(2,1)S(1)} collective-permute-done((bf16[1024,128]{1,0:T(8,128)(2,1)S(1)}, bf16[1024,128]{1,0:T(8,128)(2,1)S(1)}, u32[]{:S(2)}, u32[]{:S(2)}) %collective-permute-start.4) | collective-permute-done | bytes 262176 | tf_op jit(solution)/shard_map/ppermute | solution.py:368
  28.2 0.1 collective-permute-start.7
  28.3 0.0 copy-start.5
  28.3 4.8 %collective-permute-start.8 = (bf16[512,128]{1,0:T(8,128)(2,1)S(1)}, bf16[512,128]{1,0:T(8,128)(2,1)S(1)}, u32[]{:S(2)}, u32[]{:S(2)}) collective-permute-start(bf16[512,128]{1,0:T(8,128)(2,1)S(1)} %get-tuple-element.35), channel_id=1, source_target_pairs={{0,248},{8,0},{16,8},{24,16},{32,24},{40,32},{48,40},{56,48},{64,5... | collective-permute-start | bytes 393224 | tf_op jit(solution)/shard_map/ppermute | solution.py:368
  33.1 0.0 copy-done
  33.1 0.0 copy-done.1
  33.1 0.0 copy-done.2
  33.1 0.0 copy-done.3
  33.1 0.0 copy-done.5
  33.1 1.6 %local_features.1 = (f32[1024,256]{1,0:T(8,128)S(1)}, f32[1024,128]{1,0:T(8,128)S(1)}, f32[128,256]{1,0:T(8,128)S(1)}) custom-call(s32[1,128]{1,0:T(1,128)S(1)} %bitcast.2, bf16[128,1024]{1,0:T(8,128)(2,1)S(1)} %copy-done.1, bf16[128,128]{1,0:T(8,128)(2,1)S(1)} %copy-done.3, f32[8,128,128]{2,1,0:T(8,128)S(1)} %copy-done, f32[1,128,128]{2,1,0:T(8,128)S(1)} %copy-done.2), custom_call_target="tpu_custom_call" | custom-call | tf_op jit(solution)/shard_map/local_features/pallas_call | solution.py:391
  34.8 0.0 collective-permute-done.5.rest_3_
  34.8 0.0 collective-permute-done.6.rest_4_
  34.8 0.7 collective-permute-done.7.rest_5_
  35.5 0.0 collective-permute-done.8.rest_6_
  35.5 11.2 %attention_transfer.1 = (f32[32,48,128]{2,1,0:T(8,128)}, f32[1024,128]{1,0:T(8,128)S(1)}, f32[1024,128]{1,0:T(8,128)S(1)}, f32[128,256]{1,0:T(8,128)S(1)}) custom-call(s32[1,128]{1,0:T(1,128)S(1)} %bitcast.3, bf16[128,1024]{1,0:T(8,128)(2,1)S(1)} %copy-done.1, f32[1,128,128]{2,1,0:T(8,128)S(1)} %copy-done.2, f32[1024,256]{1,0:T(8,128)S(1)} %get-tuple-element.20.phi_ref, ...), custom_call_target="tpu_custom_call" | custom-call | tf_op jit(solution)/shard_map/attention_transfer/pallas_call | solution.py:394
  46.6 6.4 %all-to-all-start = ((f32[32,48,128]{2,1,0:T(8,128)}), f32[32,48,128]{2,1,0:T(8,128)S(1)}, u32[]{:S(2)}, u32[]{:S(2)}) async-start(f32[32,48,128]{2,1,0:T(8,128)} %get-tuple-element.26), calls=%async_computation | async-start | bytes 1572864 | tf_op jit(solution)/shard_map/all_to_all | solution.py:402
  53.1 15.9 %all-to-all-done.got_ref = f32[32,48,128]{2,1,0:T(8,128)S(1)} async-done(((f32[32,48,128]{2,1,0:T(8,128)}), f32[32,48,128]{2,1,0:T(8,128)S(1)}, u32[]{:S(2)}, u32[]{:S(2)}) %all-to-all-start) | async-done | bytes 786464 | tf_op jit(solution)/shard_map/all_to_all | solution.py:402
  69.0 0.7 sum_pieces.1
  69.8 19.0 %all_to_all.15.got_ref.tail_ref = bf16[32,56,128]{2,1,0:T(8,128)(2,1)S(1)} all-to-all(bf16[32,56,128]{2,1,0:T(8,128)(2,1)S(1)} %get-tuple-element.27), channel_id=1, replica_groups=mesh['seq'=32,'head'=8] {'seq'}, dimensions={0} | all-to-all | bytes 917504 | tf_op jit(solution)/shard_map/all_to_all | solution.py:413
  88.8 0.7 head_squares.1
  89.5 11.9 %all-to-all-start.2 = ((f32[8,8,128]{2,1,0:T(8,128)}), f32[8,8,128]{2,1,0:T(8,128)S(1)}, u32[]{:S(2)}, u32[]{:S(2)}) async-start(f32[8,8,128]{2,1,0:T(8,128)} %head_squares.1), calls=%async_computation.2 | async-start | bytes 65536 | tf_op jit(solution)/shard_map/all_to_all | solution.py:415
  101.3 0.0 copy-start.4
  101.3 1.5 %query_gradients.1 = (f32[128,1024]{1,0:T(8,128)}, f32[128,128]{1,0:T(8,128)S(1)}) custom-call(f32[1024,128]{1,0:T(8,128)S(1)} %get-tuple-element.23.dlogit_ref, f32[1024,128]{1,0:T(8,128)S(1)} %get-tuple-element.21.inner_ref, f32[1024,128]{1,0:T(8,128)S(1)} %get-tuple-element.24.gn_ref, f32[8,128,128]{2,1,0:T(8,128)S(1)} %copy-done), custom_call_target="tpu_custom_call" | custom-call | tf_op jit(solution)/shard_map/query_gradients/pallas_call | solution.py:403
  102.8 0.0 copy-done.4
  102.8 1.2 %key_gradients.1 = (f32[128,128]{1,0:T(8,128)}, f32[128,128]{1,0:T(8,128)}) custom-call(s32[1,128]{1,0:T(1,128)S(1)} %bitcast.4, bf16[32,56,128]{2,1,0:T(8,128)(2,1)S(1)} %all_to_all.15.got_ref.tail_ref, f32[1,256]{1,0:T(1,128)S(1)} %get-tuple-element.28.norms_ref, bf16[128,128]{1,0:T(8,128)(2,1)S(1)} %copy-done.4, f32[1,128,128]{2,1,0:T(8,128)S(1)} %copy-done.2, ...), custom_call_target="tpu_custom_call" | custom-call | tf_op jit(solution)/shard_map/key_gradients/pallas_call | solution.py:416
  104.0 2.0 %all-to-all-done.2.squares_ref = f32[8,8,128]{2,1,0:T(8,128)S(1)} async-done(((f32[8,8,128]{2,1,0:T(8,128)}), f32[8,8,128]{2,1,0:T(8,128)S(1)}, u32[]{:S(2)}, u32[]{:S(2)}) %all-to-all-start.2) | async-done | bytes 32800 | tf_op jit(solution)/shard_map/all_to_all | solution.py:415
  106.1 0.9 clip_maps.1
  (6 shorter events, 0.1 us)
Async XLA Ops:
  1.4 12.6 %collective-permute-start = (bf16[256,128]{1,0:T(8,128)(2,1)S(1)}, bf16[256,128]{1,0:T(8,128)(2,1)S(1)}, u32[]{:S(2)}, u32[]{:S(2)}) collective-permute-start(bf16[256,128]{1,0:T(8,128)(2,1)S(1)} %pad_add_fusion.rest_0_), channel_id=1, source_target_pairs={{0,64},{8,72},{16,80},{24,88},{32,96},{40,104},{48,112},{56,120},{... | collective-permute-start | bytes 196616 | tf_op jit(solution)/shard_map/ppermute | solution.py:368
  3.5 10.5 %collective-permute-start.1 = (bf16[256,128]{1,0:T(8,128)(2,1)S(1)}, bf16[256,128]{1,0:T(8,128)(2,1)S(1)}, u32[]{:S(2)}, u32[]{:S(2)}) collective-permute-start(bf16[256,128]{1,0:T(8,128)(2,1)S(1)} %pad_add_fusion.rest_0_), channel_id=1, source_target_pairs={{0,8},{8,16},{16,24},{24,32},{32,40},{40,48},{48,56},{56,64},{64,7... | collective-permute-start | bytes 196616 | tf_op jit(solution)/shard_map/ppermute | solution.py:368
  5.1 9.6 %collective-permute-start.2 = (bf16[256,128]{1,0:T(8,128)(2,1)S(1)}, bf16[256,128]{1,0:T(8,128)(2,1)S(1)}, u32[]{:S(2)}, u32[]{:S(2)}) collective-permute-start(bf16[256,128]{1,0:T(8,128)(2,1)S(1)} %pad_add_fusion.rest_0_), channel_id=1, source_target_pairs={{0,32},{8,40},{16,48},{24,56},{32,64},{40,72},{48,80},{56,88},{64,... | collective-permute-start | bytes 196616 | tf_op jit(solution)/shard_map/ppermute | solution.py:368
  11.1 6.6 %collective-permute-start.3 = (bf16[256,128]{1,0:T(8,128)(2,1)S(1)}, bf16[256,128]{1,0:T(8,128)(2,1)S(1)}, u32[]{:S(2)}, u32[]{:S(2)}) collective-permute-start(bf16[256,128]{1,0:T(8,128)(2,1)S(1)} %pad_add_fusion.rest_0_), channel_id=1, source_target_pairs={{0,56},{8,64},{16,72},{24,80},{32,88},{40,96},{48,104},{56,112},{6... | collective-permute-start | bytes 196616 | tf_op jit(solution)/shard_map/ppermute | solution.py:368
  17.7 15.4 %copy-start = (f32[8,128,128]{2,1,0:T(8,128)S(1)}, f32[8,128,128]{2,1,0:T(8,128)}, u32[]{:S(2)}) copy-start(f32[8,128,128]{2,1,0:T(8,128)} %qmap_ref.3) | copy-start | bytes 1572868
  17.7 10.5 %collective-permute-start.4 = (bf16[1024,128]{1,0:T(8,128)(2,1)S(1)}, bf16[1024,128]{1,0:T(8,128)(2,1)S(1)}, u32[]{:S(2)}, u32[]{:S(2)}) collective-permute-start(bf16[1024,128]{1,0:T(8,128)(2,1)S(1)} %constant_dynamic-update-slice_fusion.rest_1_), channel_id=1, source_target_pairs={{0,64},{8,72},{16,80},{24,88},{32,96},{40,104},{48,112},{56,120},{... | collective-permute-start | bytes 786440 | tf_op jit(solution)/shard_map/ppermute | solution.py:368
  17.8 17.0 %collective-permute-start.5 = (bf16[512,128]{1,0:T(8,128)(2,1)S(1)}, bf16[512,128]{1,0:T(8,128)(2,1)S(1)}, u32[]{:S(2)}, u32[]{:S(2)}) collective-permute-start(bf16[512,128]{1,0:T(8,128)(2,1)S(1)} %get-tuple-element.38), channel_id=1, source_target_pairs={{0,8},{8,16},{16,24},{24,32},{32,40},{40,48},{48,56},{56,64},{64,7... | collective-permute-start | bytes 393224 | tf_op jit(solution)/shard_map/ppermute | solution.py:368
  18.2 14.9 %copy-start.1 = (bf16[128,1024]{1,0:T(8,128)(2,1)S(1)}, bf16[128,1024]{1,0:T(8,128)(2,1)}, u32[]{:S(2)}) copy-start(bf16[128,1024]{1,0:T(8,128)(2,1)} %q_ref.3) | copy-start | bytes 786436
  18.2 14.9 %copy-start.2 = (f32[1,128,128]{2,1,0:T(8,128)S(1)}, f32[1,128,128]{2,1,0:T(8,128)}, u32[]{:S(2)}) copy-start(f32[1,128,128]{2,1,0:T(8,128)} %kmap_ref.5) | copy-start | bytes 196612
  18.2 14.9 %copy-start.3 = (bf16[128,128]{1,0:T(8,128)(2,1)S(1)}, bf16[128,128]{1,0:T(8,128)(2,1)}, u32[]{:S(2)}) copy-start(bf16[128,128]{1,0:T(8,128)(2,1)} %k_ref.1) | copy-start | bytes 98308
  18.2 16.6 %collective-permute-start.6 = (bf16[512,128]{1,0:T(8,128)(2,1)S(1)}, bf16[512,128]{1,0:T(8,128)(2,1)S(1)}, u32[]{:S(2)}, u32[]{:S(2)}) collective-permute-start(bf16[512,128]{1,0:T(8,128)(2,1)S(1)} %get-tuple-element.37), channel_id=1, source_target_pairs={{0,248},{8,0},{16,8},{24,16},{32,24},{40,32},{48,40},{56,48},{64,5... | collective-permute-start | bytes 393224 | tf_op jit(solution)/shard_map/ppermute | solution.py:368
  28.2 7.2 %collective-permute-start.7 = (bf16[512,128]{1,0:T(8,128)(2,1)S(1)}, bf16[512,128]{1,0:T(8,128)(2,1)S(1)}, u32[]{:S(2)}, u32[]{:S(2)}) collective-permute-start(bf16[512,128]{1,0:T(8,128)(2,1)S(1)} %get-tuple-element.36), channel_id=1, source_target_pairs={{0,8},{8,16},{16,24},{24,32},{32,40},{40,48},{48,56},{56,64},{64,7... | collective-permute-start | bytes 393224 | tf_op jit(solution)/shard_map/ppermute | solution.py:368
  28.3 4.8 %copy-start.5 = (s32[128]{0:T(128)S(1)}, s32[128]{0:T(128)}, u32[]{:S(2)}) copy-start(s32[128]{0:T(128)} %param.9) | copy-start | bytes 1540
  28.3 7.1 %collective-permute-start.8 = (bf16[512,128]{1,0:T(8,128)(2,1)S(1)}, bf16[512,128]{1,0:T(8,128)(2,1)S(1)}, u32[]{:S(2)}, u32[]{:S(2)}) collective-permute-start(bf16[512,128]{1,0:T(8,128)(2,1)S(1)} %get-tuple-element.35), channel_id=1, source_target_pairs={{0,248},{8,0},{16,8},{24,16},{32,24},{40,32},{48,40},{56,48},{64,5... | collective-permute-start | bytes 393224 | tf_op jit(solution)/shard_map/ppermute | solution.py:368
  46.6 22.4 %all-to-all-start = ((f32[32,48,128]{2,1,0:T(8,128)}), f32[32,48,128]{2,1,0:T(8,128)S(1)}, u32[]{:S(2)}, u32[]{:S(2)}) async-start(f32[32,48,128]{2,1,0:T(8,128)} %get-tuple-element.26), calls=%async_computation | async-start | bytes 1572864 | tf_op jit(solution)/shard_map/all_to_all | solution.py:402
  89.5 16.6 %all-to-all-start.2 = ((f32[8,8,128]{2,1,0:T(8,128)}), f32[8,8,128]{2,1,0:T(8,128)S(1)}, u32[]{:S(2)}, u32[]{:S(2)}) async-start(f32[8,8,128]{2,1,0:T(8,128)} %head_squares.1), calls=%async_computation.2 | async-start | bytes 65536 | tf_op jit(solution)/shard_map/all_to_all | solution.py:415
  101.3 1.5 %copy-start.4 = (bf16[128,128]{1,0:T(8,128)(2,1)S(1)}, bf16[128,128]{1,0:T(8,128)(2,1)}, u32[]{:S(2)}) copy-start(bf16[128,128]{1,0:T(8,128)(2,1)} %v_ref.1) | copy-start | bytes 98308

commit v6 on v5

--- a/solution.py
+++ b/solution.py
@@ -372,7 +372,7 @@
     far = shift(near, 8)
     up, down = slice(size, 3 * size), slice(2 * size, 4 * size)
     n1, n2 = shift(near[up], 1), shift(near[down], -1)
-    f1, f2 = shift(far[up], 1), shift(far[down], -1)
+    f1, f2 = shift(n1, 8), shift(n2, 8)
     arrays = [kv, near, far, n1, n2, f1, f2]
     places = [(0,), (8, 1, 4, 7), (16, 9, 12, 15), (2, 5), (3, 6), (10, 13), (11, 14)]
     return arrays, places

time: 107 us -> 103 us (0.963)
  starting transfers between devices: 40.7 us -> 32.2 us
  waiting for transfers between devices: 27.8 us -> 32.2 us
    ppermute x9, starting transfers between devices: 22.3 us -> 17.6 us  [shift(): return lax.ppermute(x, 'seq', [(i, (i + k) % n) for i in range(n)])]
    ppermute x9, waiting for transfers between devices: 9.84 us -> 12.8 us  [shift(): return lax.ppermute(x, 'seq', [(i, (i + k) % n) for i in range(n)])]
    all_to_all x1, starting transfers between devices: 6.45 us -> 3.91 us  [on_device(): gathered = lax.all_to_all(payload, 'seq', 0, 0)]
    all_to_all x1, waiting for transfers between devices: 15.9 us -> 17.4 us  [on_device(): gathered = lax.all_to_all(payload, 'seq', 0, 0)]
    all_to_all x1, starting transfers between devices: 11.9 us -> 10.8 us  [on_device(): squares = lax.all_to_all(squares, 'head', 0, 0)]
  transfers between devices with their start and end apart: 11 -> 11, of which waited for: 6 -> 8; matrix products, arithmetic and copies ran while one was open for 0% -> 0% of each run, Pallas kernels for 4% -> 4%
where the time goes in v6:
time: 103 us
  starting transfers between devices  32.2 us (31%)
  waiting for transfers between devices  32.2 us (31%)
  blocking collectives  18.9 us (18%)
  Pallas kernels  17.7 us (17%)
    all_to_all x1, blocking collectives, on_device(): back = lax.all_to_all(reduced, 'seq', 0, 0)  18.9 us
    ppermute x9, starting transfers between devices, shift(): return lax.ppermute(x, 'seq', [(i, (i + k) % n) for i in range(n)])  17.6 us
    all_to_all x1, waiting for transfers between devices, on_device(): gathered = lax.all_to_all(payload, 'seq', 0, 0)  17.4 us
    ppermute x9, waiting for transfers between devices, shift(): return lax.ppermute(x, 'seq', [(i, (i + k) % n) for i in range(n)])  12.8 us
    pallas_call x1, Pallas kernels, on_device(): call(functools.partial(main_kernel, places), 'attention_transfer', [V] *...  11.1 us
    all_to_all x1, starting transfers between devices, on_device(): squares = lax.all_to_all(squares, 'head', 0, 0)  10.8 us
    all_to_all x1, starting transfers between devices, on_device(): gathered = lax.all_to_all(payload, 'seq', 0, 0)  3.91 us
  transfers between devices with their start and end apart: 11, of which 8 were waited for; matrix products, arithmetic and copies ran while one was open for 0% of the time, Pallas kernels for 4%

profile of v6, /device:TPU:1, one launch (start us, length us, event | category | flops | bytes accessed | tf_op | source)
XLA Modules:
  0.0 102.7 jit_solution(5278066187309582003)
XLA Ops:
  0.6 0.8 pad_add_fusion.rest_0_
  1.4 0.0 copy-start
  1.4 2.1 %collective-permute-start = (bf16[256,128]{1,0:T(8,128)(2,1)S(1)}, bf16[256,128]{1,0:T(8,128)(2,1)S(1)}, u32[]{:S(2)}, u32[]{:S(2)}) collective-permute-start(bf16[256,128]{1,0:T(8,128)(2,1)S(1)} %pad_add_fusion.rest_0_), channel_id=1, source_target_pairs={{0,64},{8,72},{16,80},{24,88},{32,96},{40,104},{48,112},{56,120},{... | collective-permute-start | bytes 196616 | tf_op jit(solution)/shard_map/ppermute | solution.py:368
  3.5 1.6 %collective-permute-start.1 = (bf16[256,128]{1,0:T(8,128)(2,1)S(1)}, bf16[256,128]{1,0:T(8,128)(2,1)S(1)}, u32[]{:S(2)}, u32[]{:S(2)}) collective-permute-start(bf16[256,128]{1,0:T(8,128)(2,1)S(1)} %pad_add_fusion.rest_0_), channel_id=1, source_target_pairs={{0,8},{8,16},{16,24},{24,32},{32,40},{40,48},{48,56},{56,64},{64,7... | collective-permute-start | bytes 196616 | tf_op jit(solution)/shard_map/ppermute | solution.py:368
  5.2 6.0 %collective-permute-start.2 = (bf16[256,128]{1,0:T(8,128)(2,1)S(1)}, bf16[256,128]{1,0:T(8,128)(2,1)S(1)}, u32[]{:S(2)}, u32[]{:S(2)}) collective-permute-start(bf16[256,128]{1,0:T(8,128)(2,1)S(1)} %pad_add_fusion.rest_0_), channel_id=1, source_target_pairs={{0,32},{8,40},{16,48},{24,56},{32,64},{40,72},{48,80},{56,88},{64,... | collective-permute-start | bytes 196616 | tf_op jit(solution)/shard_map/ppermute | solution.py:368
  11.2 2.9 %collective-permute-start.3 = (bf16[256,128]{1,0:T(8,128)(2,1)S(1)}, bf16[256,128]{1,0:T(8,128)(2,1)S(1)}, u32[]{:S(2)}, u32[]{:S(2)}) collective-permute-start(bf16[256,128]{1,0:T(8,128)(2,1)S(1)} %pad_add_fusion.rest_0_), channel_id=1, source_target_pairs={{0,56},{8,64},{16,72},{24,80},{32,88},{40,96},{48,104},{56,112},{6... | collective-permute-start | bytes 196616 | tf_op jit(solution)/shard_map/ppermute | solution.py:368
  14.0 0.0 collective-permute-done
  14.0 0.0 collective-permute-done.1
  14.1 0.7 collective-permute-done.2
  14.8 2.9 %collective-permute-done.3 = bf16[256,128]{1,0:T(8,128)(2,1)S(1)} collective-permute-done((bf16[256,128]{1,0:T(8,128)(2,1)S(1)}, bf16[256,128]{1,0:T(8,128)(2,1)S(1)}, u32[]{:S(2)}, u32[]{:S(2)}) %collective-permute-start.3) | collective-permute-done | bytes 65568 | tf_op jit(solution)/shard_map/ppermute | solution.py:368
  17.8 0.0 copy-start.1
  17.8 0.0 copy-start.2
  17.8 0.0 copy-start.3
  17.8 0.1 collective-permute-start.4
  17.9 0.4 collective-permute-start.5
  18.3 0.0 copy-start.5
  18.3 4.5 %collective-permute-start.6 = (bf16[512,128]{1,0:T(8,128)(2,1)S(1)}, bf16[512,128]{1,0:T(8,128)(2,1)S(1)}, u32[]{:S(2)}, u32[]{:S(2)}) collective-permute-start(bf16[512,128]{1,0:T(8,128)(2,1)S(1)} %get-tuple-element.35), channel_id=1, source_target_pairs={{0,248},{8,0},{16,8},{24,16},{32,24},{40,32},{48,40},{56,48},{64,5... | collective-permute-start | bytes 393224 | tf_op jit(solution)/shard_map/ppermute | solution.py:368
  22.8 2.5 %collective-permute-done.5.rest_3_ = bf16[512,128]{1,0:T(8,128)(2,1)S(1)} collective-permute-done((bf16[512,128]{1,0:T(8,128)(2,1)S(1)}, bf16[512,128]{1,0:T(8,128)(2,1)S(1)}, u32[]{:S(2)}, u32[]{:S(2)}) %collective-permute-start.5) | collective-permute-done | bytes 131104 | tf_op jit(solution)/shard_map/ppermute | solution.py:368
  25.2 0.0 collective-permute-start.7
  25.2 0.0 collective-permute-done.6.rest_4_
  25.3 0.0 collective-permute-start.8
  25.3 0.0 copy-done
  25.3 0.0 copy-done.1
  25.3 0.0 copy-done.2
  25.3 0.0 copy-done.3
  25.3 0.0 copy-done.5
  25.3 1.6 %local_features.1 = (f32[1024,256]{1,0:T(8,128)S(1)}, f32[1024,128]{1,0:T(8,128)S(1)}, f32[128,256]{1,0:T(8,128)S(1)}) custom-call(s32[1,128]{1,0:T(1,128)S(1)} %bitcast.2, bf16[128,1024]{1,0:T(8,128)(2,1)S(1)} %copy-done.1, bf16[128,128]{1,0:T(8,128)(2,1)S(1)} %copy-done.3, f32[8,128,128]{2,1,0:T(8,128)S(1)} %copy-done, f32[1,128,128]{2,1,0:T(8,128)S(1)} %copy-done.2), custom_call_target="tpu_custom_call" | custom-call | tf_op jit(solution)/shard_map/local_features/pallas_call | solution.py:391
  27.0 1.3 %collective-permute-done.4.rest_2_ = bf16[1024,128]{1,0:T(8,128)(2,1)S(1)} collective-permute-done((bf16[1024,128]{1,0:T(8,128)(2,1)S(1)}, bf16[1024,128]{1,0:T(8,128)(2,1)S(1)}, u32[]{:S(2)}, u32[]{:S(2)}) %collective-permute-start.4) | collective-permute-done | bytes 262176 | tf_op jit(solution)/shard_map/ppermute | solution.py:368
  28.3 3.0 %collective-permute-done.7.rest_5_ = bf16[512,128]{1,0:T(8,128)(2,1)S(1)} collective-permute-done((bf16[512,128]{1,0:T(8,128)(2,1)S(1)}, bf16[512,128]{1,0:T(8,128)(2,1)S(1)}, u32[]{:S(2)}, u32[]{:S(2)}) %collective-permute-start.7) | collective-permute-done | bytes 131104 | tf_op jit(solution)/shard_map/ppermute | solution.py:368
  31.3 2.3 %collective-permute-done.8.rest_6_ = bf16[512,128]{1,0:T(8,128)(2,1)S(1)} collective-permute-done((bf16[512,128]{1,0:T(8,128)(2,1)S(1)}, bf16[512,128]{1,0:T(8,128)(2,1)S(1)}, u32[]{:S(2)}, u32[]{:S(2)}) %collective-permute-start.8) | collective-permute-done | bytes 131104 | tf_op jit(solution)/shard_map/ppermute | solution.py:368
  33.6 11.1 %attention_transfer.1 = (f32[32,48,128]{2,1,0:T(8,128)}, f32[1024,128]{1,0:T(8,128)S(1)}, f32[1024,128]{1,0:T(8,128)S(1)}, f32[128,256]{1,0:T(8,128)S(1)}) custom-call(s32[1,128]{1,0:T(1,128)S(1)} %bitcast.3, bf16[128,1024]{1,0:T(8,128)(2,1)S(1)} %copy-done.1, f32[1,128,128]{2,1,0:T(8,128)S(1)} %copy-done.2, f32[1024,256]{1,0:T(8,128)S(1)} %get-tuple-element.20.phi_ref, ...), custom_call_target="tpu_custom_call" | custom-call | tf_op jit(solution)/shard_map/attention_transfer/pallas_call | solution.py:394
  44.8 3.9 %all-to-all-start = ((f32[32,48,128]{2,1,0:T(8,128)}), f32[32,48,128]{2,1,0:T(8,128)S(1)}, u32[]{:S(2)}, u32[]{:S(2)}) async-start(f32[32,48,128]{2,1,0:T(8,128)} %get-tuple-element.26), calls=%async_computation | async-start | bytes 1572864 | tf_op jit(solution)/shard_map/all_to_all | solution.py:402
  48.7 17.4 %all-to-all-done.got_ref = f32[32,48,128]{2,1,0:T(8,128)S(1)} async-done(((f32[32,48,128]{2,1,0:T(8,128)}), f32[32,48,128]{2,1,0:T(8,128)S(1)}, u32[]{:S(2)}, u32[]{:S(2)}) %all-to-all-start) | async-done | bytes 786464 | tf_op jit(solution)/shard_map/all_to_all | solution.py:402
  66.1 0.7 sum_pieces.1
  66.8 18.9 %all_to_all.15.got_ref.tail_ref = bf16[32,56,128]{2,1,0:T(8,128)(2,1)S(1)} all-to-all(bf16[32,56,128]{2,1,0:T(8,128)(2,1)S(1)} %get-tuple-element.27), channel_id=1, replica_groups=mesh['seq'=32,'head'=8] {'seq'}, dimensions={0} | all-to-all | bytes 917504 | tf_op jit(solution)/shard_map/all_to_all | solution.py:413
  85.7 0.7 head_squares.1
  86.3 10.8 %all-to-all-start.2 = ((f32[8,8,128]{2,1,0:T(8,128)}), f32[8,8,128]{2,1,0:T(8,128)S(1)}, u32[]{:S(2)}, u32[]{:S(2)}) async-start(f32[8,8,128]{2,1,0:T(8,128)} %head_squares.1), calls=%async_computation.2 | async-start | bytes 65536 | tf_op jit(solution)/shard_map/all_to_all | solution.py:415
  97.1 0.0 copy-start.4
  97.1 1.5 %query_gradients.1 = (f32[128,1024]{1,0:T(8,128)}, f32[128,128]{1,0:T(8,128)S(1)}) custom-call(f32[1024,128]{1,0:T(8,128)S(1)} %get-tuple-element.23.dlogit_ref, f32[1024,128]{1,0:T(8,128)S(1)} %get-tuple-element.21.inner_ref, f32[1024,128]{1,0:T(8,128)S(1)} %get-tuple-element.24.gn_ref, f32[8,128,128]{2,1,0:T(8,128)S(1)} %copy-done), custom_call_target="tpu_custom_call" | custom-call | tf_op jit(solution)/shard_map/query_gradients/pallas_call | solution.py:403
  98.6 0.0 copy-done.4
  98.6 1.2 %key_gradients.1 = (f32[128,128]{1,0:T(8,128)}, f32[128,128]{1,0:T(8,128)}) custom-call(s32[1,128]{1,0:T(1,128)S(1)} %bitcast.4, bf16[32,56,128]{2,1,0:T(8,128)(2,1)S(1)} %all_to_all.15.got_ref.tail_ref, f32[1,256]{1,0:T(1,128)S(1)} %get-tuple-element.28.norms_ref, bf16[128,128]{1,0:T(8,128)(2,1)S(1)} %copy-done.4, f32[1,128,128]{2,1,0:T(8,128)S(1)} %copy-done.2, ...), custom_call_target="tpu_custom_call" | custom-call | tf_op jit(solution)/shard_map/key_gradients/pallas_call | solution.py:416
  99.8 2.0 %all-to-all-done.2.squares_ref = f32[8,8,128]{2,1,0:T(8,128)S(1)} async-done(((f32[8,8,128]{2,1,0:T(8,128)}), f32[8,8,128]{2,1,0:T(8,128)S(1)}, u32[]{:S(2)}, u32[]{:S(2)}) %all-to-all-start.2) | async-done | bytes 32800 | tf_op jit(solution)/shard_map/all_to_all | solution.py:415
  101.8 0.9 clip_maps.1
  (5 shorter events, 0.1 us)
Async XLA Ops:
  1.4 23.9 %copy-start = (f32[8,128,128]{2,1,0:T(8,128)S(1)}, f32[8,128,128]{2,1,0:T(8,128)}, u32[]{:S(2)}) copy-start(f32[8,128,128]{2,1,0:T(8,128)} %qmap_ref.3) | copy-start | bytes 1572868
  1.4 12.6 %collective-permute-start = (bf16[256,128]{1,0:T(8,128)(2,1)S(1)}, bf16[256,128]{1,0:T(8,128)(2,1)S(1)}, u32[]{:S(2)}, u32[]{:S(2)}) collective-permute-start(bf16[256,128]{1,0:T(8,128)(2,1)S(1)} %pad_add_fusion.rest_0_), channel_id=1, source_target_pairs={{0,64},{8,72},{16,80},{24,88},{32,96},{40,104},{48,112},{56,120},{... | collective-permute-start | bytes 196616 | tf_op jit(solution)/shard_map/ppermute | solution.py:368
  3.5 10.5 %collective-permute-start.1 = (bf16[256,128]{1,0:T(8,128)(2,1)S(1)}, bf16[256,128]{1,0:T(8,128)(2,1)S(1)}, u32[]{:S(2)}, u32[]{:S(2)}) collective-permute-start(bf16[256,128]{1,0:T(8,128)(2,1)S(1)} %pad_add_fusion.rest_0_), channel_id=1, source_target_pairs={{0,8},{8,16},{16,24},{24,32},{32,40},{40,48},{48,56},{56,64},{64,7... | collective-permute-start | bytes 196616 | tf_op jit(solution)/shard_map/ppermute | solution.py:368
  5.2 9.6 %collective-permute-start.2 = (bf16[256,128]{1,0:T(8,128)(2,1)S(1)}, bf16[256,128]{1,0:T(8,128)(2,1)S(1)}, u32[]{:S(2)}, u32[]{:S(2)}) collective-permute-start(bf16[256,128]{1,0:T(8,128)(2,1)S(1)} %pad_add_fusion.rest_0_), channel_id=1, source_target_pairs={{0,32},{8,40},{16,48},{24,56},{32,64},{40,72},{48,80},{56,88},{64,... | collective-permute-start | bytes 196616 | tf_op jit(solution)/shard_map/ppermute | solution.py:368
  11.2 6.6 %collective-permute-start.3 = (bf16[256,128]{1,0:T(8,128)(2,1)S(1)}, bf16[256,128]{1,0:T(8,128)(2,1)S(1)}, u32[]{:S(2)}, u32[]{:S(2)}) collective-permute-start(bf16[256,128]{1,0:T(8,128)(2,1)S(1)} %pad_add_fusion.rest_0_), channel_id=1, source_target_pairs={{0,56},{8,64},{16,72},{24,80},{32,88},{40,96},{48,104},{56,112},{6... | collective-permute-start | bytes 196616 | tf_op jit(solution)/shard_map/ppermute | solution.py:368
  17.8 7.5 %copy-start.1 = (bf16[128,1024]{1,0:T(8,128)(2,1)S(1)}, bf16[128,1024]{1,0:T(8,128)(2,1)}, u32[]{:S(2)}) copy-start(bf16[128,1024]{1,0:T(8,128)(2,1)} %q_ref.3) | copy-start | bytes 786436
  17.8 7.5 %copy-start.2 = (f32[1,128,128]{2,1,0:T(8,128)S(1)}, f32[1,128,128]{2,1,0:T(8,128)}, u32[]{:S(2)}) copy-start(f32[1,128,128]{2,1,0:T(8,128)} %kmap_ref.5) | copy-start | bytes 196612
  17.8 7.5 %copy-start.3 = (bf16[128,128]{1,0:T(8,128)(2,1)S(1)}, bf16[128,128]{1,0:T(8,128)(2,1)}, u32[]{:S(2)}) copy-start(bf16[128,128]{1,0:T(8,128)(2,1)} %k_ref.1) | copy-start | bytes 98308
  17.8 10.5 %collective-permute-start.4 = (bf16[1024,128]{1,0:T(8,128)(2,1)S(1)}, bf16[1024,128]{1,0:T(8,128)(2,1)S(1)}, u32[]{:S(2)}, u32[]{:S(2)}) collective-permute-start(bf16[1024,128]{1,0:T(8,128)(2,1)S(1)} %constant_dynamic-update-slice_fusion.rest_1_), channel_id=1, source_target_pairs={{0,64},{8,72},{16,80},{24,88},{32,96},{40,104},{48,112},{56,120},{... | collective-permute-start | bytes 786440 | tf_op jit(solution)/shard_map/ppermute | solution.py:368
  17.9 7.3 %collective-permute-start.5 = (bf16[512,128]{1,0:T(8,128)(2,1)S(1)}, bf16[512,128]{1,0:T(8,128)(2,1)S(1)}, u32[]{:S(2)}, u32[]{:S(2)}) collective-permute-start(bf16[512,128]{1,0:T(8,128)(2,1)S(1)} %get-tuple-element.36), channel_id=1, source_target_pairs={{0,8},{8,16},{16,24},{24,32},{32,40},{40,48},{48,56},{56,64},{64,7... | collective-permute-start | bytes 393224 | tf_op jit(solution)/shard_map/ppermute | solution.py:368
  18.3 7.0 %copy-start.5 = (s32[128]{0:T(128)S(1)}, s32[128]{0:T(128)}, u32[]{:S(2)}) copy-start(s32[128]{0:T(128)} %param.9) | copy-start | bytes 1540
  18.3 7.0 %collective-permute-start.6 = (bf16[512,128]{1,0:T(8,128)(2,1)S(1)}, bf16[512,128]{1,0:T(8,128)(2,1)S(1)}, u32[]{:S(2)}, u32[]{:S(2)}) collective-permute-start(bf16[512,128]{1,0:T(8,128)(2,1)S(1)} %get-tuple-element.35), channel_id=1, source_target_pairs={{0,248},{8,0},{16,8},{24,16},{32,24},{40,32},{48,40},{56,48},{64,5... | collective-permute-start | bytes 393224 | tf_op jit(solution)/shard_map/ppermute | solution.py:368
  25.2 6.1 %collective-permute-start.7 = (bf16[512,128]{1,0:T(8,128)(2,1)S(1)}, bf16[512,128]{1,0:T(8,128)(2,1)S(1)}, u32[]{:S(2)}, u32[]{:S(2)}) collective-permute-start(bf16[512,128]{1,0:T(8,128)(2,1)S(1)} %collective-permute-done.5.rest_3_), channel_id=1, source_target_pairs={{0,64},{8,72},{16,80},{24,88},{32,96},{40,104},{48,112},{56,120},{... | collective-permute-start | bytes 393224 | tf_op jit(solution)/shard_map/ppermute | solution.py:368
  25.3 8.4 %collective-permute-start.8 = (bf16[512,128]{1,0:T(8,128)(2,1)S(1)}, bf16[512,128]{1,0:T(8,128)(2,1)S(1)}, u32[]{:S(2)}, u32[]{:S(2)}) collective-permute-start(bf16[512,128]{1,0:T(8,128)(2,1)S(1)} %collective-permute-done.6.rest_4_), channel_id=1, source_target_pairs={{0,64},{8,72},{16,80},{24,88},{32,96},{40,104},{48,112},{56,120},{... | collective-permute-start | bytes 393224 | tf_op jit(solution)/shard_map/ppermute | solution.py:368
  44.8 21.3 %all-to-all-start = ((f32[32,48,128]{2,1,0:T(8,128)}), f32[32,48,128]{2,1,0:T(8,128)S(1)}, u32[]{:S(2)}, u32[]{:S(2)}) async-start(f32[32,48,128]{2,1,0:T(8,128)} %get-tuple-element.26), calls=%async_computation | async-start | bytes 1572864 | tf_op jit(solution)/shard_map/all_to_all | solution.py:402
  86.3 15.5 %all-to-all-start.2 = ((f32[8,8,128]{2,1,0:T(8,128)}), f32[8,8,128]{2,1,0:T(8,128)S(1)}, u32[]{:S(2)}, u32[]{:S(2)}) async-start(f32[8,8,128]{2,1,0:T(8,128)} %head_squares.1), calls=%async_computation.2 | async-start | bytes 65536 | tf_op jit(solution)/shard_map/all_to_all | solution.py:415
  97.1 1.5 %copy-start.4 = (bf16[128,128]{1,0:T(8,128)(2,1)S(1)}, bf16[128,128]{1,0:T(8,128)(2,1)}, u32[]{:S(2)}) copy-start(bf16[128,128]{1,0:T(8,128)(2,1)} %v_ref.1) | copy-start | bytes 98308

commit v7 on v6

--- a/solution.py
+++ b/solution.py
@@ -362,19 +362,18 @@
 
 def window_of(kv):
     n = lax.axis_size("seq")
-    size = kv.shape[0]
 
     def shift(x, k):
         return lax.ppermute(x, "seq", [(i, (i + k) % n) for i in range(n)])
 
-    b1, b4, b7, b8 = (shift(kv, k) for k in (1, 4, 7, 8))
-    near = jnp.concatenate([b8, b1, b4, b7], axis=0)
+    b4, b8, b1, b7 = (shift(kv, k) for k in (4, 8, 1, 7))
+    near = jnp.concatenate([b4, b8, b1, b7], axis=0)
+    n1 = shift(jnp.concatenate([b1, b4], axis=0), 1)
+    n2 = shift(jnp.concatenate([b4, b7], axis=0), -1)
     far = shift(near, 8)
-    up, down = slice(size, 3 * size), slice(2 * size, 4 * size)
-    n1, n2 = shift(near[up], 1), shift(near[down], -1)
     f1, f2 = shift(n1, 8), shift(n2, 8)
     arrays = [kv, near, far, n1, n2, f1, f2]
-    places = [(0,), (8, 1, 4, 7), (16, 9, 12, 15), (2, 5), (3, 6), (10, 13), (11, 14)]
+    places = [(0,), (4, 8, 1, 7), (12, 16, 9, 15), (2, 5), (3, 6), (10, 13), (11, 14)]
     return arrays, places
 
 

time: 103 us -> 102 us (level)
  waiting for transfers between devices: 32.2 us -> 29.6 us
  starting transfers between devices: 32.2 us -> 33.7 us
    all_to_all x1, waiting for transfers between devices: 17.4 us -> 15.9 us  [on_device(): gathered = lax.all_to_all(payload, 'seq', 0, 0)]
    ppermute x9, waiting for transfers between devices: 12.8 us -> 11.6 us  [shift(): return lax.ppermute(x, 'seq', [(i, (i + k) % n) for i in range(n)])]
    all_to_all x1, starting transfers between devices: 10.8 us -> 11.9 us  [on_device(): squares = lax.all_to_all(squares, 'head', 0, 0)]
where the time goes in v7:
time: 102 us
  starting transfers between devices  33.7 us (33%)
  waiting for transfers between devices  29.6 us (29%)
  blocking collectives  19.1 us (19%)
  Pallas kernels  17.7 us (17%)
    all_to_all x1, blocking collectives, on_device(): back = lax.all_to_all(reduced, 'seq', 0, 0)  19.1 us
    ppermute x9, starting transfers between devices, shift(): return lax.ppermute(x, 'seq', [(i, (i + k) % n) for i in range(n)])  17.6 us
    all_to_all x1, waiting for transfers between devices, on_device(): gathered = lax.all_to_all(payload, 'seq', 0, 0)  15.9 us
    all_to_all x1, starting transfers between devices, on_device(): squares = lax.all_to_all(squares, 'head', 0, 0)  11.9 us
    ppermute x9, waiting for transfers between devices, shift(): return lax.ppermute(x, 'seq', [(i, (i + k) % n) for i in range(n)])  11.6 us
    pallas_call x1, Pallas kernels, on_device(): call(functools.partial(main_kernel, places), 'attention_transfer', [V] *...  11.1 us
    all_to_all x1, starting transfers between devices, on_device(): gathered = lax.all_to_all(payload, 'seq', 0, 0)  4.27 us
    all_to_all x1, waiting for transfers between devices, on_device(): squares = lax.all_to_all(squares, 'head', 0, 0)  2.05 us
  transfers between devices with their start and end apart: 11, of which 8 were waited for; matrix products, arithmetic and copies ran while one was open for 0% of the time, Pallas kernels for 4%

profile of v7, /device:TPU:1, one launch (start us, length us, event | category | flops | bytes accessed | tf_op | source)
XLA Modules:
  0.0 101.7 jit_solution(16177330357020114257)
XLA Ops:
  0.6 0.8 pad_add_fusion.rest_0_
  1.4 0.0 copy-start
  1.4 7.8 %collective-permute-start = (bf16[256,128]{1,0:T(8,128)(2,1)S(1)}, bf16[256,128]{1,0:T(8,128)(2,1)S(1)}, u32[]{:S(2)}, u32[]{:S(2)}) collective-permute-start(bf16[256,128]{1,0:T(8,128)(2,1)S(1)} %pad_add_fusion.rest_0_), channel_id=1, source_target_pairs={{0,32},{8,40},{16,48},{24,56},{32,64},{40,72},{48,80},{56,88},{64,... | collective-permute-start | bytes 196616 | tf_op jit(solution)/shard_map/ppermute | solution.py:367
  9.2 1.2 %collective-permute-start.1 = (bf16[256,128]{1,0:T(8,128)(2,1)S(1)}, bf16[256,128]{1,0:T(8,128)(2,1)S(1)}, u32[]{:S(2)}, u32[]{:S(2)}) collective-permute-start(bf16[256,128]{1,0:T(8,128)(2,1)S(1)} %pad_add_fusion.rest_0_), channel_id=1, source_target_pairs={{0,64},{8,72},{16,80},{24,88},{32,96},{40,104},{48,112},{56,120},{... | collective-permute-start | bytes 196616 | tf_op jit(solution)/shard_map/ppermute | solution.py:367
  10.4 0.7 collective-permute-start.2
  11.2 2.9 %collective-permute-start.3 = (bf16[256,128]{1,0:T(8,128)(2,1)S(1)}, bf16[256,128]{1,0:T(8,128)(2,1)S(1)}, u32[]{:S(2)}, u32[]{:S(2)}) collective-permute-start(bf16[256,128]{1,0:T(8,128)(2,1)S(1)} %pad_add_fusion.rest_0_), channel_id=1, source_target_pairs={{0,56},{8,64},{16,72},{24,80},{32,88},{40,96},{48,104},{56,112},{6... | collective-permute-start | bytes 196616 | tf_op jit(solution)/shard_map/ppermute | solution.py:367
  14.0 0.0 collective-permute-done
  14.0 0.2 collective-permute-done.1
  14.2 3.0 %collective-permute-done.2 = bf16[256,128]{1,0:T(8,128)(2,1)S(1)} collective-permute-done((bf16[256,128]{1,0:T(8,128)(2,1)S(1)}, bf16[256,128]{1,0:T(8,128)(2,1)S(1)}, u32[]{:S(2)}, u32[]{:S(2)}) %collective-permute-start.2) | collective-permute-done | bytes 65568 | tf_op jit(solution)/shard_map/ppermute | solution.py:367
  17.3 0.1 collective-permute-done.3
  17.4 0.0 copy-start.1
  17.4 0.0 copy-start.2
  17.5 0.0 copy-start.3
  17.5 0.1 collective-permute-start.4
  17.6 0.1 collective-permute-start.5
  17.7 0.0 copy-start.5
  17.7 4.8 %collective-permute-start.6 = (bf16[512,128]{1,0:T(8,128)(2,1)S(1)}, bf16[512,128]{1,0:T(8,128)(2,1)S(1)}, u32[]{:S(2)}, u32[]{:S(2)}) collective-permute-start(bf16[512,128]{1,0:T(8,128)(2,1)S(1)} %get-tuple-element.35), channel_id=1, source_target_pairs={{0,248},{8,0},{16,8},{24,16},{32,24},{40,32},{48,40},{56,48},{64,5... | collective-permute-start | bytes 393224 | tf_op jit(solution)/shard_map/ppermute | solution.py:367
  22.5 2.5 %collective-permute-done.5.rest_3_ = bf16[512,128]{1,0:T(8,128)(2,1)S(1)} collective-permute-done((bf16[512,128]{1,0:T(8,128)(2,1)S(1)}, bf16[512,128]{1,0:T(8,128)(2,1)S(1)}, u32[]{:S(2)}, u32[]{:S(2)}) %collective-permute-start.5) | collective-permute-done | bytes 131104 | tf_op jit(solution)/shard_map/ppermute | solution.py:367
  24.9 0.0 collective-permute-start.7
  24.9 0.0 collective-permute-done.6.rest_4_
  24.9 0.0 collective-permute-start.8
  24.9 0.0 copy-done
  25.0 0.0 copy-done.1
  25.0 0.0 copy-done.2
  25.0 0.0 copy-done.3
  25.0 0.0 copy-done.5
  25.0 1.6 %local_features.1 = (f32[1024,256]{1,0:T(8,128)S(1)}, f32[1024,128]{1,0:T(8,128)S(1)}, f32[128,256]{1,0:T(8,128)S(1)}) custom-call(s32[1,128]{1,0:T(1,128)S(1)} %bitcast.2, bf16[128,1024]{1,0:T(8,128)(2,1)S(1)} %copy-done.1, bf16[128,128]{1,0:T(8,128)(2,1)S(1)} %copy-done.3, f32[8,128,128]{2,1,0:T(8,128)S(1)} %copy-done, f32[1,128,128]{2,1,0:T(8,128)S(1)} %copy-done.2), custom_call_target="tpu_custom_call" | custom-call | tf_op jit(solution)/shard_map/local_features/pallas_call | solution.py:390
  26.6 0.0 collective-permute-done.4.rest_2_
  26.6 4.4 %collective-permute-done.7.rest_5_ = bf16[512,128]{1,0:T(8,128)(2,1)S(1)} collective-permute-done((bf16[512,128]{1,0:T(8,128)(2,1)S(1)}, bf16[512,128]{1,0:T(8,128)(2,1)S(1)}, u32[]{:S(2)}, u32[]{:S(2)}) %collective-permute-start.7) | collective-permute-done | bytes 131104 | tf_op jit(solution)/shard_map/ppermute | solution.py:367
  31.0 1.4 %collective-permute-done.8.rest_6_ = bf16[512,128]{1,0:T(8,128)(2,1)S(1)} collective-permute-done((bf16[512,128]{1,0:T(8,128)(2,1)S(1)}, bf16[512,128]{1,0:T(8,128)(2,1)S(1)}, u32[]{:S(2)}, u32[]{:S(2)}) %collective-permute-start.8) | collective-permute-done | bytes 131104 | tf_op jit(solution)/shard_map/ppermute | solution.py:367
  32.4 11.1 %attention_transfer.1 = (f32[32,48,128]{2,1,0:T(8,128)}, f32[1024,128]{1,0:T(8,128)S(1)}, f32[1024,128]{1,0:T(8,128)S(1)}, f32[128,256]{1,0:T(8,128)S(1)}) custom-call(s32[1,128]{1,0:T(1,128)S(1)} %bitcast.3, bf16[128,1024]{1,0:T(8,128)(2,1)S(1)} %copy-done.1, f32[1,128,128]{2,1,0:T(8,128)S(1)} %copy-done.2, f32[1024,256]{1,0:T(8,128)S(1)} %get-tuple-element.20.phi_ref, ...), custom_call_target="tpu_custom_call" | custom-call | tf_op jit(solution)/shard_map/attention_transfer/pallas_call | solution.py:393
  43.6 4.3 %all-to-all-start = ((f32[32,48,128]{2,1,0:T(8,128)}), f32[32,48,128]{2,1,0:T(8,128)S(1)}, u32[]{:S(2)}, u32[]{:S(2)}) async-start(f32[32,48,128]{2,1,0:T(8,128)} %get-tuple-element.26), calls=%async_computation | async-start | bytes 1572864 | tf_op jit(solution)/shard_map/all_to_all | solution.py:401
  47.8 15.9 %all-to-all-done.got_ref = f32[32,48,128]{2,1,0:T(8,128)S(1)} async-done(((f32[32,48,128]{2,1,0:T(8,128)}), f32[32,48,128]{2,1,0:T(8,128)S(1)}, u32[]{:S(2)}, u32[]{:S(2)}) %all-to-all-start) | async-done | bytes 786464 | tf_op jit(solution)/shard_map/all_to_all | solution.py:401
  63.8 0.7 sum_pieces.1
  64.5 19.1 %all_to_all.15.got_ref.tail_ref = bf16[32,56,128]{2,1,0:T(8,128)(2,1)S(1)} all-to-all(bf16[32,56,128]{2,1,0:T(8,128)(2,1)S(1)} %get-tuple-element.27), channel_id=1, replica_groups=mesh['seq'=32,'head'=8] {'seq'}, dimensions={0} | all-to-all | bytes 917504 | tf_op jit(solution)/shard_map/all_to_all | solution.py:412
  83.6 0.7 head_squares.1
  84.2 11.9 %all-to-all-start.2 = ((f32[8,8,128]{2,1,0:T(8,128)}), f32[8,8,128]{2,1,0:T(8,128)S(1)}, u32[]{:S(2)}, u32[]{:S(2)}) async-start(f32[8,8,128]{2,1,0:T(8,128)} %head_squares.1), calls=%async_computation.2 | async-start | bytes 65536 | tf_op jit(solution)/shard_map/all_to_all | solution.py:414
  96.1 0.0 copy-start.4
  96.1 1.5 %query_gradients.1 = (f32[128,1024]{1,0:T(8,128)}, f32[128,128]{1,0:T(8,128)S(1)}) custom-call(f32[1024,128]{1,0:T(8,128)S(1)} %get-tuple-element.23.dlogit_ref, f32[1024,128]{1,0:T(8,128)S(1)} %get-tuple-element.21.inner_ref, f32[1024,128]{1,0:T(8,128)S(1)} %get-tuple-element.24.gn_ref, f32[8,128,128]{2,1,0:T(8,128)S(1)} %copy-done), custom_call_target="tpu_custom_call" | custom-call | tf_op jit(solution)/shard_map/query_gradients/pallas_call | solution.py:402
  97.6 0.0 copy-done.4
  97.6 1.2 %key_gradients.1 = (f32[128,128]{1,0:T(8,128)}, f32[128,128]{1,0:T(8,128)}) custom-call(s32[1,128]{1,0:T(1,128)S(1)} %bitcast.4, bf16[32,56,128]{2,1,0:T(8,128)(2,1)S(1)} %all_to_all.15.got_ref.tail_ref, f32[1,256]{1,0:T(1,128)S(1)} %get-tuple-element.28.norms_ref, bf16[128,128]{1,0:T(8,128)(2,1)S(1)} %copy-done.4, f32[1,128,128]{2,1,0:T(8,128)S(1)} %copy-done.2, ...), custom_call_target="tpu_custom_call" | custom-call | tf_op jit(solution)/shard_map/key_gradients/pallas_call | solution.py:415
  98.8 2.0 %all-to-all-done.2.squares_ref = f32[8,8,128]{2,1,0:T(8,128)S(1)} async-done(((f32[8,8,128]{2,1,0:T(8,128)}), f32[8,8,128]{2,1,0:T(8,128)S(1)}, u32[]{:S(2)}, u32[]{:S(2)}) %all-to-all-start.2) | async-done | bytes 32800 | tf_op jit(solution)/shard_map/all_to_all | solution.py:414
  100.8 0.9 clip_maps.1
  (5 shorter events, 0.1 us)
Async XLA Ops:
  1.4 23.5 %copy-start = (f32[8,128,128]{2,1,0:T(8,128)S(1)}, f32[8,128,128]{2,1,0:T(8,128)}, u32[]{:S(2)}) copy-start(f32[8,128,128]{2,1,0:T(8,128)} %qmap_ref.3) | copy-start | bytes 1572868
  1.4 12.6 %collective-permute-start = (bf16[256,128]{1,0:T(8,128)(2,1)S(1)}, bf16[256,128]{1,0:T(8,128)(2,1)S(1)}, u32[]{:S(2)}, u32[]{:S(2)}) collective-permute-start(bf16[256,128]{1,0:T(8,128)(2,1)S(1)} %pad_add_fusion.rest_0_), channel_id=1, source_target_pairs={{0,32},{8,40},{16,48},{24,56},{32,64},{40,72},{48,80},{56,88},{64,... | collective-permute-start | bytes 196616 | tf_op jit(solution)/shard_map/ppermute | solution.py:367
  9.2 5.0 %collective-permute-start.1 = (bf16[256,128]{1,0:T(8,128)(2,1)S(1)}, bf16[256,128]{1,0:T(8,128)(2,1)S(1)}, u32[]{:S(2)}, u32[]{:S(2)}) collective-permute-start(bf16[256,128]{1,0:T(8,128)(2,1)S(1)} %pad_add_fusion.rest_0_), channel_id=1, source_target_pairs={{0,64},{8,72},{16,80},{24,88},{32,96},{40,104},{48,112},{56,120},{... | collective-permute-start | bytes 196616 | tf_op jit(solution)/shard_map/ppermute | solution.py:367
  10.4 6.8 %collective-permute-start.2 = (bf16[256,128]{1,0:T(8,128)(2,1)S(1)}, bf16[256,128]{1,0:T(8,128)(2,1)S(1)}, u32[]{:S(2)}, u32[]{:S(2)}) collective-permute-start(bf16[256,128]{1,0:T(8,128)(2,1)S(1)} %pad_add_fusion.rest_0_), channel_id=1, source_target_pairs={{0,8},{8,16},{16,24},{24,32},{32,40},{40,48},{48,56},{56,64},{64,7... | collective-permute-start | bytes 196616 | tf_op jit(solution)/shard_map/ppermute | solution.py:367
  11.2 6.3 %collective-permute-start.3 = (bf16[256,128]{1,0:T(8,128)(2,1)S(1)}, bf16[256,128]{1,0:T(8,128)(2,1)S(1)}, u32[]{:S(2)}, u32[]{:S(2)}) collective-permute-start(bf16[256,128]{1,0:T(8,128)(2,1)S(1)} %pad_add_fusion.rest_0_), channel_id=1, source_target_pairs={{0,56},{8,64},{16,72},{24,80},{32,88},{40,96},{48,104},{56,112},{6... | collective-permute-start | bytes 196616 | tf_op jit(solution)/shard_map/ppermute | solution.py:367
  17.4 7.5 %copy-start.1 = (bf16[128,1024]{1,0:T(8,128)(2,1)S(1)}, bf16[128,1024]{1,0:T(8,128)(2,1)}, u32[]{:S(2)}) copy-start(bf16[128,1024]{1,0:T(8,128)(2,1)} %q_ref.3) | copy-start | bytes 786436
  17.4 7.5 %copy-start.2 = (f32[1,128,128]{2,1,0:T(8,128)S(1)}, f32[1,128,128]{2,1,0:T(8,128)}, u32[]{:S(2)}) copy-start(f32[1,128,128]{2,1,0:T(8,128)} %kmap_ref.5) | copy-start | bytes 196612
  17.5 7.5 %copy-start.3 = (bf16[128,128]{1,0:T(8,128)(2,1)S(1)}, bf16[128,128]{1,0:T(8,128)(2,1)}, u32[]{:S(2)}) copy-start(bf16[128,128]{1,0:T(8,128)(2,1)} %k_ref.1) | copy-start | bytes 98308
  17.5 9.2 %collective-permute-start.4 = (bf16[1024,128]{1,0:T(8,128)(2,1)S(1)}, bf16[1024,128]{1,0:T(8,128)(2,1)S(1)}, u32[]{:S(2)}, u32[]{:S(2)}) collective-permute-start(bf16[1024,128]{1,0:T(8,128)(2,1)S(1)} %constant_dynamic-update-slice_fusion.rest_1_), channel_id=1, source_target_pairs={{0,64},{8,72},{16,80},{24,88},{32,96},{40,104},{48,112},{56,120},{... | collective-permute-start | bytes 786440 | tf_op jit(solution)/shard_map/ppermute | solution.py:367
  17.6 7.3 %collective-permute-start.5 = (bf16[512,128]{1,0:T(8,128)(2,1)S(1)}, bf16[512,128]{1,0:T(8,128)(2,1)S(1)}, u32[]{:S(2)}, u32[]{:S(2)}) collective-permute-start(bf16[512,128]{1,0:T(8,128)(2,1)S(1)} %get-tuple-element.36), channel_id=1, source_target_pairs={{0,8},{8,16},{16,24},{24,32},{32,40},{40,48},{48,56},{56,64},{64,7... | collective-permute-start | bytes 393224 | tf_op jit(solution)/shard_map/ppermute | solution.py:367
  17.7 7.3 %copy-start.5 = (s32[128]{0:T(128)S(1)}, s32[128]{0:T(128)}, u32[]{:S(2)}) copy-start(s32[128]{0:T(128)} %param.9) | copy-start | bytes 1540
  17.7 7.2 %collective-permute-start.6 = (bf16[512,128]{1,0:T(8,128)(2,1)S(1)}, bf16[512,128]{1,0:T(8,128)(2,1)S(1)}, u32[]{:S(2)}, u32[]{:S(2)}) collective-permute-start(bf16[512,128]{1,0:T(8,128)(2,1)S(1)} %get-tuple-element.35), channel_id=1, source_target_pairs={{0,248},{8,0},{16,8},{24,16},{32,24},{40,32},{48,40},{56,48},{64,5... | collective-permute-start | bytes 393224 | tf_op jit(solution)/shard_map/ppermute | solution.py:367
  24.9 6.1 %collective-permute-start.7 = (bf16[512,128]{1,0:T(8,128)(2,1)S(1)}, bf16[512,128]{1,0:T(8,128)(2,1)S(1)}, u32[]{:S(2)}, u32[]{:S(2)}) collective-permute-start(bf16[512,128]{1,0:T(8,128)(2,1)S(1)} %collective-permute-done.5.rest_3_), channel_id=1, source_target_pairs={{0,64},{8,72},{16,80},{24,88},{32,96},{40,104},{48,112},{56,120},{... | collective-permute-start | bytes 393224 | tf_op jit(solution)/shard_map/ppermute | solution.py:367
  24.9 7.5 %collective-permute-start.8 = (bf16[512,128]{1,0:T(8,128)(2,1)S(1)}, bf16[512,128]{1,0:T(8,128)(2,1)S(1)}, u32[]{:S(2)}, u32[]{:S(2)}) collective-permute-start(bf16[512,128]{1,0:T(8,128)(2,1)S(1)} %collective-permute-done.6.rest_4_), channel_id=1, source_target_pairs={{0,64},{8,72},{16,80},{24,88},{32,96},{40,104},{48,112},{56,120},{... | collective-permute-start | bytes 393224 | tf_op jit(solution)/shard_map/ppermute | solution.py:367
  43.6 20.2 %all-to-all-start = ((f32[32,48,128]{2,1,0:T(8,128)}), f32[32,48,128]{2,1,0:T(8,128)S(1)}, u32[]{:S(2)}, u32[]{:S(2)}) async-start(f32[32,48,128]{2,1,0:T(8,128)} %get-tuple-element.26), calls=%async_computation | async-start | bytes 1572864 | tf_op jit(solution)/shard_map/all_to_all | solution.py:401
  84.2 16.6 %all-to-all-start.2 = ((f32[8,8,128]{2,1,0:T(8,128)}), f32[8,8,128]{2,1,0:T(8,128)S(1)}, u32[]{:S(2)}, u32[]{:S(2)}) async-start(f32[8,8,128]{2,1,0:T(8,128)} %head_squares.1), calls=%async_computation.2 | async-start | bytes 65536 | tf_op jit(solution)/shard_map/all_to_all | solution.py:414
  96.1 1.5 %copy-start.4 = (bf16[128,128]{1,0:T(8,128)(2,1)S(1)}, bf16[128,128]{1,0:T(8,128)(2,1)}, u32[]{:S(2)}) copy-start(bf16[128,128]{1,0:T(8,128)(2,1)} %v_ref.1) | copy-start | bytes 98308

commit v8 on v7

--- a/solution.py
+++ b/solution.py
@@ -16,7 +16,6 @@
 WINDOW = 16
 KEYS = (WINDOW + 1) * T
 TEACHER = 512
-CHUNK = 1024
 PIECE = 48
 STATE_ROW, KMAP_ROW, NORM_ROW, INFO_ROW = 32, 40, 44, 46
 REPLY = 56
@@ -147,59 +146,109 @@
     inner_ref[...] = product(nt, split2(phi), split2(own)) * seen
 
 
-def main_kernel(places, pos_ref, q_ref, kmap_ref, phi_ref, inner_ref, own_ref, *rest):
+def hold_keys(arrays, places, pos_ref, k_s, v_s):
+    row = lax.broadcasted_iota(jnp.int32, (T, 1), 0).astype(F32)
+    entry = -pos_ref[0:1, 0:1].astype(F32)
+    lane = lax.broadcasted_iota(jnp.int32, (T, T), 1)
+    at = 0
+    keys = []
+    for ref, held in zip(arrays, places):
+        for slot, block in enumerate(held):
+            k_s[at : at + T, :T] = ref[slot * 2 * T : slot * 2 * T + T, :]
+            v_s[at : at + T, :T] = ref[slot * 2 * T + T : slot * 2 * T + 2 * T, :]
+            key = row - float(block * T)
+            hidden = jnp.where(key >= entry, 0.0, NEGATIVE)
+            hidden = jnp.where(lane == 0, NEGATIVE, jnp.where(lane == 1, hidden, 0.0))
+            k_s[at : at + T, T:] = (hidden if block else jnp.zeros((T, T), F32)).astype(BF16)
+            keys.append(key)
+            at += T
+    v_s[:, T:] = jnp.ones(v_s[:, T:].shape, BF16)
+    return keys, entry
+
+
+def key_features(rows, keys, entry, matrix, k_s, v_s):
+    features = feature_map(logits_of(k_s[rows, :T], matrix))
+    features = jnp.where(jnp.concatenate(keys, axis=0) >= entry, features, 0.0)
+    return features, exact_right(tn, split2(features), v_s[rows, :])
+
+
+def asking(q_ref, crossing):
+    heads = q_ref.shape[1] // T
+    lane = lax.broadcasted_iota(jnp.int32, (T, T), 1)
+    hider = jnp.where(lane == 0, 1.0 - crossing, jnp.where(lane == 1, 1.0, 0.0)).astype(BF16)
+    return deep([stacked(q_ref), every_head(hider, heads)])
+
+
+RATE = math.log2(math.e) / math.sqrt(T)
+
+
+def part_kernel(places, pos_ref, q_ref, kmap_ref, *rest):
+    count = len(places)
+    phi_ref, state_ref, top_ref, total_ref, sum_ref = rest[count : count + 5]
+    k_s, v_s = rest[count + 5 :]
+    _, start = positions_of(pos_ref)
+    keys, entry = hold_keys(rest[:count], places, pos_ref, k_s, v_s)
+    phi_ref[...], state_ref[...] = key_features(
+        slice(None), keys, entry, map_of(kmap_ref[0]), k_s, v_s
+    )
+    queries = asking(q_ref, (start < 0.0).astype(F32))
+    for at in range(0, queries.shape[0], TEACHER):
+        rows = slice(at, at + TEACHER)
+        scores = nt(queries[rows, :], k_s[...])
+        top = jnp.max(scores, axis=-1, keepdims=True)
+        weights = jnp.exp2((scores - top) * RATE)
+        total = jnp.sum(weights, axis=-1, keepdims=True)
+        sum_ref[rows, :] = nn(weights.astype(BF16), v_s[:, :T])
+        top_ref[rows, :] = jnp.broadcast_to(top, (TEACHER, T))
+        total_ref[rows, :] = jnp.broadcast_to(total, (TEACHER, T))
+
+
+def main_kernel(places, parts, pos_ref, q_ref, kmap_ref, phi_ref, inner_ref, own_ref, *rest):
     count = len(places)
     blocks = rest[:count]
-    payload_ref, dlogit_ref, gn_ref, gkphi_ref = rest[count : count + 4]
-    k_s, v_s, phi_s = rest[count + 4 :]
+    done = [rest[count + 5 * i : count + 5 * i + 5] for i in range(parts)]
+    rest = rest[count + 5 * parts :]
+    payload_ref, dlogit_ref, gn_ref, gkphi_ref, k_s, v_s = rest
     heads = q_ref.shape[1] // T
     row, start = positions_of(pos_ref)
-    entry = -pos_ref[0:1, 0:1].astype(F32)
     crossing = (start < 0.0).astype(F32)
-    lane = lax.broadcasted_iota(jnp.int32, (T, T), 1)
-    for ref, held in zip(blocks, places):
-        for slot, block in enumerate(held):
-            at = (WINDOW - block) * T
-            k_s[at : at + T, :T] = ref[slot * 2 * T : slot * 2 * T + T, :]
-            v_s[at : at + T, :T] = ref[slot * 2 * T + T : slot * 2 * T + 2 * T, :]
-            hidden = jnp.where(row - float(block * T) >= entry, 0.0, NEGATIVE)
-            hidden = jnp.where(lane == 0, NEGATIVE, jnp.where(lane == 1, hidden, 0.0))
-            k_s[at : at + T, T:] = (hidden if block else jnp.zeros((T, T), F32)).astype(BF16)
-    v_s[:, T:] = jnp.ones((KEYS, T), BF16)
-
-    matrix = map_of(kmap_ref[0])
-    state = jnp.zeros((2 * T, 2 * T), F32)
-    for at in range(0, WINDOW * T, CHUNK):
-        key_row = lax.broadcasted_iota(jnp.int32, (CHUNK, 1), 0) + (at - WINDOW * T)
-        features = feature_map(logits_of(k_s[at : at + CHUNK, :T], matrix))
-        features = jnp.where(key_row.astype(F32) >= entry, features, 0.0)
-        phi_s[at : at + CHUNK, :] = features
-        state = state + exact_right(tn, split2(features), v_s[at : at + CHUNK, :])
+    keys, entry = hold_keys(blocks, places, pos_ref, k_s, v_s)
+    first = sum(part[0].shape[0] for part in done)
+    late, state = key_features(
+        slice(first, WINDOW * T), keys[first // T : WINDOW], entry, map_of(kmap_ref[0]), k_s, v_s
+    )
+    for part in done:
+        state = state + part[1][...]
     norms = jnp.transpose(state[:, T:])[0:1, :]
     state = split2(state)
 
-    own_key = lane.astype(F32)
+    own_key = lax.broadcasted_iota(jnp.int32, (T, T), 1).astype(F32)
     visible = (own_key <= row) & (own_key >= start)
     seen = every_head(visible.astype(F32), heads)
     bias = every_head(jnp.where(visible, 0.0, NEGATIVE), heads)
     cross = every_head(jnp.broadcast_to(crossing, (T, T)), heads)
-    hider = jnp.where(lane == 0, 1.0 - crossing, jnp.where(lane == 1, 1.0, 0.0)).astype(BF16)
-    queries = jnp.concatenate([stacked(q_ref), every_head(hider, heads)], axis=1)
+    queries = asking(q_ref, crossing)
     own_v = v_s[WINDOW * T :, :]
-    rate = math.log2(math.e) / math.sqrt(T)
     teachers = []
     for at in range(0, heads * T, TEACHER):
         rows = slice(at, at + TEACHER)
-        scores = nt(queries[rows, :], k_s[...])
-        near = scores[:, WINDOW * T :] + bias[rows, :]
-        far = scores[:, : WINDOW * T]
-        highest = jnp.maximum(
+        scores = nt(queries[rows, :], k_s[first:, :])
+        near = scores[:, WINDOW * T - first :] + bias[rows, :]
+        far = scores[:, : WINDOW * T - first]
+        top = jnp.maximum(
             jnp.max(near, axis=-1, keepdims=True), jnp.max(far, axis=-1, keepdims=True)
         )
-        near = jnp.exp2((near - highest) * rate)
-        far = jnp.exp2((far - highest) * rate)
+        top = jnp.broadcast_to(top, (TEACHER, T))
+        for part in done:
+            top = jnp.maximum(top, part[2][rows, :])
+        near = jnp.exp2((near - top) * RATE)
+        far = jnp.exp2((far - top[:, 0:1]) * RATE)
         total = jnp.sum(near, axis=-1, keepdims=True) + jnp.sum(far, axis=-1, keepdims=True)
-        summed = nn(near.astype(BF16), own_v[:, :T]) + nn(far.astype(BF16), v_s[: WINDOW * T, :T])
+        summed = nn(deep([far, near]).astype(BF16), v_s[first:, :T])
+        for part in done:
+            fading = jnp.exp2((part[2][rows, :] - top) * RATE)
+            total = total + fading * part[3][rows, :]
+            summed = summed + fading * part[4][rows, :]
         teachers.append(summed / total)
     teacher = jnp.concatenate(teachers, axis=0)
 
@@ -249,10 +298,13 @@
     part = split2(feature_back(own, gkphi))
     grad_map = wide_exact_left(tn, k_s[WINDOW * T :, :T], part)
     back_parts = split2(jnp.concatenate([back[:, :T], back[:, T:] * (1.0 / T)], axis=1))
-    for at in range(0, WINDOW * T, CHUNK):
-        grad = exact_left(nt, v_s[at : at + CHUNK, :], back_parts)
-        part = split2(feature_back(phi_s[at : at + CHUNK, :], grad))
-        grad_map = grad_map + wide_exact_left(tn, k_s[at : at + CHUNK, :T], part)
+    at = 0
+    for features in [part[0][...] for part in done] + [late]:
+        rows = slice(at, at + features.shape[0])
+        grad = exact_left(nt, v_s[rows, :], back_parts)
+        part = split2(feature_back(features, grad))
+        grad_map = grad_map + wide_exact_left(tn, k_s[rows, :T], part)
+        at += features.shape[0]
     tail = jnp.concatenate(
         [
             backn[:, :T],
@@ -360,23 +412,6 @@
     )
 
 
-def window_of(kv):
-    n = lax.axis_size("seq")
-
-    def shift(x, k):
-        return lax.ppermute(x, "seq", [(i, (i + k) % n) for i in range(n)])
-
-    b4, b8, b1, b7 = (shift(kv, k) for k in (4, 8, 1, 7))
-    near = jnp.concatenate([b4, b8, b1, b7], axis=0)
-    n1 = shift(jnp.concatenate([b1, b4], axis=0), 1)
-    n2 = shift(jnp.concatenate([b4, b7], axis=0), -1)
-    far = shift(near, 8)
-    f1, f2 = shift(n1, 8), shift(n2, 8)
-    arrays = [kv, near, far, n1, n2, f1, f2]
-    places = [(0,), (4, 8, 1, 7), (12, 16, 9, 15), (2, 5), (3, 6), (10, 13), (11, 14)]
-    return arrays, places
-
-
 def on_device(queries, key_vectors, value_vectors, positions, query_map, key_map):
     group = query_map.shape[0]
     pieces = lax.axis_size("seq")
@@ -385,19 +420,45 @@
     me = lax.axis_index("seq").astype(jnp.int32).reshape(1)
     pos = positions.reshape(1, T)
     kv = joined(key_vectors, value_vectors)
-    arrays, places = window_of(kv)
     V = pltpu.VMEM
+
+    def shift(x, k):
+        return lax.ppermute(x, "seq", [(i, (i + k) % pieces) for i in range(pieces)])
+
+    def part_of(name, arrays, places):
+        size = T * sum(len(held) for held in places)
+        return call(
+            functools.partial(part_kernel, places),
+            name,
+            [V] * (3 + len(arrays)),
+            [(size, 2 * T), (2 * T, 2 * T), (rows, T), (rows, T), (rows, T)],
+            [V((size, 2 * T), BF16), V((size, 2 * T), BF16)],
+            24,
+        )(pos, queries, key_map, *arrays)
+
+    b4, b8, b1, b7 = (shift(kv, k) for k in (4, 8, 1, 7))
     phi, inner, own = call(
         local_kernel, "local_features", [V] * 5, [(rows, 2 * T), (rows, T), (T, 2 * T)]
     )(pos, queries, key_vectors, query_map, key_map)
+    b4, b8, b1, b7, own = lax.optimization_barrier((b4, b8, b1, b7, own))
+    near = jnp.concatenate([b4, b8, b1, b7], axis=0)
+    n1 = shift(jnp.concatenate([b1, b4], axis=0), 1)
+    n2 = shift(jnp.concatenate([b4, b7], axis=0), -1)
+    far = shift(near, 8)
+    early = list(part_of("early_keys", [near], [(4, 8, 1, 7)]))
+    n1, n2, early[1] = lax.optimization_barrier((n1, n2, early[1]))
+    f1, f2 = shift(n1, 8), shift(n2, 8)
+    middle = part_of("middle_keys", [far, n1, n2], [(12, 16, 9, 15), (2, 5), (3, 6)])
+    arrays = [near, far, n1, n2, f1, f2, kv]
+    places = [(4, 8, 1, 7), (12, 16, 9, 15), (2, 5), (3, 6), (10, 13), (11, 14), (0,)]
     payload, dlogit, grad_numer, gkphi = call(
-        functools.partial(main_kernel, places),
+        functools.partial(main_kernel, places, 2),
         "attention_transfer",
-        [V] * (6 + len(arrays)),
+        [V] * (6 + len(arrays) + 10),
         [(pieces, PIECE, T), (rows, T), (rows, T), (T, 2 * T)],
-        [V((KEYS, 2 * T), BF16), V((KEYS, 2 * T), BF16), V((WINDOW * T, 2 * T), F32)],
+        [V((KEYS, 2 * T), BF16), V((KEYS, 2 * T), BF16)],
         32,
-    )(pos, queries, key_map, phi, inner, own, *arrays)
+    )(pos, queries, key_map, phi, inner, own, *arrays, *early, *middle)
     gathered = lax.all_to_all(payload, "seq", 0, 0)
     grad_queries, near_values = call(
         query_kernel, "query_gradients", [V] * 4, [(T, rows), (T, T)]

time: 102 us -> 105 us (1.029)
  Pallas kernels: 17.7 us -> 20.6 us
  local copies, waits for them, and re-layouts: 0.08 us -> 2.06 us
    ppermute x9, waiting for transfers between devices: 11.6 us -> 8.48 us  [shift(): lax.ppermute(x, 'seq', [(i, (i + k) % pieces) for i in range(pieces)])]
    pallas_call x1 -> x3, Pallas kernels: 11.1 us -> 14 us  [the longest x1 9.03 us: on_device(): call(functools.partial(main_kernel, places, 2), 'attention_transfer', [V]...]
    all_to_all x1, waiting for transfers between devices: 15.9 us -> 18.3 us  [on_device(): gathered = lax.all_to_all(payload, 'seq', 0, 0)]
    unnamed x15 -> x17, local copies, waits for them, and re-layouts: 0.06 us -> 2.04 us
    all_to_all x1, starting transfers between devices: 11.9 us -> 10.7 us  [on_device(): squares = lax.all_to_all(squares, 'head', 0, 0)]
  transfers between devices with their start and end apart: 11 -> 11, of which waited for: 8 -> 5; matrix products, arithmetic and copies ran while one was open for 0% -> 0% of each run, Pallas kernels for 4% -> 9%
where the time goes in v8:
time: 105 us; the launch traced here: 104 us
  starting transfers between devices  33 us (31%)
  waiting for transfers between devices  28.8 us (27%)
  Pallas kernels  20.6 us (20%)
  blocking collectives  18.1 us (17%)
  local copies, waits for them, and re-layouts  2.06 us (2%)
    ppermute x9, starting transfers between devices, shift(): lax.ppermute(x, 'seq', [(i, (i + k) % pieces) for i in range(pieces)])  18.3 us
    all_to_all x1, waiting for transfers between devices, on_device(): gathered = lax.all_to_all(payload, 'seq', 0, 0)  18.3 us
    all_to_all x1, blocking collectives, on_device(): back = lax.all_to_all(reduced, 'seq', 0, 0)  18.1 us
    all_to_all x1, starting transfers between devices, on_device(): squares = lax.all_to_all(squares, 'head', 0, 0)  10.7 us
    pallas_call x1, Pallas kernels, on_device(): call(functools.partial(main_kernel, places, 2), 'attention_transfer', [V]...  9.03 us
    ppermute x9, waiting for transfers between devices, shift(): lax.ppermute(x, 'seq', [(i, (i + k) % pieces) for i in range(pieces)])  8.48 us
    pallas_call x2, Pallas kernels, part_of(): call(functools.partial(part_kernel, places), name, [V] * (3 + len(arrays)...  4.99 us
    all_to_all x1, starting transfers between devices, on_device(): gathered = lax.all_to_all(payload, 'seq', 0, 0)  3.91 us
  transfers between devices with their start and end apart: 11, of which 5 were waited for; matrix products, arithmetic and copies ran while one was open for 0% of the time, Pallas kernels for 9%

profile of v8, /device:TPU:1, one launch (start us, length us, event | category | flops | bytes accessed | tf_op | source)
XLA Modules:
  0.0 104.2 jit_solution(3239110011847448178)
XLA Ops:
  0.6 0.0 copy-start.4
  0.6 0.0 copy-start.3
  0.7 0.8 pad_add_fusion.rest_6_
  1.5 0.0 copy-start.6
  1.5 7.8 %collective-permute-start = (bf16[256,128]{1,0:T(8,128)(2,1)S(1)}, bf16[256,128]{1,0:T(8,128)(2,1)S(1)}, u32[]{:S(2)}, u32[]{:S(2)}) collective-permute-start(bf16[256,128]{1,0:T(8,128)(2,1)S(1)} %pad_add_fusion.rest_6_), channel_id=1, source_target_pairs={{0,32},{8,40},{16,48},{24,56},{32,64},{40,72},{48,80},{56,88},{64,... | collective-permute-start | bytes 196616 | tf_op jit(solution)/shard_map/ppermute | solution.py:426
  9.3 1.2 %collective-permute-start.1 = (bf16[256,128]{1,0:T(8,128)(2,1)S(1)}, bf16[256,128]{1,0:T(8,128)(2,1)S(1)}, u32[]{:S(2)}, u32[]{:S(2)}) collective-permute-start(bf16[256,128]{1,0:T(8,128)(2,1)S(1)} %pad_add_fusion.rest_6_), channel_id=1, source_target_pairs={{0,64},{8,72},{16,80},{24,88},{32,96},{40,104},{48,112},{56,120},{... | collective-permute-start | bytes 196616 | tf_op jit(solution)/shard_map/ppermute | solution.py:426
  10.5 0.7 collective-permute-start.2
  11.2 2.9 %collective-permute-start.3 = (bf16[256,128]{1,0:T(8,128)(2,1)S(1)}, bf16[256,128]{1,0:T(8,128)(2,1)S(1)}, u32[]{:S(2)}, u32[]{:S(2)}) collective-permute-start(bf16[256,128]{1,0:T(8,128)(2,1)S(1)} %pad_add_fusion.rest_6_), channel_id=1, source_target_pairs={{0,56},{8,64},{16,72},{24,80},{32,88},{40,96},{48,104},{56,112},{6... | collective-permute-start | bytes 196616 | tf_op jit(solution)/shard_map/ppermute | solution.py:426
  14.1 0.0 copy-done.4
  14.1 0.0 copy-done.3
  14.1 0.0 copy-done.6
  14.1 0.0 copy-start
  14.1 0.9 copy-done
  15.0 0.0 copy-start.1
  15.0 1.0 copy-done.1
  16.1 1.6 %local_features.1 = (f32[1024,256]{1,0:T(8,128)S(1)}, f32[1024,128]{1,0:T(8,128)S(1)}, f32[128,256]{1,0:T(8,128)S(1)}) custom-call(s32[1,128]{1,0:T(1,128)S(1)} %bitcast.2, bf16[128,1024]{1,0:T(8,128)(2,1)S(1)} %copy-done, bf16[128,128]{1,0:T(8,128)(2,1)S(1)} %copy-done.4, f32[8,128,128]{2,1,0:T(8,128)S(1)} %copy-done.1, f32[1,128,128]{2,1,0:T(8,128)S(1)} %copy-done.3), custom_call_target="tpu_custom_call" | custom-call | tf_op jit(solution)/shard_map/local_features/pallas_call | solution.py:440
  17.7 0.0 collective-permute-done
  17.8 0.0 collective-permute-done.1
  17.8 0.0 collective-permute-done.2
  17.8 0.0 collective-permute-done.3
  17.9 0.1 collective-permute-start.5
  18.0 4.8 %collective-permute-start.6 = (bf16[512,128]{1,0:T(8,128)(2,1)S(1)}, bf16[512,128]{1,0:T(8,128)(2,1)S(1)}, u32[]{:S(2)}, u32[]{:S(2)}) collective-permute-start(bf16[512,128]{1,0:T(8,128)(2,1)S(1)} %get-tuple-element.71), channel_id=1, source_target_pairs={{0,248},{8,0},{16,8},{24,16},{32,24},{40,32},{48,40},{56,48},{64,5... | collective-permute-start | bytes 393224 | tf_op jit(solution)/shard_map/ppermute | solution.py:426
  22.7 0.1 collective-permute-start.4
  22.8 1.8 %early_keys.1 = (f32[512,256]{1,0:T(8,128)S(1)}, f32[256,256]{1,0:T(8,128)S(1)}, f32[1024,128]{1,0:T(8,128)S(1)}, f32[1024,128]{1,0:T(8,128)S(1)}, f32[1024,128]{1,0:T(8,128)S(1)}) custom-call(s32[1,128]{1,0:T(1,128)S(1)} %bitcast.3, bf16[128,1024]{1,0:T(8,128)(2,1)S(1)} %copy-done, f32[1,128,128]{2,1,0:T(8,128)S(1)} %copy-done.3, ...), custom_call_target="tpu_custom_call" | custom-call | tf_op jit(solution)/shard_map/early_keys/pallas_call | solution.py:430
  24.7 0.4 collective-permute-done.5.rest_1_.rest_2_
  25.1 0.0 collective-permute-done.6.rest_2_.rest_3_
  25.1 0.0 collective-permute-start.7
  25.1 0.8 collective-permute-start.8
  25.9 5.6 %collective-permute-done.4.rest_0_.rest_1_ = bf16[1024,128]{1,0:T(8,128)(2,1)S(1)} collective-permute-done((bf16[1024,128]{1,0:T(8,128)(2,1)S(1)}, bf16[1024,128]{1,0:T(8,128)(2,1)S(1)}, u32[]{:S(2)}, u32[]{:S(2)}) %collective-permute-start.4) | collective-permute-done | bytes 262176 | tf_op jit(solution)/shard_map/ppermute | solution.py:426
  31.5 3.2 %middle_keys.1 = (f32[1024,256]{1,0:T(8,128)S(1)}, f32[256,256]{1,0:T(8,128)S(1)}, f32[1024,128]{1,0:T(8,128)S(1)}, f32[1024,128]{1,0:T(8,128)S(1)}, f32[1024,128]{1,0:T(8,128)S(1)}) custom-call(s32[1,128]{1,0:T(1,128)S(1)} %bitcast.4, bf16[128,1024]{1,0:T(8,128)(2,1)S(1)} %copy-done, f32[1,128,128]{2,1,0:T(8,128)S(1)} %copy-done.3, ...), custom_call_target="tpu_custom_call" | custom-call | tf_op jit(solution)/shard_map/middle_keys/pallas_call | solution.py:430
  34.6 0.0 collective-permute-done.7.rest_4_
  34.7 2.4 %collective-permute-done.8.rest_5_ = bf16[512,128]{1,0:T(8,128)(2,1)S(1)} collective-permute-done((bf16[512,128]{1,0:T(8,128)(2,1)S(1)}, bf16[512,128]{1,0:T(8,128)(2,1)S(1)}, u32[]{:S(2)}, u32[]{:S(2)}) %collective-permute-start.8) | collective-permute-done | bytes 131104 | tf_op jit(solution)/shard_map/ppermute | solution.py:426
  37.1 9.0 %attention_transfer.1 = (f32[32,48,128]{2,1,0:T(8,128)}, f32[1024,128]{1,0:T(8,128)S(1)}, f32[1024,128]{1,0:T(8,128)S(1)}, f32[128,256]{1,0:T(8,128)S(1)}) custom-call(s32[1,128]{1,0:T(1,128)S(1)} %bitcast.5, bf16[128,1024]{1,0:T(8,128)(2,1)S(1)} %copy-done, f32[1,128,128]{2,1,0:T(8,128)S(1)} %copy-done.3, f32[1024,256]{1,0:T(8,128)S(1)} %get-tuple-element.38.phi_ref, ...), custom_call_target="tpu_custom_call" | custom-call | tf_op jit(solution)/shard_map/attention_transfer/pallas_call | solution.py:454
  46.1 3.9 %all-to-all-start = ((f32[32,48,128]{2,1,0:T(8,128)}), f32[32,48,128]{2,1,0:T(8,128)S(1)}, u32[]{:S(2)}, u32[]{:S(2)}) async-start(f32[32,48,128]{2,1,0:T(8,128)} %get-tuple-element.62), calls=%async_computation | async-start | bytes 1572864 | tf_op jit(solution)/shard_map/all_to_all | solution.py:462
  50.1 18.3 %all-to-all-done.got_ref = f32[32,48,128]{2,1,0:T(8,128)S(1)} async-done(((f32[32,48,128]{2,1,0:T(8,128)}), f32[32,48,128]{2,1,0:T(8,128)S(1)}, u32[]{:S(2)}, u32[]{:S(2)}) %all-to-all-start) | async-done | bytes 786464 | tf_op jit(solution)/shard_map/all_to_all | solution.py:462
  68.3 0.7 sum_pieces.1
  69.1 0.0 copy-start.2
  69.1 18.1 %all_to_all.15.got_ref.tail_ref = bf16[32,56,128]{2,1,0:T(8,128)(2,1)S(1)} all-to-all(bf16[32,56,128]{2,1,0:T(8,128)(2,1)S(1)} %get-tuple-element.63), channel_id=1, replica_groups=mesh['seq'=32,'head'=8] {'seq'}, dimensions={0} | all-to-all | bytes 917504 | tf_op jit(solution)/shard_map/all_to_all | solution.py:473
  87.2 0.7 head_squares.1
  87.9 10.7 %all-to-all-start.2 = ((f32[8,8,128]{2,1,0:T(8,128)}), f32[8,8,128]{2,1,0:T(8,128)S(1)}, u32[]{:S(2)}, u32[]{:S(2)}) async-start(f32[8,8,128]{2,1,0:T(8,128)} %head_squares.1), calls=%async_computation.2 | async-start | bytes 65536 | tf_op jit(solution)/shard_map/all_to_all | solution.py:475
  98.6 0.0 copy-done.2
  98.6 0.0 copy-start.5
  98.6 1.5 %query_gradients.1 = (f32[128,1024]{1,0:T(8,128)}, f32[128,128]{1,0:T(8,128)S(1)}) custom-call(f32[1024,128]{1,0:T(8,128)S(1)} %get-tuple-element.59.dlogit_ref, f32[1024,128]{1,0:T(8,128)S(1)} %get-tuple-element.39.inner_ref, f32[1024,128]{1,0:T(8,128)S(1)} %get-tuple-element.60.gn_ref, f32[8,128,128]{2,1,0:T(8,128)S(1)} %copy-done.2), custom_call_target="tpu_custom_call" | custom-call | tf_op jit(solution)/shard_map/query_gradients/pallas_call | solution.py:463
  100.1 0.0 copy-done.5
  100.1 1.2 %key_gradients.1 = (f32[128,128]{1,0:T(8,128)}, f32[128,128]{1,0:T(8,128)}) custom-call(s32[1,128]{1,0:T(1,128)S(1)} %bitcast.6, bf16[32,56,128]{2,1,0:T(8,128)(2,1)S(1)} %all_to_all.15.got_ref.tail_ref, f32[1,256]{1,0:T(1,128)S(1)} %get-tuple-element.64.norms_ref, bf16[128,128]{1,0:T(8,128)(2,1)S(1)} %copy-done.5, f32[1,128,128]{2,1,0:T(8,128)S(1)} %copy-done.3, ...), custom_call_target="tpu_custom_call" | custom-call | tf_op jit(solution)/shard_map/key_gradients/pallas_call | solution.py:476
  101.3 2.0 %all-to-all-done.2.squares_ref = f32[8,8,128]{2,1,0:T(8,128)S(1)} async-done(((f32[8,8,128]{2,1,0:T(8,128)}), f32[8,8,128]{2,1,0:T(8,128)S(1)}, u32[]{:S(2)}, u32[]{:S(2)}) %all-to-all-start.2) | async-done | bytes 32800 | tf_op jit(solution)/shard_map/all_to_all | solution.py:475
  103.3 0.9 clip_maps.1
  (5 shorter events, 0.1 us)
Async XLA Ops:
  0.6 13.5 %copy-start.4 = (bf16[128,128]{1,0:T(8,128)(2,1)S(1)}, bf16[128,128]{1,0:T(8,128)(2,1)}, u32[]{:S(2)}) copy-start(bf16[128,128]{1,0:T(8,128)(2,1)} %k_ref.1) | copy-start | bytes 98308
  0.6 13.5 %copy-start.3 = (f32[1,128,128]{2,1,0:T(8,128)S(1)}, f32[1,128,128]{2,1,0:T(8,128)}, u32[]{:S(2)}) copy-start(f32[1,128,128]{2,1,0:T(8,128)} %kmap_ref.9) | copy-start | bytes 196612
  1.5 12.6 %copy-start.6 = (s32[128]{0:T(128)S(1)}, s32[128]{0:T(128)}, u32[]{:S(2)}) copy-start(s32[128]{0:T(128)} %param.9) | copy-start | bytes 1540
  1.5 16.3 %collective-permute-start = (bf16[256,128]{1,0:T(8,128)(2,1)S(1)}, bf16[256,128]{1,0:T(8,128)(2,1)S(1)}, u32[]{:S(2)}, u32[]{:S(2)}) collective-permute-start(bf16[256,128]{1,0:T(8,128)(2,1)S(1)} %pad_add_fusion.rest_6_), channel_id=1, source_target_pairs={{0,32},{8,40},{16,48},{24,56},{32,64},{40,72},{48,80},{56,88},{64,... | collective-permute-start | bytes 196616 | tf_op jit(solution)/shard_map/ppermute | solution.py:426
  9.3 8.5 %collective-permute-start.1 = (bf16[256,128]{1,0:T(8,128)(2,1)S(1)}, bf16[256,128]{1,0:T(8,128)(2,1)S(1)}, u32[]{:S(2)}, u32[]{:S(2)}) collective-permute-start(bf16[256,128]{1,0:T(8,128)(2,1)S(1)} %pad_add_fusion.rest_6_), channel_id=1, source_target_pairs={{0,64},{8,72},{16,80},{24,88},{32,96},{40,104},{48,112},{56,120},{... | collective-permute-start | bytes 196616 | tf_op jit(solution)/shard_map/ppermute | solution.py:426
  10.5 7.3 %collective-permute-start.2 = (bf16[256,128]{1,0:T(8,128)(2,1)S(1)}, bf16[256,128]{1,0:T(8,128)(2,1)S(1)}, u32[]{:S(2)}, u32[]{:S(2)}) collective-permute-start(bf16[256,128]{1,0:T(8,128)(2,1)S(1)} %pad_add_fusion.rest_6_), channel_id=1, source_target_pairs={{0,8},{8,16},{16,24},{24,32},{32,40},{40,48},{48,56},{56,64},{64,7... | collective-permute-start | bytes 196616 | tf_op jit(solution)/shard_map/ppermute | solution.py:426
  11.2 6.6 %collective-permute-start.3 = (bf16[256,128]{1,0:T(8,128)(2,1)S(1)}, bf16[256,128]{1,0:T(8,128)(2,1)S(1)}, u32[]{:S(2)}, u32[]{:S(2)}) collective-permute-start(bf16[256,128]{1,0:T(8,128)(2,1)S(1)} %pad_add_fusion.rest_6_), channel_id=1, source_target_pairs={{0,56},{8,64},{16,72},{24,80},{32,88},{40,96},{48,104},{56,112},{6... | collective-permute-start | bytes 196616 | tf_op jit(solution)/shard_map/ppermute | solution.py:426
  14.1 1.0 copy-start
  15.0 1.0 copy-start.1
  17.9 7.2 %collective-permute-start.5 = (bf16[512,128]{1,0:T(8,128)(2,1)S(1)}, bf16[512,128]{1,0:T(8,128)(2,1)S(1)}, u32[]{:S(2)}, u32[]{:S(2)}) collective-permute-start(bf16[512,128]{1,0:T(8,128)(2,1)S(1)} %get-tuple-element.72), channel_id=1, source_target_pairs={{0,8},{8,16},{16,24},{24,32},{32,40},{40,48},{48,56},{56,64},{64,7... | collective-permute-start | bytes 393224 | tf_op jit(solution)/shard_map/ppermute | solution.py:426
  18.0 7.1 %collective-permute-start.6 = (bf16[512,128]{1,0:T(8,128)(2,1)S(1)}, bf16[512,128]{1,0:T(8,128)(2,1)S(1)}, u32[]{:S(2)}, u32[]{:S(2)}) collective-permute-start(bf16[512,128]{1,0:T(8,128)(2,1)S(1)} %get-tuple-element.71), channel_id=1, source_target_pairs={{0,248},{8,0},{16,8},{24,16},{32,24},{40,32},{48,40},{56,48},{64,5... | collective-permute-start | bytes 393224 | tf_op jit(solution)/shard_map/ppermute | solution.py:426
  22.7 8.8 %collective-permute-start.4 = (bf16[1024,128]{1,0:T(8,128)(2,1)S(1)}, bf16[1024,128]{1,0:T(8,128)(2,1)S(1)}, u32[]{:S(2)}, u32[]{:S(2)}) collective-permute-start(bf16[1024,128]{1,0:T(8,128)(2,1)S(1)} %constant_dynamic-update-slice_fusion.rest_0_), channel_id=1, source_target_pairs={{0,64},{8,72},{16,80},{24,88},{32,96},{40,104},{48,112},{56,120},{... | collective-permute-start | bytes 786440 | tf_op jit(solution)/shard_map/ppermute | solution.py:426
  25.1 9.6 %collective-permute-start.7 = (bf16[512,128]{1,0:T(8,128)(2,1)S(1)}, bf16[512,128]{1,0:T(8,128)(2,1)S(1)}, u32[]{:S(2)}, u32[]{:S(2)}) collective-permute-start(bf16[512,128]{1,0:T(8,128)(2,1)S(1)} %collective-permute-done.5.rest_1_.rest_2_), channel_id=1, source_target_pairs={{0,64},{8,72},{16,80},{24,88},{32,96},{40,104},{48,112},{56,120},{... | collective-permute-start | bytes 393224 | tf_op jit(solution)/shard_map/ppermute | solution.py:426
  25.1 12.0 %collective-permute-start.8 = (bf16[512,128]{1,0:T(8,128)(2,1)S(1)}, bf16[512,128]{1,0:T(8,128)(2,1)S(1)}, u32[]{:S(2)}, u32[]{:S(2)}) collective-permute-start(bf16[512,128]{1,0:T(8,128)(2,1)S(1)} %collective-permute-done.6.rest_2_.rest_3_), channel_id=1, source_target_pairs={{0,64},{8,72},{16,80},{24,88},{32,96},{40,104},{48,112},{56,120},{... | collective-permute-start | bytes 393224 | tf_op jit(solution)/shard_map/ppermute | solution.py:426
  46.1 22.2 %all-to-all-start = ((f32[32,48,128]{2,1,0:T(8,128)}), f32[32,48,128]{2,1,0:T(8,128)S(1)}, u32[]{:S(2)}, u32[]{:S(2)}) async-start(f32[32,48,128]{2,1,0:T(8,128)} %get-tuple-element.62), calls=%async_computation | async-start | bytes 1572864 | tf_op jit(solution)/shard_map/all_to_all | solution.py:462
  69.1 29.5 %copy-start.2 = (f32[8,128,128]{2,1,0:T(8,128)S(1)}, f32[8,128,128]{2,1,0:T(8,128)}, u32[]{:S(2)}) copy-start(f32[8,128,128]{2,1,0:T(8,128)} %qmap_ref.3) | copy-start | bytes 1572868
  87.9 15.5 %all-to-all-start.2 = ((f32[8,8,128]{2,1,0:T(8,128)}), f32[8,8,128]{2,1,0:T(8,128)S(1)}, u32[]{:S(2)}, u32[]{:S(2)}) async-start(f32[8,8,128]{2,1,0:T(8,128)} %head_squares.1), calls=%async_computation.2 | async-start | bytes 65536 | tf_op jit(solution)/shard_map/all_to_all | solution.py:475
  98.6 1.5 %copy-start.5 = (bf16[128,128]{1,0:T(8,128)(2,1)S(1)}, bf16[128,128]{1,0:T(8,128)(2,1)}, u32[]{:S(2)}) copy-start(bf16[128,128]{1,0:T(8,128)(2,1)} %v_ref.1) | copy-start | bytes 98308

commit v9 on v8

--- a/solution.py
+++ b/solution.py
@@ -442,11 +442,12 @@
     )(pos, queries, key_vectors, query_map, key_map)
     b4, b8, b1, b7, own = lax.optimization_barrier((b4, b8, b1, b7, own))
     near = jnp.concatenate([b4, b8, b1, b7], axis=0)
+    near, b4, b1, b7 = lax.optimization_barrier((near, b4, b1, b7))
+    far = shift(near, 8)
     n1 = shift(jnp.concatenate([b1, b4], axis=0), 1)
     n2 = shift(jnp.concatenate([b4, b7], axis=0), -1)
-    far = shift(near, 8)
     early = list(part_of("early_keys", [near], [(4, 8, 1, 7)]))
-    n1, n2, early[1] = lax.optimization_barrier((n1, n2, early[1]))
+    n1, n2, far, early[1] = lax.optimization_barrier((n1, n2, far, early[1]))
     f1, f2 = shift(n1, 8), shift(n2, 8)
     middle = part_of("middle_keys", [far, n1, n2], [(12, 16, 9, 15), (2, 5), (3, 6)])
     arrays = [near, far, n1, n2, f1, f2, kv]

time: 105 us -> 99.7 us (0.950)
  waiting for transfers between devices: 28.8 us -> 21.7 us
  starting transfers between devices: 33 us -> 35.5 us
    ppermute x9, waiting for transfers between devices: 8.48 us -> 3.78 us  [shift(): lax.ppermute(x, 'seq', [(i, (i + k) % pieces) for i in range(pieces)])]
    all_to_all x1, waiting for transfers between devices: 18.3 us -> 15.9 us  [on_device(): gathered = lax.all_to_all(payload, 'seq', 0, 0)]
    all_to_all x1, starting transfers between devices: 3.91 us -> 4.98 us  [on_device(): gathered = lax.all_to_all(payload, 'seq', 0, 0)]
where the time goes in v9:
time: 99.7 us; the launch traced here: 99.2 us
  starting transfers between devices  35.5 us (36%)
  waiting for transfers between devices  21.7 us (22%)
  Pallas kernels  20.6 us (21%)
  blocking collectives  17.8 us (18%)
  local copies, waits for them, and re-layouts  2.01 us (2%)
    ppermute x9, starting transfers between devices, shift(): lax.ppermute(x, 'seq', [(i, (i + k) % pieces) for i in range(pieces)])  18.7 us
    all_to_all x1, blocking collectives, on_device(): back = lax.all_to_all(reduced, 'seq', 0, 0)  17.8 us
    all_to_all x1, waiting for transfers between devices, on_device(): gathered = lax.all_to_all(payload, 'seq', 0, 0)  15.9 us
    all_to_all x1, starting transfers between devices, on_device(): squares = lax.all_to_all(squares, 'head', 0, 0)  11.7 us
    pallas_call x1, Pallas kernels, on_device(): call(functools.partial(main_kernel, places, 2), 'attention_transfer', [V]...  9.03 us
    pallas_call x2, Pallas kernels, part_of(): call(functools.partial(part_kernel, places), name, [V] * (3 + len(arrays)...  4.99 us
    all_to_all x1, starting transfers between devices, on_device(): gathered = lax.all_to_all(payload, 'seq', 0, 0)  4.98 us
    ppermute x9, waiting for transfers between devices, shift(): lax.ppermute(x, 'seq', [(i, (i + k) % pieces) for i in range(pieces)])  3.78 us
  transfers between devices with their start and end apart: 11, of which 5 were waited for; matrix products, arithmetic and copies ran while one was open for 0% of the time, Pallas kernels for 9%

profile of v9, /device:TPU:1, one launch (start us, length us, event | category | flops | bytes accessed | tf_op | source)
XLA Modules:
  0.0 99.2 jit_solution(4895795366414527556)
XLA Ops:
  0.6 0.0 copy-start.4
  0.6 0.0 copy-start.3
  0.7 0.8 pad_add_fusion.rest_6_
  1.5 0.0 copy-start.6
  1.5 7.8 %collective-permute-start = (bf16[256,128]{1,0:T(8,128)(2,1)S(1)}, bf16[256,128]{1,0:T(8,128)(2,1)S(1)}, u32[]{:S(2)}, u32[]{:S(2)}) collective-permute-start(bf16[256,128]{1,0:T(8,128)(2,1)S(1)} %pad_add_fusion.rest_6_), channel_id=1, source_target_pairs={{0,32},{8,40},{16,48},{24,56},{32,64},{40,72},{48,80},{56,88},{64,... | collective-permute-start | bytes 196616 | tf_op jit(solution)/shard_map/ppermute | solution.py:426
  9.3 1.2 %collective-permute-start.1 = (bf16[256,128]{1,0:T(8,128)(2,1)S(1)}, bf16[256,128]{1,0:T(8,128)(2,1)S(1)}, u32[]{:S(2)}, u32[]{:S(2)}) collective-permute-start(bf16[256,128]{1,0:T(8,128)(2,1)S(1)} %pad_add_fusion.rest_6_), channel_id=1, source_target_pairs={{0,64},{8,72},{16,80},{24,88},{32,96},{40,104},{48,112},{56,120},{... | collective-permute-start | bytes 196616 | tf_op jit(solution)/shard_map/ppermute | solution.py:426
  10.5 0.7 collective-permute-start.2
  11.2 2.9 %collective-permute-start.3 = (bf16[256,128]{1,0:T(8,128)(2,1)S(1)}, bf16[256,128]{1,0:T(8,128)(2,1)S(1)}, u32[]{:S(2)}, u32[]{:S(2)}) collective-permute-start(bf16[256,128]{1,0:T(8,128)(2,1)S(1)} %pad_add_fusion.rest_6_), channel_id=1, source_target_pairs={{0,56},{8,64},{16,72},{24,80},{32,88},{40,96},{48,104},{56,112},{6... | collective-permute-start | bytes 196616 | tf_op jit(solution)/shard_map/ppermute | solution.py:426
  14.1 0.0 copy-done.4
  14.1 0.0 copy-done.3
  14.1 0.0 copy-done.6
  14.1 0.0 copy-start
  14.1 0.9 copy-done
  15.0 0.0 copy-start.1
  15.0 1.0 %copy-done.1 = f32[8,128,128]{2,1,0:T(8,128)S(1)} copy-done((f32[8,128,128]{2,1,0:T(8,128)S(1)}, f32[8,128,128]{2,1,0:T(8,128)}, u32[]{:S(2)}) %copy-start.1) | copy-done | bytes 524312
  16.1 1.6 %local_features.1 = (f32[1024,256]{1,0:T(8,128)S(1)}, f32[1024,128]{1,0:T(8,128)S(1)}, f32[128,256]{1,0:T(8,128)S(1)}) custom-call(s32[1,128]{1,0:T(1,128)S(1)} %bitcast.2, bf16[128,1024]{1,0:T(8,128)(2,1)S(1)} %copy-done, bf16[128,128]{1,0:T(8,128)(2,1)S(1)} %copy-done.4, f32[8,128,128]{2,1,0:T(8,128)S(1)} %copy-done.1, f32[1,128,128]{2,1,0:T(8,128)S(1)} %copy-done.3), custom_call_target="tpu_custom_call" | custom-call | tf_op jit(solution)/shard_map/local_features/pallas_call | solution.py:440
  17.7 0.0 collective-permute-done
  17.8 0.0 collective-permute-done.1
  17.8 0.0 collective-permute-done.2
  17.8 0.0 collective-permute-done.3
  17.8 1.0 %collective-permute-start.6 = (bf16[1024,128]{1,0:T(8,128)(2,1)S(1)}, bf16[1024,128]{1,0:T(8,128)(2,1)S(1)}, u32[]{:S(2)}, u32[]{:S(2)}) collective-permute-start(bf16[1024,128]{1,0:T(8,128)(2,1)S(1)} %pad_maximum_fusion.rest_0_), channel_id=1, source_target_pairs={{0,64},{8,72},{16,80},{24,88},{32,96},{40,104},{48,112},{56,120},{... | collective-permute-start | bytes 786440 | tf_op jit(solution)/shard_map/ppermute | solution.py:426
  18.8 0.1 collective-permute-start.4
  18.9 4.8 %collective-permute-start.5 = (bf16[512,128]{1,0:T(8,128)(2,1)S(1)}, bf16[512,128]{1,0:T(8,128)(2,1)S(1)}, u32[]{:S(2)}, u32[]{:S(2)}) collective-permute-start(bf16[512,128]{1,0:T(8,128)(2,1)S(1)} %get-tuple-element.81), channel_id=1, source_target_pairs={{0,248},{8,0},{16,8},{24,16},{32,24},{40,32},{48,40},{56,48},{64,5... | collective-permute-start | bytes 393224 | tf_op jit(solution)/shard_map/ppermute | solution.py:426
  23.7 1.8 %early_keys.1 = (f32[512,256]{1,0:T(8,128)S(1)}, f32[256,256]{1,0:T(8,128)S(1)}, f32[1024,128]{1,0:T(8,128)S(1)}, f32[1024,128]{1,0:T(8,128)S(1)}, f32[1024,128]{1,0:T(8,128)S(1)}) custom-call(s32[1,128]{1,0:T(1,128)S(1)} %bitcast.3, bf16[128,1024]{1,0:T(8,128)(2,1)S(1)} %copy-done, f32[1,128,128]{2,1,0:T(8,128)S(1)} %copy-done.3, ...), custom_call_target="tpu_custom_call" | custom-call | tf_op jit(solution)/shard_map/early_keys/pallas_call | solution.py:430
  25.5 0.6 collective-permute-done.4.rest_1_.rest_2_
  26.2 0.0 collective-permute-done.5.rest_2_.rest_3_
  26.2 0.0 collective-permute-done.6.rest_0_.rest_1_
  26.2 0.1 collective-permute-start.7
  26.2 0.2 collective-permute-start.8
  26.4 3.2 %middle_keys.1 = (f32[1024,256]{1,0:T(8,128)S(1)}, f32[256,256]{1,0:T(8,128)S(1)}, f32[1024,128]{1,0:T(8,128)S(1)}, f32[1024,128]{1,0:T(8,128)S(1)}, f32[1024,128]{1,0:T(8,128)S(1)}) custom-call(s32[1,128]{1,0:T(1,128)S(1)} %bitcast.4, bf16[128,1024]{1,0:T(8,128)(2,1)S(1)} %copy-done, f32[1,128,128]{2,1,0:T(8,128)S(1)} %copy-done.3, ...), custom_call_target="tpu_custom_call" | custom-call | tf_op jit(solution)/shard_map/middle_keys/pallas_call | solution.py:430
  29.6 1.7 %collective-permute-done.7.rest_4_ = bf16[512,128]{1,0:T(8,128)(2,1)S(1)} collective-permute-done((bf16[512,128]{1,0:T(8,128)(2,1)S(1)}, bf16[512,128]{1,0:T(8,128)(2,1)S(1)}, u32[]{:S(2)}, u32[]{:S(2)}) %collective-permute-start.7) | collective-permute-done | bytes 131104 | tf_op jit(solution)/shard_map/ppermute | solution.py:426
  31.3 1.4 %collective-permute-done.8.rest_5_ = bf16[512,128]{1,0:T(8,128)(2,1)S(1)} collective-permute-done((bf16[512,128]{1,0:T(8,128)(2,1)S(1)}, bf16[512,128]{1,0:T(8,128)(2,1)S(1)}, u32[]{:S(2)}, u32[]{:S(2)}) %collective-permute-start.8) | collective-permute-done | bytes 131104 | tf_op jit(solution)/shard_map/ppermute | solution.py:426
  32.7 9.0 %attention_transfer.1 = (f32[32,48,128]{2,1,0:T(8,128)}, f32[1024,128]{1,0:T(8,128)S(1)}, f32[1024,128]{1,0:T(8,128)S(1)}, f32[128,256]{1,0:T(8,128)S(1)}) custom-call(s32[1,128]{1,0:T(1,128)S(1)} %bitcast.5, bf16[128,1024]{1,0:T(8,128)(2,1)S(1)} %copy-done, f32[1,128,128]{2,1,0:T(8,128)S(1)} %copy-done.3, f32[1024,256]{1,0:T(8,128)S(1)} %get-tuple-element.43.phi_ref, ...), custom_call_target="tpu_custom_call" | custom-call | tf_op jit(solution)/shard_map/attention_transfer/pallas_call | solution.py:455
  41.8 5.0 %all-to-all-start = ((f32[32,48,128]{2,1,0:T(8,128)}), f32[32,48,128]{2,1,0:T(8,128)S(1)}, u32[]{:S(2)}, u32[]{:S(2)}) async-start(f32[32,48,128]{2,1,0:T(8,128)} %get-tuple-element.72), calls=%async_computation | async-start | bytes 1572864 | tf_op jit(solution)/shard_map/all_to_all | solution.py:463
  46.8 15.9 %all-to-all-done.got_ref = f32[32,48,128]{2,1,0:T(8,128)S(1)} async-done(((f32[32,48,128]{2,1,0:T(8,128)}), f32[32,48,128]{2,1,0:T(8,128)S(1)}, u32[]{:S(2)}, u32[]{:S(2)}) %all-to-all-start) | async-done | bytes 786464 | tf_op jit(solution)/shard_map/all_to_all | solution.py:463
  62.7 0.7 sum_pieces.1
  63.4 0.0 copy-start.2
  63.4 17.8 %all_to_all.15.got_ref.tail_ref = bf16[32,56,128]{2,1,0:T(8,128)(2,1)S(1)} all-to-all(bf16[32,56,128]{2,1,0:T(8,128)(2,1)S(1)} %get-tuple-element.73), channel_id=1, replica_groups=mesh['seq'=32,'head'=8] {'seq'}, dimensions={0} | all-to-all | bytes 917504 | tf_op jit(solution)/shard_map/all_to_all | solution.py:474
  81.2 0.7 head_squares.1
  81.9 11.7 %all-to-all-start.2 = ((f32[8,8,128]{2,1,0:T(8,128)}), f32[8,8,128]{2,1,0:T(8,128)S(1)}, u32[]{:S(2)}, u32[]{:S(2)}) async-start(f32[8,8,128]{2,1,0:T(8,128)} %head_squares.1), calls=%async_computation.2 | async-start | bytes 65536 | tf_op jit(solution)/shard_map/all_to_all | solution.py:476
  93.6 0.0 copy-done.2
  93.6 0.0 copy-start.5
  93.6 1.5 %query_gradients.1 = (f32[128,1024]{1,0:T(8,128)}, f32[128,128]{1,0:T(8,128)S(1)}) custom-call(f32[1024,128]{1,0:T(8,128)S(1)} %get-tuple-element.69.dlogit_ref, f32[1024,128]{1,0:T(8,128)S(1)} %get-tuple-element.44.inner_ref, f32[1024,128]{1,0:T(8,128)S(1)} %get-tuple-element.70.gn_ref, f32[8,128,128]{2,1,0:T(8,128)S(1)} %copy-done.2), custom_call_target="tpu_custom_call" | custom-call | tf_op jit(solution)/shard_map/query_gradients/pallas_call | solution.py:464
  95.1 0.0 copy-done.5
  95.1 1.2 %key_gradients.1 = (f32[128,128]{1,0:T(8,128)}, f32[128,128]{1,0:T(8,128)}) custom-call(s32[1,128]{1,0:T(1,128)S(1)} %bitcast.6, bf16[32,56,128]{2,1,0:T(8,128)(2,1)S(1)} %all_to_all.15.got_ref.tail_ref, f32[1,256]{1,0:T(1,128)S(1)} %get-tuple-element.74.norms_ref, bf16[128,128]{1,0:T(8,128)(2,1)S(1)} %copy-done.5, f32[1,128,128]{2,1,0:T(8,128)S(1)} %copy-done.3, ...), custom_call_target="tpu_custom_call" | custom-call | tf_op jit(solution)/shard_map/key_gradients/pallas_call | solution.py:477
  96.3 2.0 %all-to-all-done.2.squares_ref = f32[8,8,128]{2,1,0:T(8,128)S(1)} async-done(((f32[8,8,128]{2,1,0:T(8,128)}), f32[8,8,128]{2,1,0:T(8,128)S(1)}, u32[]{:S(2)}, u32[]{:S(2)}) %all-to-all-start.2) | async-done | bytes 32800 | tf_op jit(solution)/shard_map/all_to_all | solution.py:476
  98.3 0.9 clip_maps.1
  (2 shorter events, 0.0 us)
Async XLA Ops:
  0.6 13.5 %copy-start.4 = (bf16[128,128]{1,0:T(8,128)(2,1)S(1)}, bf16[128,128]{1,0:T(8,128)(2,1)}, u32[]{:S(2)}) copy-start(bf16[128,128]{1,0:T(8,128)(2,1)} %k_ref.1) | copy-start | bytes 98308
  0.6 13.5 %copy-start.3 = (f32[1,128,128]{2,1,0:T(8,128)S(1)}, f32[1,128,128]{2,1,0:T(8,128)}, u32[]{:S(2)}) copy-start(f32[1,128,128]{2,1,0:T(8,128)} %kmap_ref.9) | copy-start | bytes 196612
  1.5 12.6 %copy-start.6 = (s32[128]{0:T(128)S(1)}, s32[128]{0:T(128)}, u32[]{:S(2)}) copy-start(s32[128]{0:T(128)} %param.9) | copy-start | bytes 1540
  1.5 16.3 %collective-permute-start = (bf16[256,128]{1,0:T(8,128)(2,1)S(1)}, bf16[256,128]{1,0:T(8,128)(2,1)S(1)}, u32[]{:S(2)}, u32[]{:S(2)}) collective-permute-start(bf16[256,128]{1,0:T(8,128)(2,1)S(1)} %pad_add_fusion.rest_6_), channel_id=1, source_target_pairs={{0,32},{8,40},{16,48},{24,56},{32,64},{40,72},{48,80},{56,88},{64,... | collective-permute-start | bytes 196616 | tf_op jit(solution)/shard_map/ppermute | solution.py:426
  9.3 8.5 %collective-permute-start.1 = (bf16[256,128]{1,0:T(8,128)(2,1)S(1)}, bf16[256,128]{1,0:T(8,128)(2,1)S(1)}, u32[]{:S(2)}, u32[]{:S(2)}) collective-permute-start(bf16[256,128]{1,0:T(8,128)(2,1)S(1)} %pad_add_fusion.rest_6_), channel_id=1, source_target_pairs={{0,64},{8,72},{16,80},{24,88},{32,96},{40,104},{48,112},{56,120},{... | collective-permute-start | bytes 196616 | tf_op jit(solution)/shard_map/ppermute | solution.py:426
  10.5 7.3 %collective-permute-start.2 = (bf16[256,128]{1,0:T(8,128)(2,1)S(1)}, bf16[256,128]{1,0:T(8,128)(2,1)S(1)}, u32[]{:S(2)}, u32[]{:S(2)}) collective-permute-start(bf16[256,128]{1,0:T(8,128)(2,1)S(1)} %pad_add_fusion.rest_6_), channel_id=1, source_target_pairs={{0,8},{8,16},{16,24},{24,32},{32,40},{40,48},{48,56},{56,64},{64,7... | collective-permute-start | bytes 196616 | tf_op jit(solution)/shard_map/ppermute | solution.py:426
  11.2 6.6 %collective-permute-start.3 = (bf16[256,128]{1,0:T(8,128)(2,1)S(1)}, bf16[256,128]{1,0:T(8,128)(2,1)S(1)}, u32[]{:S(2)}, u32[]{:S(2)}) collective-permute-start(bf16[256,128]{1,0:T(8,128)(2,1)S(1)} %pad_add_fusion.rest_6_), channel_id=1, source_target_pairs={{0,56},{8,64},{16,72},{24,80},{32,88},{40,96},{48,104},{56,112},{6... | collective-permute-start | bytes 196616 | tf_op jit(solution)/shard_map/ppermute | solution.py:426
  14.1 1.0 copy-start
  15.0 1.0 %copy-start.1 = (f32[8,128,128]{2,1,0:T(8,128)S(1)}, f32[8,128,128]{2,1,0:T(8,128)}, u32[]{:S(2)}) copy-start(f32[8,128,128]{2,1,0:T(8,128)} %qmap_ref.3) | copy-start | bytes 1572868
  17.8 8.3 %collective-permute-start.6 = (bf16[1024,128]{1,0:T(8,128)(2,1)S(1)}, bf16[1024,128]{1,0:T(8,128)(2,1)S(1)}, u32[]{:S(2)}, u32[]{:S(2)}) collective-permute-start(bf16[1024,128]{1,0:T(8,128)(2,1)S(1)} %pad_maximum_fusion.rest_0_), channel_id=1, source_target_pairs={{0,64},{8,72},{16,80},{24,88},{32,96},{40,104},{48,112},{56,120},{... | collective-permute-start | bytes 786440 | tf_op jit(solution)/shard_map/ppermute | solution.py:426
  18.8 7.3 %collective-permute-start.4 = (bf16[512,128]{1,0:T(8,128)(2,1)S(1)}, bf16[512,128]{1,0:T(8,128)(2,1)S(1)}, u32[]{:S(2)}, u32[]{:S(2)}) collective-permute-start(bf16[512,128]{1,0:T(8,128)(2,1)S(1)} %get-tuple-element.82), channel_id=1, source_target_pairs={{0,8},{8,16},{16,24},{24,32},{32,40},{40,48},{48,56},{56,64},{64,7... | collective-permute-start | bytes 393224 | tf_op jit(solution)/shard_map/ppermute | solution.py:426
  18.9 7.2 %collective-permute-start.5 = (bf16[512,128]{1,0:T(8,128)(2,1)S(1)}, bf16[512,128]{1,0:T(8,128)(2,1)S(1)}, u32[]{:S(2)}, u32[]{:S(2)}) collective-permute-start(bf16[512,128]{1,0:T(8,128)(2,1)S(1)} %get-tuple-element.81), channel_id=1, source_target_pairs={{0,248},{8,0},{16,8},{24,16},{32,24},{40,32},{48,40},{56,48},{64,5... | collective-permute-start | bytes 393224 | tf_op jit(solution)/shard_map/ppermute | solution.py:426
  26.2 5.2 %collective-permute-start.7 = (bf16[512,128]{1,0:T(8,128)(2,1)S(1)}, bf16[512,128]{1,0:T(8,128)(2,1)S(1)}, u32[]{:S(2)}, u32[]{:S(2)}) collective-permute-start(bf16[512,128]{1,0:T(8,128)(2,1)S(1)} %collective-permute-done.4.rest_1_.rest_2_), channel_id=1, source_target_pairs={{0,64},{8,72},{16,80},{24,88},{32,96},{40,104},{48,112},{56,120},{... | collective-permute-start | bytes 393224 | tf_op jit(solution)/shard_map/ppermute | solution.py:426
  26.2 6.5 %collective-permute-start.8 = (bf16[512,128]{1,0:T(8,128)(2,1)S(1)}, bf16[512,128]{1,0:T(8,128)(2,1)S(1)}, u32[]{:S(2)}, u32[]{:S(2)}) collective-permute-start(bf16[512,128]{1,0:T(8,128)(2,1)S(1)} %collective-permute-done.5.rest_2_.rest_3_), channel_id=1, source_target_pairs={{0,64},{8,72},{16,80},{24,88},{32,96},{40,104},{48,112},{56,120},{... | collective-permute-start | bytes 393224 | tf_op jit(solution)/shard_map/ppermute | solution.py:426
  41.8 20.9 %all-to-all-start = ((f32[32,48,128]{2,1,0:T(8,128)}), f32[32,48,128]{2,1,0:T(8,128)S(1)}, u32[]{:S(2)}, u32[]{:S(2)}) async-start(f32[32,48,128]{2,1,0:T(8,128)} %get-tuple-element.72), calls=%async_computation | async-start | bytes 1572864 | tf_op jit(solution)/shard_map/all_to_all | solution.py:463
  63.4 30.2 %copy-start.2 = (f32[8,128,128]{2,1,0:T(8,128)S(1)}, f32[8,128,128]{2,1,0:T(8,128)}, u32[]{:S(2)}) copy-start(f32[8,128,128]{2,1,0:T(8,128)} %qmap_ref.3) | copy-start | bytes 1572868
  81.9 16.5 %all-to-all-start.2 = ((f32[8,8,128]{2,1,0:T(8,128)}), f32[8,8,128]{2,1,0:T(8,128)S(1)}, u32[]{:S(2)}, u32[]{:S(2)}) async-start(f32[8,8,128]{2,1,0:T(8,128)} %head_squares.1), calls=%async_computation.2 | async-start | bytes 65536 | tf_op jit(solution)/shard_map/all_to_all | solution.py:476
  93.6 1.5 %copy-start.5 = (bf16[128,128]{1,0:T(8,128)(2,1)S(1)}, bf16[128,128]{1,0:T(8,128)(2,1)}, u32[]{:S(2)}) copy-start(bf16[128,128]{1,0:T(8,128)(2,1)} %v_ref.1) | copy-start | bytes 98308

commit v10 on v9

--- a/solution.py
+++ b/solution.py
@@ -440,7 +440,6 @@
     phi, inner, own = call(
         local_kernel, "local_features", [V] * 5, [(rows, 2 * T), (rows, T), (T, 2 * T)]
     )(pos, queries, key_vectors, query_map, key_map)
-    b4, b8, b1, b7, own = lax.optimization_barrier((b4, b8, b1, b7, own))
     near = jnp.concatenate([b4, b8, b1, b7], axis=0)
     near, b4, b1, b7 = lax.optimization_barrier((near, b4, b1, b7))
     far = shift(near, 8)

time: 99.7 us -> 106 us (1.063)
  waiting for transfers between devices: 21.7 us -> 32.9 us
  starting transfers between devices: 35.5 us -> 32.3 us
  local copies, waits for them, and re-layouts: 2.01 us -> 0.03 us
    ppermute x9, waiting for transfers between devices: 3.78 us -> 12.9 us  [shift(): lax.ppermute(x, 'seq', [(i, (i + k) % pieces) for i in range(pieces)])]
    all_to_all x1, waiting for transfers between devices: 15.9 us -> 18 us  [on_device(): gathered = lax.all_to_all(payload, 'seq', 0, 0)]
    unnamed x14 -> x12, local copies, waits for them, and re-layouts: 2.01 us -> 0.03 us
    ppermute x9, starting transfers between devices: 18.7 us -> 17.5 us  [shift(): lax.ppermute(x, 'seq', [(i, (i + k) % pieces) for i in range(pieces)])]
  transfers between devices with their start and end apart: 11 -> 11, of which waited for: 5 -> 9; matrix products, arithmetic and copies ran while one was open for 0% -> 0% of each run, Pallas kernels for 9% -> 9%
where the time goes in v10:
time: 106 us; the launch traced here: 105 us
  waiting for transfers between devices  32.9 us (31%)
  starting transfers between devices  32.3 us (30%)
  Pallas kernels  20.6 us (19%)
  blocking collectives  18 us (17%)
    all_to_all x1, blocking collectives, on_device(): back = lax.all_to_all(reduced, 'seq', 0, 0)  18 us
    all_to_all x1, waiting for transfers between devices, on_device(): gathered = lax.all_to_all(payload, 'seq', 0, 0)  18 us
    ppermute x9, starting transfers between devices, shift(): lax.ppermute(x, 'seq', [(i, (i + k) % pieces) for i in range(pieces)])  17.5 us
    ppermute x9, waiting for transfers between devices, shift(): lax.ppermute(x, 'seq', [(i, (i + k) % pieces) for i in range(pieces)])  12.9 us
    all_to_all x1, starting transfers between devices, on_device(): squares = lax.all_to_all(squares, 'head', 0, 0)  10.7 us
    pallas_call x1, Pallas kernels, on_device(): call(functools.partial(main_kernel, places, 2), 'attention_transfer', [V]...  9.02 us
    pallas_call x2, Pallas kernels, part_of(): call(functools.partial(part_kernel, places), name, [V] * (3 + len(arrays)...  4.99 us
    all_to_all x1, starting transfers between devices, on_device(): gathered = lax.all_to_all(payload, 'seq', 0, 0)  4.13 us
  transfers between devices with their start and end apart: 11, of which 9 were waited for; matrix products, arithmetic and copies ran while one was open for 0% of the time, Pallas kernels for 9%

profile of v10, /device:TPU:1, one launch (start us, length us, event | category | flops | bytes accessed | tf_op | source)
XLA Modules:
  0.0 105.5 jit_solution(18277171261440231943)
XLA Ops:
  0.6 0.8 pad_add_fusion.rest_6_
  1.4 7.7 %collective-permute-start = (bf16[256,128]{1,0:T(8,128)(2,1)S(1)}, bf16[256,128]{1,0:T(8,128)(2,1)S(1)}, u32[]{:S(2)}, u32[]{:S(2)}) collective-permute-start(bf16[256,128]{1,0:T(8,128)(2,1)S(1)} %pad_add_fusion.rest_6_), channel_id=1, source_target_pairs={{0,32},{8,40},{16,48},{24,56},{32,64},{40,72},{48,80},{56,88},{64,... | collective-permute-start | bytes 196616 | tf_op jit(solution)/shard_map/ppermute | solution.py:426
  9.2 0.7 collective-permute-start.2
  9.9 2.9 %collective-permute-start.3 = (bf16[256,128]{1,0:T(8,128)(2,1)S(1)}, bf16[256,128]{1,0:T(8,128)(2,1)S(1)}, u32[]{:S(2)}, u32[]{:S(2)}) collective-permute-start(bf16[256,128]{1,0:T(8,128)(2,1)S(1)} %pad_add_fusion.rest_6_), channel_id=1, source_target_pairs={{0,56},{8,64},{16,72},{24,80},{32,88},{40,96},{48,104},{56,112},{6... | collective-permute-start | bytes 196616 | tf_op jit(solution)/shard_map/ppermute | solution.py:426
  12.8 1.2 %collective-permute-start.1 = (bf16[256,128]{1,0:T(8,128)(2,1)S(1)}, bf16[256,128]{1,0:T(8,128)(2,1)S(1)}, u32[]{:S(2)}, u32[]{:S(2)}) collective-permute-start(bf16[256,128]{1,0:T(8,128)(2,1)S(1)} %pad_add_fusion.rest_6_), channel_id=1, source_target_pairs={{0,64},{8,72},{16,80},{24,88},{32,96},{40,104},{48,112},{56,120},{... | collective-permute-start | bytes 196616 | tf_op jit(solution)/shard_map/ppermute | solution.py:426
  14.0 0.0 collective-permute-done
  14.0 1.7 %collective-permute-done.2 = bf16[256,128]{1,0:T(8,128)(2,1)S(1)} collective-permute-done((bf16[256,128]{1,0:T(8,128)(2,1)S(1)}, bf16[256,128]{1,0:T(8,128)(2,1)S(1)}, u32[]{:S(2)}, u32[]{:S(2)}) %collective-permute-start.2) | collective-permute-done | bytes 65568 | tf_op jit(solution)/shard_map/ppermute | solution.py:426
  15.6 2.1 %collective-permute-done.3 = bf16[256,128]{1,0:T(8,128)(2,1)S(1)} collective-permute-done((bf16[256,128]{1,0:T(8,128)(2,1)S(1)}, bf16[256,128]{1,0:T(8,128)(2,1)S(1)}, u32[]{:S(2)}, u32[]{:S(2)}) %collective-permute-start.3) | collective-permute-done | bytes 65568 | tf_op jit(solution)/shard_map/ppermute | solution.py:426
  17.8 1.9 %collective-permute-done.1 = bf16[256,128]{1,0:T(8,128)(2,1)S(1)} collective-permute-done((bf16[256,128]{1,0:T(8,128)(2,1)S(1)}, bf16[256,128]{1,0:T(8,128)(2,1)S(1)}, u32[]{:S(2)}, u32[]{:S(2)}) %collective-permute-start.1) | collective-permute-done | bytes 65568 | tf_op jit(solution)/shard_map/ppermute | solution.py:426
  19.6 0.0 copy-start.2
  19.6 0.0 copy-start.5
  19.7 0.0 copy-start
  19.7 0.0 copy-start.1
  19.7 0.1 collective-permute-start.6
  19.8 0.1 collective-permute-start.4
  19.9 4.8 %collective-permute-start.5 = (bf16[512,128]{1,0:T(8,128)(2,1)S(1)}, bf16[512,128]{1,0:T(8,128)(2,1)S(1)}, u32[]{:S(2)}, u32[]{:S(2)}) collective-permute-start(bf16[512,128]{1,0:T(8,128)(2,1)S(1)} %get-tuple-element.71), channel_id=1, source_target_pairs={{0,248},{8,0},{16,8},{24,16},{32,24},{40,32},{48,40},{56,48},{64,5... | collective-permute-start | bytes 393224 | tf_op jit(solution)/shard_map/ppermute | solution.py:426
  24.7 0.0 copy-done.2
  24.7 0.0 copy-done.5
  24.7 0.0 copy-done
  24.7 0.0 copy-start.3
  24.7 1.8 %early_keys.1 = (f32[512,256]{1,0:T(8,128)S(1)}, f32[256,256]{1,0:T(8,128)S(1)}, f32[1024,128]{1,0:T(8,128)S(1)}, f32[1024,128]{1,0:T(8,128)S(1)}, f32[1024,128]{1,0:T(8,128)S(1)}) custom-call(s32[1,128]{1,0:T(1,128)S(1)} %bitcast.2, bf16[128,1024]{1,0:T(8,128)(2,1)S(1)} %copy-done, f32[1,128,128]{2,1,0:T(8,128)S(1)} %copy-done.2, ...), custom_call_target="tpu_custom_call" | custom-call | tf_op jit(solution)/shard_map/early_keys/pallas_call | solution.py:430
  26.5 1.1 %collective-permute-done.4.rest_1_.rest_2_ = bf16[512,128]{1,0:T(8,128)(2,1)S(1)} collective-permute-done((bf16[512,128]{1,0:T(8,128)(2,1)S(1)}, bf16[512,128]{1,0:T(8,128)(2,1)S(1)}, u32[]{:S(2)}, u32[]{:S(2)}) %collective-permute-start.4) | collective-permute-done | bytes 131104 | tf_op jit(solution)/shard_map/ppermute | solution.py:426
  27.6 0.0 collective-permute-done.5.rest_2_.rest_3_
  27.6 3.4 %collective-permute-done.6.rest_0_.rest_1_ = bf16[1024,128]{1,0:T(8,128)(2,1)S(1)} collective-permute-done((bf16[1024,128]{1,0:T(8,128)(2,1)S(1)}, bf16[1024,128]{1,0:T(8,128)(2,1)S(1)}, u32[]{:S(2)}, u32[]{:S(2)}) %collective-permute-start.6) | collective-permute-done | bytes 262176 | tf_op jit(solution)/shard_map/ppermute | solution.py:426
  31.0 0.0 collective-permute-start.7
  31.0 0.0 collective-permute-start.8
  31.0 0.0 copy-done.1
  31.0 0.0 copy-done.3
  31.1 1.6 %local_features.1 = (f32[1024,256]{1,0:T(8,128)S(1)}, f32[1024,128]{1,0:T(8,128)S(1)}, f32[128,256]{1,0:T(8,128)S(1)}) custom-call(s32[1,128]{1,0:T(1,128)S(1)} %bitcast.3, bf16[128,1024]{1,0:T(8,128)(2,1)S(1)} %copy-done, bf16[128,128]{1,0:T(8,128)(2,1)S(1)} %copy-done.3, f32[8,128,128]{2,1,0:T(8,128)S(1)} %copy-done.1, f32[1,128,128]{2,1,0:T(8,128)S(1)} %copy-done.2), custom_call_target="tpu_custom_call" | custom-call | tf_op jit(solution)/shard_map/local_features/pallas_call | solution.py:440
  32.7 3.2 %middle_keys.1 = (f32[1024,256]{1,0:T(8,128)S(1)}, f32[256,256]{1,0:T(8,128)S(1)}, f32[1024,128]{1,0:T(8,128)S(1)}, f32[1024,128]{1,0:T(8,128)S(1)}, f32[1024,128]{1,0:T(8,128)S(1)}) custom-call(s32[1,128]{1,0:T(1,128)S(1)} %bitcast.4, bf16[128,1024]{1,0:T(8,128)(2,1)S(1)} %copy-done, f32[1,128,128]{2,1,0:T(8,128)S(1)} %copy-done.2, ...), custom_call_target="tpu_custom_call" | custom-call | tf_op jit(solution)/shard_map/middle_keys/pallas_call | solution.py:430
  35.9 0.2 collective-permute-done.7.rest_4_
  36.1 2.5 %collective-permute-done.8.rest_5_ = bf16[512,128]{1,0:T(8,128)(2,1)S(1)} collective-permute-done((bf16[512,128]{1,0:T(8,128)(2,1)S(1)}, bf16[512,128]{1,0:T(8,128)(2,1)S(1)}, u32[]{:S(2)}, u32[]{:S(2)}) %collective-permute-start.8) | collective-permute-done | bytes 131104 | tf_op jit(solution)/shard_map/ppermute | solution.py:426
  38.6 9.0 %attention_transfer.1 = (f32[32,48,128]{2,1,0:T(8,128)}, f32[1024,128]{1,0:T(8,128)S(1)}, f32[1024,128]{1,0:T(8,128)S(1)}, f32[128,256]{1,0:T(8,128)S(1)}) custom-call(s32[1,128]{1,0:T(1,128)S(1)} %bitcast.5, bf16[128,1024]{1,0:T(8,128)(2,1)S(1)} %copy-done, f32[1,128,128]{2,1,0:T(8,128)S(1)} %copy-done.2, f32[1024,256]{1,0:T(8,128)S(1)} %get-tuple-element.38.phi_ref, ...), custom_call_target="tpu_custom_call" | custom-call | tf_op jit(solution)/shard_map/attention_transfer/pallas_call | solution.py:454
  47.6 4.1 %all-to-all-start = ((f32[32,48,128]{2,1,0:T(8,128)}), f32[32,48,128]{2,1,0:T(8,128)S(1)}, u32[]{:S(2)}, u32[]{:S(2)}) async-start(f32[32,48,128]{2,1,0:T(8,128)} %get-tuple-element.62), calls=%async_computation | async-start | bytes 1572864 | tf_op jit(solution)/shard_map/all_to_all | solution.py:462
  51.7 18.0 %all-to-all-done.got_ref = f32[32,48,128]{2,1,0:T(8,128)S(1)} async-done(((f32[32,48,128]{2,1,0:T(8,128)}), f32[32,48,128]{2,1,0:T(8,128)S(1)}, u32[]{:S(2)}, u32[]{:S(2)}) %all-to-all-start) | async-done | bytes 786464 | tf_op jit(solution)/shard_map/all_to_all | solution.py:462
  69.7 0.7 sum_pieces.1
  70.5 18.0 %all_to_all.15.got_ref.tail_ref = bf16[32,56,128]{2,1,0:T(8,128)(2,1)S(1)} all-to-all(bf16[32,56,128]{2,1,0:T(8,128)(2,1)S(1)} %get-tuple-element.63), channel_id=1, replica_groups=mesh['seq'=32,'head'=8] {'seq'}, dimensions={0} | all-to-all | bytes 917504 | tf_op jit(solution)/shard_map/all_to_all | solution.py:473
  88.5 0.7 head_squares.1
  89.2 10.7 %all-to-all-start.2 = ((f32[8,8,128]{2,1,0:T(8,128)}), f32[8,8,128]{2,1,0:T(8,128)S(1)}, u32[]{:S(2)}, u32[]{:S(2)}) async-start(f32[8,8,128]{2,1,0:T(8,128)} %head_squares.1), calls=%async_computation.2 | async-start | bytes 65536 | tf_op jit(solution)/shard_map/all_to_all | solution.py:475
  99.9 0.0 copy-start.4
  99.9 1.5 %query_gradients.1 = (f32[128,1024]{1,0:T(8,128)}, f32[128,128]{1,0:T(8,128)S(1)}) custom-call(f32[1024,128]{1,0:T(8,128)S(1)} %get-tuple-element.59.dlogit_ref, f32[1024,128]{1,0:T(8,128)S(1)} %get-tuple-element.39.inner_ref, f32[1024,128]{1,0:T(8,128)S(1)} %get-tuple-element.60.gn_ref, f32[8,128,128]{2,1,0:T(8,128)S(1)} %copy-done.1), custom_call_target="tpu_custom_call" | custom-call | tf_op jit(solution)/shard_map/query_gradients/pallas_call | solution.py:463
  101.3 0.0 copy-done.4
  101.4 1.2 %key_gradients.1 = (f32[128,128]{1,0:T(8,128)}, f32[128,128]{1,0:T(8,128)}) custom-call(s32[1,128]{1,0:T(1,128)S(1)} %bitcast.6, bf16[32,56,128]{2,1,0:T(8,128)(2,1)S(1)} %all_to_all.15.got_ref.tail_ref, f32[1,256]{1,0:T(1,128)S(1)} %get-tuple-element.64.norms_ref, bf16[128,128]{1,0:T(8,128)(2,1)S(1)} %copy-done.4, f32[1,128,128]{2,1,0:T(8,128)S(1)} %copy-done.2, ...), custom_call_target="tpu_custom_call" | custom-call | tf_op jit(solution)/shard_map/key_gradients/pallas_call | solution.py:476
  102.5 2.0 %all-to-all-done.2.squares_ref = f32[8,8,128]{2,1,0:T(8,128)S(1)} async-done(((f32[8,8,128]{2,1,0:T(8,128)}), f32[8,8,128]{2,1,0:T(8,128)S(1)}, u32[]{:S(2)}, u32[]{:S(2)}) %all-to-all-start.2) | async-done | bytes 32800 | tf_op jit(solution)/shard_map/all_to_all | solution.py:475
  104.6 0.9 clip_maps.1
  (2 shorter events, 0.0 us)
Async XLA Ops:
  1.4 12.6 %collective-permute-start = (bf16[256,128]{1,0:T(8,128)(2,1)S(1)}, bf16[256,128]{1,0:T(8,128)(2,1)S(1)}, u32[]{:S(2)}, u32[]{:S(2)}) collective-permute-start(bf16[256,128]{1,0:T(8,128)(2,1)S(1)} %pad_add_fusion.rest_6_), channel_id=1, source_target_pairs={{0,32},{8,40},{16,48},{24,56},{32,64},{40,72},{48,80},{56,88},{64,... | collective-permute-start | bytes 196616 | tf_op jit(solution)/shard_map/ppermute | solution.py:426
  9.2 6.5 %collective-permute-start.2 = (bf16[256,128]{1,0:T(8,128)(2,1)S(1)}, bf16[256,128]{1,0:T(8,128)(2,1)S(1)}, u32[]{:S(2)}, u32[]{:S(2)}) collective-permute-start(bf16[256,128]{1,0:T(8,128)(2,1)S(1)} %pad_add_fusion.rest_6_), channel_id=1, source_target_pairs={{0,8},{8,16},{16,24},{24,32},{32,40},{40,48},{48,56},{56,64},{64,7... | collective-permute-start | bytes 196616 | tf_op jit(solution)/shard_map/ppermute | solution.py:426
  9.9 7.9 %collective-permute-start.3 = (bf16[256,128]{1,0:T(8,128)(2,1)S(1)}, bf16[256,128]{1,0:T(8,128)(2,1)S(1)}, u32[]{:S(2)}, u32[]{:S(2)}) collective-permute-start(bf16[256,128]{1,0:T(8,128)(2,1)S(1)} %pad_add_fusion.rest_6_), channel_id=1, source_target_pairs={{0,56},{8,64},{16,72},{24,80},{32,88},{40,96},{48,104},{56,112},{6... | collective-permute-start | bytes 196616 | tf_op jit(solution)/shard_map/ppermute | solution.py:426
  12.8 6.9 %collective-permute-start.1 = (bf16[256,128]{1,0:T(8,128)(2,1)S(1)}, bf16[256,128]{1,0:T(8,128)(2,1)S(1)}, u32[]{:S(2)}, u32[]{:S(2)}) collective-permute-start(bf16[256,128]{1,0:T(8,128)(2,1)S(1)} %pad_add_fusion.rest_6_), channel_id=1, source_target_pairs={{0,64},{8,72},{16,80},{24,88},{32,96},{40,104},{48,112},{56,120},{... | collective-permute-start | bytes 196616 | tf_op jit(solution)/shard_map/ppermute | solution.py:426
  19.6 5.0 %copy-start.2 = (f32[1,128,128]{2,1,0:T(8,128)S(1)}, f32[1,128,128]{2,1,0:T(8,128)}, u32[]{:S(2)}) copy-start(f32[1,128,128]{2,1,0:T(8,128)} %kmap_ref.9) | copy-start | bytes 196612
  19.6 5.0 %copy-start.5 = (s32[128]{0:T(128)S(1)}, s32[128]{0:T(128)}, u32[]{:S(2)}) copy-start(s32[128]{0:T(128)} %param.9) | copy-start | bytes 1540
  19.7 5.0 %copy-start = (bf16[128,1024]{1,0:T(8,128)(2,1)S(1)}, bf16[128,1024]{1,0:T(8,128)(2,1)}, u32[]{:S(2)}) copy-start(bf16[128,1024]{1,0:T(8,128)(2,1)} %q_ref.7) | copy-start | bytes 786436
  19.7 11.4 %copy-start.1 = (f32[8,128,128]{2,1,0:T(8,128)S(1)}, f32[8,128,128]{2,1,0:T(8,128)}, u32[]{:S(2)}) copy-start(f32[8,128,128]{2,1,0:T(8,128)} %qmap_ref.3) | copy-start | bytes 1572868
  19.7 11.3 %collective-permute-start.6 = (bf16[1024,128]{1,0:T(8,128)(2,1)S(1)}, bf16[1024,128]{1,0:T(8,128)(2,1)S(1)}, u32[]{:S(2)}, u32[]{:S(2)}) collective-permute-start(bf16[1024,128]{1,0:T(8,128)(2,1)S(1)} %pad_maximum_fusion.rest_0_), channel_id=1, source_target_pairs={{0,64},{8,72},{16,80},{24,88},{32,96},{40,104},{48,112},{56,120},{... | collective-permute-start | bytes 786440 | tf_op jit(solution)/shard_map/ppermute | solution.py:426
  19.8 7.8 %collective-permute-start.4 = (bf16[512,128]{1,0:T(8,128)(2,1)S(1)}, bf16[512,128]{1,0:T(8,128)(2,1)S(1)}, u32[]{:S(2)}, u32[]{:S(2)}) collective-permute-start(bf16[512,128]{1,0:T(8,128)(2,1)S(1)} %get-tuple-element.72), channel_id=1, source_target_pairs={{0,8},{8,16},{16,24},{24,32},{32,40},{40,48},{48,56},{56,64},{64,7... | collective-permute-start | bytes 393224 | tf_op jit(solution)/shard_map/ppermute | solution.py:426
  19.9 7.8 %collective-permute-start.5 = (bf16[512,128]{1,0:T(8,128)(2,1)S(1)}, bf16[512,128]{1,0:T(8,128)(2,1)S(1)}, u32[]{:S(2)}, u32[]{:S(2)}) collective-permute-start(bf16[512,128]{1,0:T(8,128)(2,1)S(1)} %get-tuple-element.71), channel_id=1, source_target_pairs={{0,248},{8,0},{16,8},{24,16},{32,24},{40,32},{48,40},{56,48},{64,5... | collective-permute-start | bytes 393224 | tf_op jit(solution)/shard_map/ppermute | solution.py:426
  24.7 6.4 %copy-start.3 = (bf16[128,128]{1,0:T(8,128)(2,1)S(1)}, bf16[128,128]{1,0:T(8,128)(2,1)}, u32[]{:S(2)}) copy-start(bf16[128,128]{1,0:T(8,128)(2,1)} %k_ref.1) | copy-start | bytes 98308
  31.0 5.0 %collective-permute-start.7 = (bf16[512,128]{1,0:T(8,128)(2,1)S(1)}, bf16[512,128]{1,0:T(8,128)(2,1)S(1)}, u32[]{:S(2)}, u32[]{:S(2)}) collective-permute-start(bf16[512,128]{1,0:T(8,128)(2,1)S(1)} %collective-permute-done.4.rest_1_.rest_2_), channel_id=1, source_target_pairs={{0,64},{8,72},{16,80},{24,88},{32,96},{40,104},{48,112},{56,120},{... | collective-permute-start | bytes 393224 | tf_op jit(solution)/shard_map/ppermute | solution.py:426
  31.0 7.5 %collective-permute-start.8 = (bf16[512,128]{1,0:T(8,128)(2,1)S(1)}, bf16[512,128]{1,0:T(8,128)(2,1)S(1)}, u32[]{:S(2)}, u32[]{:S(2)}) collective-permute-start(bf16[512,128]{1,0:T(8,128)(2,1)S(1)} %collective-permute-done.5.rest_2_.rest_3_), channel_id=1, source_target_pairs={{0,64},{8,72},{16,80},{24,88},{32,96},{40,104},{48,112},{56,120},{... | collective-permute-start | bytes 393224 | tf_op jit(solution)/shard_map/ppermute | solution.py:426
  47.6 22.1 %all-to-all-start = ((f32[32,48,128]{2,1,0:T(8,128)}), f32[32,48,128]{2,1,0:T(8,128)S(1)}, u32[]{:S(2)}, u32[]{:S(2)}) async-start(f32[32,48,128]{2,1,0:T(8,128)} %get-tuple-element.62), calls=%async_computation | async-start | bytes 1572864 | tf_op jit(solution)/shard_map/all_to_all | solution.py:462
  89.2 15.4 %all-to-all-start.2 = ((f32[8,8,128]{2,1,0:T(8,128)}), f32[8,8,128]{2,1,0:T(8,128)S(1)}, u32[]{:S(2)}, u32[]{:S(2)}) async-start(f32[8,8,128]{2,1,0:T(8,128)} %head_squares.1), calls=%async_computation.2 | async-start | bytes 65536 | tf_op jit(solution)/shard_map/all_to_all | solution.py:475
  99.9 1.5 %copy-start.4 = (bf16[128,128]{1,0:T(8,128)(2,1)S(1)}, bf16[128,128]{1,0:T(8,128)(2,1)}, u32[]{:S(2)}) copy-start(bf16[128,128]{1,0:T(8,128)(2,1)} %v_ref.1) | copy-start | bytes 98308

commit v11 on v10

--- a/solution.py
+++ b/solution.py
@@ -440,6 +440,7 @@
     phi, inner, own = call(
         local_kernel, "local_features", [V] * 5, [(rows, 2 * T), (rows, T), (T, 2 * T)]
     )(pos, queries, key_vectors, query_map, key_map)
+    b4, b8, b1, b7 = lax.optimization_barrier((b4, b8, b1, b7))
     near = jnp.concatenate([b4, b8, b1, b7], axis=0)
     near, b4, b1, b7 = lax.optimization_barrier((near, b4, b1, b7))
     far = shift(near, 8)

time: 106 us -> 99.1 us (0.935)
  waiting for transfers between devices: 32.9 us -> 24.1 us
  starting transfers between devices: 32.3 us -> 34 us
    ppermute x9, waiting for transfers between devices: 12.9 us -> 6.76 us  [shift(): lax.ppermute(x, 'seq', [(i, (i + k) % pieces) for i in range(pieces)])]
    all_to_all x1, waiting for transfers between devices: 18 us -> 15.3 us  [on_device(): gathered = lax.all_to_all(payload, 'seq', 0, 0)]
where the time goes in v11:
time: 99.1 us; the launch traced here: 98.7 us
  starting transfers between devices  34 us (34%)
  waiting for transfers between devices  24.1 us (24%)
  Pallas kernels  20.6 us (21%)
  blocking collectives  18.4 us (19%)
    all_to_all x1, blocking collectives, on_device(): back = lax.all_to_all(reduced, 'seq', 0, 0)  18.4 us
    ppermute x9, starting transfers between devices, shift(): lax.ppermute(x, 'seq', [(i, (i + k) % pieces) for i in range(pieces)])  17.5 us
    all_to_all x1, waiting for transfers between devices, on_device(): gathered = lax.all_to_all(payload, 'seq', 0, 0)  15.3 us
    all_to_all x1, starting transfers between devices, on_device(): squares = lax.all_to_all(squares, 'head', 0, 0)  11.5 us
    pallas_call x1, Pallas kernels, on_device(): call(functools.partial(main_kernel, places, 2), 'attention_transfer', [V]...  9.01 us
    ppermute x9, waiting for transfers between devices, shift(): lax.ppermute(x, 'seq', [(i, (i + k) % pieces) for i in range(pieces)])  6.76 us
    all_to_all x1, starting transfers between devices, on_device(): gathered = lax.all_to_all(payload, 'seq', 0, 0)  5.03 us
    pallas_call x2, Pallas kernels, part_of(): call(functools.partial(part_kernel, places), name, [V] * (3 + len(arrays)...  4.99 us
  transfers between devices with their start and end apart: 11, of which 9 were waited for; matrix products, arithmetic and copies ran while one was open for 0% of the time, Pallas kernels for 9%

profile of v11, /device:TPU:1, one launch (start us, length us, event | category | flops | bytes accessed | tf_op | source)
XLA Modules:
  0.0 98.7 jit_solution(15115469023941084610)
XLA Ops:
  0.6 0.8 pad_add_fusion.rest_6_
  1.4 7.7 %collective-permute-start = (bf16[256,128]{1,0:T(8,128)(2,1)S(1)}, bf16[256,128]{1,0:T(8,128)(2,1)S(1)}, u32[]{:S(2)}, u32[]{:S(2)}) collective-permute-start(bf16[256,128]{1,0:T(8,128)(2,1)S(1)} %pad_add_fusion.rest_6_), channel_id=1, source_target_pairs={{0,32},{8,40},{16,48},{24,56},{32,64},{40,72},{48,80},{56,88},{64,... | collective-permute-start | bytes 196616 | tf_op jit(solution)/shard_map/ppermute | solution.py:426
  9.2 1.2 %collective-permute-start.1 = (bf16[256,128]{1,0:T(8,128)(2,1)S(1)}, bf16[256,128]{1,0:T(8,128)(2,1)S(1)}, u32[]{:S(2)}, u32[]{:S(2)}) collective-permute-start(bf16[256,128]{1,0:T(8,128)(2,1)S(1)} %pad_add_fusion.rest_6_), channel_id=1, source_target_pairs={{0,64},{8,72},{16,80},{24,88},{32,96},{40,104},{48,112},{56,120},{... | collective-permute-start | bytes 196616 | tf_op jit(solution)/shard_map/ppermute | solution.py:426
  10.4 0.7 collective-permute-start.2
  11.1 2.9 %collective-permute-start.3 = (bf16[256,128]{1,0:T(8,128)(2,1)S(1)}, bf16[256,128]{1,0:T(8,128)(2,1)S(1)}, u32[]{:S(2)}, u32[]{:S(2)}) collective-permute-start(bf16[256,128]{1,0:T(8,128)(2,1)S(1)} %pad_add_fusion.rest_6_), channel_id=1, source_target_pairs={{0,56},{8,64},{16,72},{24,80},{32,88},{40,96},{48,104},{56,112},{6... | collective-permute-start | bytes 196616 | tf_op jit(solution)/shard_map/ppermute | solution.py:426
  14.0 0.0 collective-permute-done
  14.0 0.2 collective-permute-done.1
  14.1 3.0 %collective-permute-done.2 = bf16[256,128]{1,0:T(8,128)(2,1)S(1)} collective-permute-done((bf16[256,128]{1,0:T(8,128)(2,1)S(1)}, bf16[256,128]{1,0:T(8,128)(2,1)S(1)}, u32[]{:S(2)}, u32[]{:S(2)}) %collective-permute-start.2) | collective-permute-done | bytes 65568 | tf_op jit(solution)/shard_map/ppermute | solution.py:426
  17.2 0.2 collective-permute-done.3
  17.4 0.0 copy-start.2
  17.4 0.0 copy-start.5
  17.4 0.0 copy-start
  17.4 0.0 copy-start.1
  17.4 0.1 collective-permute-start.6
  17.5 0.1 collective-permute-start.4
  17.6 4.8 %collective-permute-start.5 = (bf16[512,128]{1,0:T(8,128)(2,1)S(1)}, bf16[512,128]{1,0:T(8,128)(2,1)S(1)}, u32[]{:S(2)}, u32[]{:S(2)}) collective-permute-start(bf16[512,128]{1,0:T(8,128)(2,1)S(1)} %get-tuple-element.79), channel_id=1, source_target_pairs={{0,248},{8,0},{16,8},{24,16},{32,24},{40,32},{48,40},{56,48},{64,5... | collective-permute-start | bytes 393224 | tf_op jit(solution)/shard_map/ppermute | solution.py:426
  22.4 0.0 copy-done.2
  22.4 0.0 copy-done.5
  22.4 0.0 copy-done
  22.4 0.0 copy-start.3
  22.4 1.8 %early_keys.1 = (f32[512,256]{1,0:T(8,128)S(1)}, f32[256,256]{1,0:T(8,128)S(1)}, f32[1024,128]{1,0:T(8,128)S(1)}, f32[1024,128]{1,0:T(8,128)S(1)}, f32[1024,128]{1,0:T(8,128)S(1)}) custom-call(s32[1,128]{1,0:T(1,128)S(1)} %bitcast.2, bf16[128,1024]{1,0:T(8,128)(2,1)S(1)} %copy-done, f32[1,128,128]{2,1,0:T(8,128)S(1)} %copy-done.2, ...), custom_call_target="tpu_custom_call" | custom-call | tf_op jit(solution)/shard_map/early_keys/pallas_call | solution.py:430
  24.3 0.6 collective-permute-done.4.rest_1_.rest_2_
  24.9 0.0 collective-permute-done.5.rest_2_.rest_3_
  24.9 1.2 %collective-permute-done.6.rest_0_.rest_1_ = bf16[1024,128]{1,0:T(8,128)(2,1)S(1)} collective-permute-done((bf16[1024,128]{1,0:T(8,128)(2,1)S(1)}, bf16[1024,128]{1,0:T(8,128)(2,1)S(1)}, u32[]{:S(2)}, u32[]{:S(2)}) %collective-permute-start.6) | collective-permute-done | bytes 262176 | tf_op jit(solution)/shard_map/ppermute | solution.py:426
  26.0 0.0 collective-permute-start.7
  26.0 0.0 collective-permute-start.8
  26.0 0.0 copy-done.1
  26.0 0.0 copy-done.3
  26.1 1.6 %local_features.1 = (f32[1024,256]{1,0:T(8,128)S(1)}, f32[1024,128]{1,0:T(8,128)S(1)}, f32[128,256]{1,0:T(8,128)S(1)}) custom-call(s32[1,128]{1,0:T(1,128)S(1)} %bitcast.3, bf16[128,1024]{1,0:T(8,128)(2,1)S(1)} %copy-done, bf16[128,128]{1,0:T(8,128)(2,1)S(1)} %copy-done.3, f32[8,128,128]{2,1,0:T(8,128)S(1)} %copy-done.1, f32[1,128,128]{2,1,0:T(8,128)S(1)} %copy-done.2), custom_call_target="tpu_custom_call" | custom-call | tf_op jit(solution)/shard_map/local_features/pallas_call | solution.py:440
  27.7 3.2 %middle_keys.1 = (f32[1024,256]{1,0:T(8,128)S(1)}, f32[256,256]{1,0:T(8,128)S(1)}, f32[1024,128]{1,0:T(8,128)S(1)}, f32[1024,128]{1,0:T(8,128)S(1)}, f32[1024,128]{1,0:T(8,128)S(1)}) custom-call(s32[1,128]{1,0:T(1,128)S(1)} %bitcast.4, bf16[128,1024]{1,0:T(8,128)(2,1)S(1)} %copy-done, f32[1,128,128]{2,1,0:T(8,128)S(1)} %copy-done.2, ...), custom_call_target="tpu_custom_call" | custom-call | tf_op jit(solution)/shard_map/middle_keys/pallas_call | solution.py:430
  30.9 0.2 collective-permute-done.7.rest_4_
  31.1 1.4 %collective-permute-done.8.rest_5_ = bf16[512,128]{1,0:T(8,128)(2,1)S(1)} collective-permute-done((bf16[512,128]{1,0:T(8,128)(2,1)S(1)}, bf16[512,128]{1,0:T(8,128)(2,1)S(1)}, u32[]{:S(2)}, u32[]{:S(2)}) %collective-permute-start.8) | collective-permute-done | bytes 131104 | tf_op jit(solution)/shard_map/ppermute | solution.py:426
  32.5 9.0 %attention_transfer.1 = (f32[32,48,128]{2,1,0:T(8,128)}, f32[1024,128]{1,0:T(8,128)S(1)}, f32[1024,128]{1,0:T(8,128)S(1)}, f32[128,256]{1,0:T(8,128)S(1)}) custom-call(s32[1,128]{1,0:T(1,128)S(1)} %bitcast.5, bf16[128,1024]{1,0:T(8,128)(2,1)S(1)} %copy-done, f32[1,128,128]{2,1,0:T(8,128)S(1)} %copy-done.2, f32[1024,256]{1,0:T(8,128)S(1)} %get-tuple-element.42.phi_ref, ...), custom_call_target="tpu_custom_call" | custom-call | tf_op jit(solution)/shard_map/attention_transfer/pallas_call | solution.py:455
  41.5 5.0 %all-to-all-start = ((f32[32,48,128]{2,1,0:T(8,128)}), f32[32,48,128]{2,1,0:T(8,128)S(1)}, u32[]{:S(2)}, u32[]{:S(2)}) async-start(f32[32,48,128]{2,1,0:T(8,128)} %get-tuple-element.70), calls=%async_computation | async-start | bytes 1572864 | tf_op jit(solution)/shard_map/all_to_all | solution.py:463
  46.5 15.3 %all-to-all-done.got_ref = f32[32,48,128]{2,1,0:T(8,128)S(1)} async-done(((f32[32,48,128]{2,1,0:T(8,128)}), f32[32,48,128]{2,1,0:T(8,128)S(1)}, u32[]{:S(2)}, u32[]{:S(2)}) %all-to-all-start) | async-done | bytes 786464 | tf_op jit(solution)/shard_map/all_to_all | solution.py:463
  61.8 0.7 sum_pieces.1
  62.6 18.4 %all_to_all.15.got_ref.tail_ref = bf16[32,56,128]{2,1,0:T(8,128)(2,1)S(1)} all-to-all(bf16[32,56,128]{2,1,0:T(8,128)(2,1)S(1)} %get-tuple-element.71), channel_id=1, replica_groups=mesh['seq'=32,'head'=8] {'seq'}, dimensions={0} | all-to-all | bytes 917504 | tf_op jit(solution)/shard_map/all_to_all | solution.py:474
  81.0 0.7 head_squares.1
  81.6 11.5 %all-to-all-start.2 = ((f32[8,8,128]{2,1,0:T(8,128)}), f32[8,8,128]{2,1,0:T(8,128)S(1)}, u32[]{:S(2)}, u32[]{:S(2)}) async-start(f32[8,8,128]{2,1,0:T(8,128)} %head_squares.1), calls=%async_computation.2 | async-start | bytes 65536 | tf_op jit(solution)/shard_map/all_to_all | solution.py:476
  93.1 0.0 copy-start.4
  93.1 1.5 %query_gradients.1 = (f32[128,1024]{1,0:T(8,128)}, f32[128,128]{1,0:T(8,128)S(1)}) custom-call(f32[1024,128]{1,0:T(8,128)S(1)} %get-tuple-element.67.dlogit_ref, f32[1024,128]{1,0:T(8,128)S(1)} %get-tuple-element.43.inner_ref, f32[1024,128]{1,0:T(8,128)S(1)} %get-tuple-element.68.gn_ref, f32[8,128,128]{2,1,0:T(8,128)S(1)} %copy-done.1), custom_call_target="tpu_custom_call" | custom-call | tf_op jit(solution)/shard_map/query_gradients/pallas_call | solution.py:464
  94.6 0.0 copy-done.4
  94.6 1.2 %key_gradients.1 = (f32[128,128]{1,0:T(8,128)}, f32[128,128]{1,0:T(8,128)}) custom-call(s32[1,128]{1,0:T(1,128)S(1)} %bitcast.6, bf16[32,56,128]{2,1,0:T(8,128)(2,1)S(1)} %all_to_all.15.got_ref.tail_ref, f32[1,256]{1,0:T(1,128)S(1)} %get-tuple-element.72.norms_ref, bf16[128,128]{1,0:T(8,128)(2,1)S(1)} %copy-done.4, f32[1,128,128]{2,1,0:T(8,128)S(1)} %copy-done.2, ...), custom_call_target="tpu_custom_call" | custom-call | tf_op jit(solution)/shard_map/key_gradients/pallas_call | solution.py:477
  95.8 2.0 %all-to-all-done.2.squares_ref = f32[8,8,128]{2,1,0:T(8,128)S(1)} async-done(((f32[8,8,128]{2,1,0:T(8,128)}), f32[8,8,128]{2,1,0:T(8,128)S(1)}, u32[]{:S(2)}, u32[]{:S(2)}) %all-to-all-start.2) | async-done | bytes 32800 | tf_op jit(solution)/shard_map/all_to_all | solution.py:476
  97.9 0.9 clip_maps.1
  (2 shorter events, 0.0 us)
Async XLA Ops:
  1.4 12.6 %collective-permute-start = (bf16[256,128]{1,0:T(8,128)(2,1)S(1)}, bf16[256,128]{1,0:T(8,128)(2,1)S(1)}, u32[]{:S(2)}, u32[]{:S(2)}) collective-permute-start(bf16[256,128]{1,0:T(8,128)(2,1)S(1)} %pad_add_fusion.rest_6_), channel_id=1, source_target_pairs={{0,32},{8,40},{16,48},{24,56},{32,64},{40,72},{48,80},{56,88},{64,... | collective-permute-start | bytes 196616 | tf_op jit(solution)/shard_map/ppermute | solution.py:426
  9.2 5.0 %collective-permute-start.1 = (bf16[256,128]{1,0:T(8,128)(2,1)S(1)}, bf16[256,128]{1,0:T(8,128)(2,1)S(1)}, u32[]{:S(2)}, u32[]{:S(2)}) collective-permute-start(bf16[256,128]{1,0:T(8,128)(2,1)S(1)} %pad_add_fusion.rest_6_), channel_id=1, source_target_pairs={{0,64},{8,72},{16,80},{24,88},{32,96},{40,104},{48,112},{56,120},{... | collective-permute-start | bytes 196616 | tf_op jit(solution)/shard_map/ppermute | solution.py:426
  10.4 6.8 %collective-permute-start.2 = (bf16[256,128]{1,0:T(8,128)(2,1)S(1)}, bf16[256,128]{1,0:T(8,128)(2,1)S(1)}, u32[]{:S(2)}, u32[]{:S(2)}) collective-permute-start(bf16[256,128]{1,0:T(8,128)(2,1)S(1)} %pad_add_fusion.rest_6_), channel_id=1, source_target_pairs={{0,8},{8,16},{16,24},{24,32},{32,40},{40,48},{48,56},{56,64},{64,7... | collective-permute-start | bytes 196616 | tf_op jit(solution)/shard_map/ppermute | solution.py:426
  11.1 6.3 %collective-permute-start.3 = (bf16[256,128]{1,0:T(8,128)(2,1)S(1)}, bf16[256,128]{1,0:T(8,128)(2,1)S(1)}, u32[]{:S(2)}, u32[]{:S(2)}) collective-permute-start(bf16[256,128]{1,0:T(8,128)(2,1)S(1)} %pad_add_fusion.rest_6_), channel_id=1, source_target_pairs={{0,56},{8,64},{16,72},{24,80},{32,88},{40,96},{48,104},{56,112},{6... | collective-permute-start | bytes 196616 | tf_op jit(solution)/shard_map/ppermute | solution.py:426
  17.4 5.0 %copy-start.2 = (f32[1,128,128]{2,1,0:T(8,128)S(1)}, f32[1,128,128]{2,1,0:T(8,128)}, u32[]{:S(2)}) copy-start(f32[1,128,128]{2,1,0:T(8,128)} %kmap_ref.9) | copy-start | bytes 196612
  17.4 5.0 %copy-start.5 = (s32[128]{0:T(128)S(1)}, s32[128]{0:T(128)}, u32[]{:S(2)}) copy-start(s32[128]{0:T(128)} %param.9) | copy-start | bytes 1540
  17.4 5.0 %copy-start = (bf16[128,1024]{1,0:T(8,128)(2,1)S(1)}, bf16[128,1024]{1,0:T(8,128)(2,1)}, u32[]{:S(2)}) copy-start(bf16[128,1024]{1,0:T(8,128)(2,1)} %q_ref.7) | copy-start | bytes 786436
  17.4 8.6 %copy-start.1 = (f32[8,128,128]{2,1,0:T(8,128)S(1)}, f32[8,128,128]{2,1,0:T(8,128)}, u32[]{:S(2)}) copy-start(f32[8,128,128]{2,1,0:T(8,128)} %qmap_ref.3) | copy-start | bytes 1572868
  17.4 8.6 %collective-permute-start.6 = (bf16[1024,128]{1,0:T(8,128)(2,1)S(1)}, bf16[1024,128]{1,0:T(8,128)(2,1)S(1)}, u32[]{:S(2)}, u32[]{:S(2)}) collective-permute-start(bf16[1024,128]{1,0:T(8,128)(2,1)S(1)} %pad_maximum_fusion.rest_0_), channel_id=1, source_target_pairs={{0,64},{8,72},{16,80},{24,88},{32,96},{40,104},{48,112},{56,120},{... | collective-permute-start | bytes 786440 | tf_op jit(solution)/shard_map/ppermute | solution.py:426
  17.5 7.3 %collective-permute-start.4 = (bf16[512,128]{1,0:T(8,128)(2,1)S(1)}, bf16[512,128]{1,0:T(8,128)(2,1)S(1)}, u32[]{:S(2)}, u32[]{:S(2)}) collective-permute-start(bf16[512,128]{1,0:T(8,128)(2,1)S(1)} %get-tuple-element.80), channel_id=1, source_target_pairs={{0,8},{8,16},{16,24},{24,32},{32,40},{40,48},{48,56},{56,64},{64,7... | collective-permute-start | bytes 393224 | tf_op jit(solution)/shard_map/ppermute | solution.py:426
  17.6 7.2 %collective-permute-start.5 = (bf16[512,128]{1,0:T(8,128)(2,1)S(1)}, bf16[512,128]{1,0:T(8,128)(2,1)S(1)}, u32[]{:S(2)}, u32[]{:S(2)}) collective-permute-start(bf16[512,128]{1,0:T(8,128)(2,1)S(1)} %get-tuple-element.79), channel_id=1, source_target_pairs={{0,248},{8,0},{16,8},{24,16},{32,24},{40,32},{48,40},{56,48},{64,5... | collective-permute-start | bytes 393224 | tf_op jit(solution)/shard_map/ppermute | solution.py:426
  22.4 3.6 %copy-start.3 = (bf16[128,128]{1,0:T(8,128)(2,1)S(1)}, bf16[128,128]{1,0:T(8,128)(2,1)}, u32[]{:S(2)}) copy-start(bf16[128,128]{1,0:T(8,128)(2,1)} %k_ref.1) | copy-start | bytes 98308
  26.0 5.0 %collective-permute-start.7 = (bf16[512,128]{1,0:T(8,128)(2,1)S(1)}, bf16[512,128]{1,0:T(8,128)(2,1)S(1)}, u32[]{:S(2)}, u32[]{:S(2)}) collective-permute-start(bf16[512,128]{1,0:T(8,128)(2,1)S(1)} %collective-permute-done.4.rest_1_.rest_2_), channel_id=1, source_target_pairs={{0,64},{8,72},{16,80},{24,88},{32,96},{40,104},{48,112},{56,120},{... | collective-permute-start | bytes 393224 | tf_op jit(solution)/shard_map/ppermute | solution.py:426
  26.0 6.4 %collective-permute-start.8 = (bf16[512,128]{1,0:T(8,128)(2,1)S(1)}, bf16[512,128]{1,0:T(8,128)(2,1)S(1)}, u32[]{:S(2)}, u32[]{:S(2)}) collective-permute-start(bf16[512,128]{1,0:T(8,128)(2,1)S(1)} %collective-permute-done.5.rest_2_.rest_3_), channel_id=1, source_target_pairs={{0,64},{8,72},{16,80},{24,88},{32,96},{40,104},{48,112},{56,120},{... | collective-permute-start | bytes 393224 | tf_op jit(solution)/shard_map/ppermute | solution.py:426
  41.5 20.3 %all-to-all-start = ((f32[32,48,128]{2,1,0:T(8,128)}), f32[32,48,128]{2,1,0:T(8,128)S(1)}, u32[]{:S(2)}, u32[]{:S(2)}) async-start(f32[32,48,128]{2,1,0:T(8,128)} %get-tuple-element.70), calls=%async_computation | async-start | bytes 1572864 | tf_op jit(solution)/shard_map/all_to_all | solution.py:463
  81.6 16.2 %all-to-all-start.2 = ((f32[8,8,128]{2,1,0:T(8,128)}), f32[8,8,128]{2,1,0:T(8,128)S(1)}, u32[]{:S(2)}, u32[]{:S(2)}) async-start(f32[8,8,128]{2,1,0:T(8,128)} %head_squares.1), calls=%async_computation.2 | async-start | bytes 65536 | tf_op jit(solution)/shard_map/all_to_all | solution.py:476
  93.1 1.5 %copy-start.4 = (bf16[128,128]{1,0:T(8,128)(2,1)S(1)}, bf16[128,128]{1,0:T(8,128)(2,1)}, u32[]{:S(2)}) copy-start(bf16[128,128]{1,0:T(8,128)(2,1)} %v_ref.1) | copy-start | bytes 98308

commit v12 on v11

--- a/solution.py
+++ b/solution.py
@@ -447,7 +447,8 @@
     n1 = shift(jnp.concatenate([b1, b4], axis=0), 1)
     n2 = shift(jnp.concatenate([b4, b7], axis=0), -1)
     early = list(part_of("early_keys", [near], [(4, 8, 1, 7)]))
-    n1, n2, far, early[1] = lax.optimization_barrier((n1, n2, far, early[1]))
+    n1, early[1] = lax.optimization_barrier((n1, early[1]))
+    n2, far = lax.optimization_barrier((n2, far))
     f1, f2 = shift(n1, 8), shift(n2, 8)
     middle = part_of("middle_keys", [far, n1, n2], [(12, 16, 9, 15), (2, 5), (3, 6)])
     arrays = [near, far, n1, n2, f1, f2, kv]

time: 99.1 us -> 99.1 us (level)
  no operation moved by 1% of the time
where the time goes in v12:
time: 99.1 us; the launch traced here: 98.7 us
  starting transfers between devices  34.1 us (34%)
  waiting for transfers between devices  24 us (24%)
  Pallas kernels  20.6 us (21%)
  blocking collectives  18.4 us (19%)
    all_to_all x1, blocking collectives, on_device(): back = lax.all_to_all(reduced, 'seq', 0, 0)  18.4 us
    ppermute x9, starting transfers between devices, shift(): lax.ppermute(x, 'seq', [(i, (i + k) % pieces) for i in range(pieces)])  17.5 us
    all_to_all x1, waiting for transfers between devices, on_device(): gathered = lax.all_to_all(payload, 'seq', 0, 0)  15.3 us
    all_to_all x1, starting transfers between devices, on_device(): squares = lax.all_to_all(squares, 'head', 0, 0)  11.5 us
    pallas_call x1, Pallas kernels, on_device(): call(functools.partial(main_kernel, places, 2), 'attention_transfer', [V]...  9.02 us
    ppermute x9, waiting for transfers between devices, shift(): lax.ppermute(x, 'seq', [(i, (i + k) % pieces) for i in range(pieces)])  6.65 us
    all_to_all x1, starting transfers between devices, on_device(): gathered = lax.all_to_all(payload, 'seq', 0, 0)  5.11 us
    pallas_call x2, Pallas kernels, part_of(): call(functools.partial(part_kernel, places), name, [V] * (3 + len(arrays)...  4.99 us
  transfers between devices with their start and end apart: 11, of which 9 were waited for; matrix products, arithmetic and copies ran while one was open for 0% of the time, Pallas kernels for 9%

profile of v12, /device:TPU:1, one launch (start us, length us, event | category | flops | bytes accessed | tf_op | source)
XLA Modules:
  0.0 98.7 jit_solution(3283462031857951248)
XLA Ops:
  0.6 0.8 pad_add_fusion.rest_6_
  1.4 7.7 %collective-permute-start = (bf16[256,128]{1,0:T(8,128)(2,1)S(1)}, bf16[256,128]{1,0:T(8,128)(2,1)S(1)}, u32[]{:S(2)}, u32[]{:S(2)}) collective-permute-start(bf16[256,128]{1,0:T(8,128)(2,1)S(1)} %pad_add_fusion.rest_6_), channel_id=1, source_target_pairs={{0,32},{8,40},{16,48},{24,56},{32,64},{40,72},{48,80},{56,88},{64,... | collective-permute-start | bytes 196616 | tf_op jit(solution)/shard_map/ppermute | solution.py:426
  9.2 1.2 %collective-permute-start.1 = (bf16[256,128]{1,0:T(8,128)(2,1)S(1)}, bf16[256,128]{1,0:T(8,128)(2,1)S(1)}, u32[]{:S(2)}, u32[]{:S(2)}) collective-permute-start(bf16[256,128]{1,0:T(8,128)(2,1)S(1)} %pad_add_fusion.rest_6_), channel_id=1, source_target_pairs={{0,64},{8,72},{16,80},{24,88},{32,96},{40,104},{48,112},{56,120},{... | collective-permute-start | bytes 196616 | tf_op jit(solution)/shard_map/ppermute | solution.py:426
  10.4 0.7 collective-permute-start.2
  11.1 2.9 %collective-permute-start.3 = (bf16[256,128]{1,0:T(8,128)(2,1)S(1)}, bf16[256,128]{1,0:T(8,128)(2,1)S(1)}, u32[]{:S(2)}, u32[]{:S(2)}) collective-permute-start(bf16[256,128]{1,0:T(8,128)(2,1)S(1)} %pad_add_fusion.rest_6_), channel_id=1, source_target_pairs={{0,56},{8,64},{16,72},{24,80},{32,88},{40,96},{48,104},{56,112},{6... | collective-permute-start | bytes 196616 | tf_op jit(solution)/shard_map/ppermute | solution.py:426
  14.0 0.0 collective-permute-done
  14.0 0.2 collective-permute-done.1
  14.1 3.0 %collective-permute-done.2 = bf16[256,128]{1,0:T(8,128)(2,1)S(1)} collective-permute-done((bf16[256,128]{1,0:T(8,128)(2,1)S(1)}, bf16[256,128]{1,0:T(8,128)(2,1)S(1)}, u32[]{:S(2)}, u32[]{:S(2)}) %collective-permute-start.2) | collective-permute-done | bytes 65568 | tf_op jit(solution)/shard_map/ppermute | solution.py:426
  17.2 0.2 collective-permute-done.3
  17.4 0.0 copy-start.2
  17.4 0.0 copy-start.5
  17.4 0.0 copy-start
  17.4 0.0 copy-start.1
  17.4 0.1 collective-permute-start.5
  17.5 0.1 collective-permute-start.6
  17.6 4.8 %collective-permute-start.4 = (bf16[512,128]{1,0:T(8,128)(2,1)S(1)}, bf16[512,128]{1,0:T(8,128)(2,1)S(1)}, u32[]{:S(2)}, u32[]{:S(2)}) collective-permute-start(bf16[512,128]{1,0:T(8,128)(2,1)S(1)} %get-tuple-element.80), channel_id=1, source_target_pairs={{0,248},{8,0},{16,8},{24,16},{32,24},{40,32},{48,40},{56,48},{64,5... | collective-permute-start | bytes 393224 | tf_op jit(solution)/shard_map/ppermute | solution.py:426
  22.4 0.0 copy-done.2
  22.4 0.0 copy-done.5
  22.4 0.0 copy-done
  22.4 0.0 copy-start.3
  22.4 1.8 %early_keys.1 = (f32[512,256]{1,0:T(8,128)S(1)}, f32[256,256]{1,0:T(8,128)S(1)}, f32[1024,128]{1,0:T(8,128)S(1)}, f32[1024,128]{1,0:T(8,128)S(1)}, f32[1024,128]{1,0:T(8,128)S(1)}) custom-call(s32[1,128]{1,0:T(1,128)S(1)} %bitcast.2, bf16[128,1024]{1,0:T(8,128)(2,1)S(1)} %copy-done, f32[1,128,128]{2,1,0:T(8,128)S(1)} %copy-done.2, ...), custom_call_target="tpu_custom_call" | custom-call | tf_op jit(solution)/shard_map/early_keys/pallas_call | solution.py:430
  24.3 0.6 collective-permute-done.6.rest_1_.rest_2_
  24.9 0.0 collective-permute-start.7
  24.9 0.0 collective-permute-done.4.rest_2_.rest_3_
  24.9 1.2 %collective-permute-done.5.rest_0_.rest_1_ = bf16[1024,128]{1,0:T(8,128)(2,1)S(1)} collective-permute-done((bf16[1024,128]{1,0:T(8,128)(2,1)S(1)}, bf16[1024,128]{1,0:T(8,128)(2,1)S(1)}, u32[]{:S(2)}, u32[]{:S(2)}) %collective-permute-start.5) | collective-permute-done | bytes 262176 | tf_op jit(solution)/shard_map/ppermute | solution.py:426
  26.0 0.0 collective-permute-start.8
  26.0 0.0 copy-done.1
  26.0 0.0 copy-done.3
  26.0 1.6 %local_features.1 = (f32[1024,256]{1,0:T(8,128)S(1)}, f32[1024,128]{1,0:T(8,128)S(1)}, f32[128,256]{1,0:T(8,128)S(1)}) custom-call(s32[1,128]{1,0:T(1,128)S(1)} %bitcast.3, bf16[128,1024]{1,0:T(8,128)(2,1)S(1)} %copy-done, bf16[128,128]{1,0:T(8,128)(2,1)S(1)} %copy-done.3, f32[8,128,128]{2,1,0:T(8,128)S(1)} %copy-done.1, f32[1,128,128]{2,1,0:T(8,128)S(1)} %copy-done.2), custom_call_target="tpu_custom_call" | custom-call | tf_op jit(solution)/shard_map/local_features/pallas_call | solution.py:440
  27.7 3.2 %middle_keys.1 = (f32[1024,256]{1,0:T(8,128)S(1)}, f32[256,256]{1,0:T(8,128)S(1)}, f32[1024,128]{1,0:T(8,128)S(1)}, f32[1024,128]{1,0:T(8,128)S(1)}, f32[1024,128]{1,0:T(8,128)S(1)}) custom-call(s32[1,128]{1,0:T(1,128)S(1)} %bitcast.4, bf16[128,1024]{1,0:T(8,128)(2,1)S(1)} %copy-done, f32[1,128,128]{2,1,0:T(8,128)S(1)} %copy-done.2, ...), custom_call_target="tpu_custom_call" | custom-call | tf_op jit(solution)/shard_map/middle_keys/pallas_call | solution.py:430
  30.9 0.1 collective-permute-done.7.rest_4_
  30.9 1.4 %collective-permute-done.8.rest_5_ = bf16[512,128]{1,0:T(8,128)(2,1)S(1)} collective-permute-done((bf16[512,128]{1,0:T(8,128)(2,1)S(1)}, bf16[512,128]{1,0:T(8,128)(2,1)S(1)}, u32[]{:S(2)}, u32[]{:S(2)}) %collective-permute-start.8) | collective-permute-done | bytes 131104 | tf_op jit(solution)/shard_map/ppermute | solution.py:426
  32.3 9.0 %attention_transfer.1 = (f32[32,48,128]{2,1,0:T(8,128)}, f32[1024,128]{1,0:T(8,128)S(1)}, f32[1024,128]{1,0:T(8,128)S(1)}, f32[128,256]{1,0:T(8,128)S(1)}) custom-call(s32[1,128]{1,0:T(1,128)S(1)} %bitcast.5, bf16[128,1024]{1,0:T(8,128)(2,1)S(1)} %copy-done, f32[1,128,128]{2,1,0:T(8,128)S(1)} %copy-done.2, f32[1024,256]{1,0:T(8,128)S(1)} %get-tuple-element.42.phi_ref, ...), custom_call_target="tpu_custom_call" | custom-call | tf_op jit(solution)/shard_map/attention_transfer/pallas_call | solution.py:456
  41.4 5.1 %all-to-all-start = ((f32[32,48,128]{2,1,0:T(8,128)}), f32[32,48,128]{2,1,0:T(8,128)S(1)}, u32[]{:S(2)}, u32[]{:S(2)}) async-start(f32[32,48,128]{2,1,0:T(8,128)} %get-tuple-element.70), calls=%async_computation | async-start | bytes 1572864 | tf_op jit(solution)/shard_map/all_to_all | solution.py:464
  46.5 15.3 %all-to-all-done.got_ref = f32[32,48,128]{2,1,0:T(8,128)S(1)} async-done(((f32[32,48,128]{2,1,0:T(8,128)}), f32[32,48,128]{2,1,0:T(8,128)S(1)}, u32[]{:S(2)}, u32[]{:S(2)}) %all-to-all-start) | async-done | bytes 786464 | tf_op jit(solution)/shard_map/all_to_all | solution.py:464
  61.8 0.7 sum_pieces.1
  62.6 18.4 %all_to_all.15.got_ref.tail_ref = bf16[32,56,128]{2,1,0:T(8,128)(2,1)S(1)} all-to-all(bf16[32,56,128]{2,1,0:T(8,128)(2,1)S(1)} %get-tuple-element.71), channel_id=1, replica_groups=mesh['seq'=32,'head'=8] {'seq'}, dimensions={0} | all-to-all | bytes 917504 | tf_op jit(solution)/shard_map/all_to_all | solution.py:475
  81.0 0.7 head_squares.1
  81.7 11.5 %all-to-all-start.2 = ((f32[8,8,128]{2,1,0:T(8,128)}), f32[8,8,128]{2,1,0:T(8,128)S(1)}, u32[]{:S(2)}, u32[]{:S(2)}) async-start(f32[8,8,128]{2,1,0:T(8,128)} %head_squares.1), calls=%async_computation.2 | async-start | bytes 65536 | tf_op jit(solution)/shard_map/all_to_all | solution.py:477
  93.1 0.0 copy-start.4
  93.1 1.5 %query_gradients.1 = (f32[128,1024]{1,0:T(8,128)}, f32[128,128]{1,0:T(8,128)S(1)}) custom-call(f32[1024,128]{1,0:T(8,128)S(1)} %get-tuple-element.67.dlogit_ref, f32[1024,128]{1,0:T(8,128)S(1)} %get-tuple-element.43.inner_ref, f32[1024,128]{1,0:T(8,128)S(1)} %get-tuple-element.68.gn_ref, f32[8,128,128]{2,1,0:T(8,128)S(1)} %copy-done.1), custom_call_target="tpu_custom_call" | custom-call | tf_op jit(solution)/shard_map/query_gradients/pallas_call | solution.py:465
  94.6 0.0 copy-done.4
  94.6 1.2 %key_gradients.1 = (f32[128,128]{1,0:T(8,128)}, f32[128,128]{1,0:T(8,128)}) custom-call(s32[1,128]{1,0:T(1,128)S(1)} %bitcast.6, bf16[32,56,128]{2,1,0:T(8,128)(2,1)S(1)} %all_to_all.15.got_ref.tail_ref, f32[1,256]{1,0:T(1,128)S(1)} %get-tuple-element.72.norms_ref, bf16[128,128]{1,0:T(8,128)(2,1)S(1)} %copy-done.4, f32[1,128,128]{2,1,0:T(8,128)S(1)} %copy-done.2, ...), custom_call_target="tpu_custom_call" | custom-call | tf_op jit(solution)/shard_map/key_gradients/pallas_call | solution.py:478
  95.8 2.0 %all-to-all-done.2.squares_ref = f32[8,8,128]{2,1,0:T(8,128)S(1)} async-done(((f32[8,8,128]{2,1,0:T(8,128)}), f32[8,8,128]{2,1,0:T(8,128)S(1)}, u32[]{:S(2)}, u32[]{:S(2)}) %all-to-all-start.2) | async-done | bytes 32800 | tf_op jit(solution)/shard_map/all_to_all | solution.py:477
  97.8 0.9 clip_maps.1
  (2 shorter events, 0.0 us)
Async XLA Ops:
  1.4 12.6 %collective-permute-start = (bf16[256,128]{1,0:T(8,128)(2,1)S(1)}, bf16[256,128]{1,0:T(8,128)(2,1)S(1)}, u32[]{:S(2)}, u32[]{:S(2)}) collective-permute-start(bf16[256,128]{1,0:T(8,128)(2,1)S(1)} %pad_add_fusion.rest_6_), channel_id=1, source_target_pairs={{0,32},{8,40},{16,48},{24,56},{32,64},{40,72},{48,80},{56,88},{64,... | collective-permute-start | bytes 196616 | tf_op jit(solution)/shard_map/ppermute | solution.py:426
  9.2 5.0 %collective-permute-start.1 = (bf16[256,128]{1,0:T(8,128)(2,1)S(1)}, bf16[256,128]{1,0:T(8,128)(2,1)S(1)}, u32[]{:S(2)}, u32[]{:S(2)}) collective-permute-start(bf16[256,128]{1,0:T(8,128)(2,1)S(1)} %pad_add_fusion.rest_6_), channel_id=1, source_target_pairs={{0,64},{8,72},{16,80},{24,88},{32,96},{40,104},{48,112},{56,120},{... | collective-permute-start | bytes 196616 | tf_op jit(solution)/shard_map/ppermute | solution.py:426
  10.4 6.8 %collective-permute-start.2 = (bf16[256,128]{1,0:T(8,128)(2,1)S(1)}, bf16[256,128]{1,0:T(8,128)(2,1)S(1)}, u32[]{:S(2)}, u32[]{:S(2)}) collective-permute-start(bf16[256,128]{1,0:T(8,128)(2,1)S(1)} %pad_add_fusion.rest_6_), channel_id=1, source_target_pairs={{0,8},{8,16},{16,24},{24,32},{32,40},{40,48},{48,56},{56,64},{64,7... | collective-permute-start | bytes 196616 | tf_op jit(solution)/shard_map/ppermute | solution.py:426
  11.1 6.3 %collective-permute-start.3 = (bf16[256,128]{1,0:T(8,128)(2,1)S(1)}, bf16[256,128]{1,0:T(8,128)(2,1)S(1)}, u32[]{:S(2)}, u32[]{:S(2)}) collective-permute-start(bf16[256,128]{1,0:T(8,128)(2,1)S(1)} %pad_add_fusion.rest_6_), channel_id=1, source_target_pairs={{0,56},{8,64},{16,72},{24,80},{32,88},{40,96},{48,104},{56,112},{6... | collective-permute-start | bytes 196616 | tf_op jit(solution)/shard_map/ppermute | solution.py:426
  17.4 5.0 %copy-start.2 = (f32[1,128,128]{2,1,0:T(8,128)S(1)}, f32[1,128,128]{2,1,0:T(8,128)}, u32[]{:S(2)}) copy-start(f32[1,128,128]{2,1,0:T(8,128)} %kmap_ref.9) | copy-start | bytes 196612
  17.4 5.0 %copy-start.5 = (s32[128]{0:T(128)S(1)}, s32[128]{0:T(128)}, u32[]{:S(2)}) copy-start(s32[128]{0:T(128)} %param.9) | copy-start | bytes 1540
  17.4 5.0 %copy-start = (bf16[128,1024]{1,0:T(8,128)(2,1)S(1)}, bf16[128,1024]{1,0:T(8,128)(2,1)}, u32[]{:S(2)}) copy-start(bf16[128,1024]{1,0:T(8,128)(2,1)} %q_ref.7) | copy-start | bytes 786436
  17.4 8.6 %copy-start.1 = (f32[8,128,128]{2,1,0:T(8,128)S(1)}, f32[8,128,128]{2,1,0:T(8,128)}, u32[]{:S(2)}) copy-start(f32[8,128,128]{2,1,0:T(8,128)} %qmap_ref.3) | copy-start | bytes 1572868
  17.4 8.6 %collective-permute-start.5 = (bf16[1024,128]{1,0:T(8,128)(2,1)S(1)}, bf16[1024,128]{1,0:T(8,128)(2,1)S(1)}, u32[]{:S(2)}, u32[]{:S(2)}) collective-permute-start(bf16[1024,128]{1,0:T(8,128)(2,1)S(1)} %pad_maximum_fusion.rest_0_), channel_id=1, source_target_pairs={{0,64},{8,72},{16,80},{24,88},{32,96},{40,104},{48,112},{56,120},{... | collective-permute-start | bytes 786440 | tf_op jit(solution)/shard_map/ppermute | solution.py:426
  17.5 7.3 %collective-permute-start.6 = (bf16[512,128]{1,0:T(8,128)(2,1)S(1)}, bf16[512,128]{1,0:T(8,128)(2,1)S(1)}, u32[]{:S(2)}, u32[]{:S(2)}) collective-permute-start(bf16[512,128]{1,0:T(8,128)(2,1)S(1)} %get-tuple-element.79), channel_id=1, source_target_pairs={{0,8},{8,16},{16,24},{24,32},{32,40},{40,48},{48,56},{56,64},{64,7... | collective-permute-start | bytes 393224 | tf_op jit(solution)/shard_map/ppermute | solution.py:426
  17.6 7.2 %collective-permute-start.4 = (bf16[512,128]{1,0:T(8,128)(2,1)S(1)}, bf16[512,128]{1,0:T(8,128)(2,1)S(1)}, u32[]{:S(2)}, u32[]{:S(2)}) collective-permute-start(bf16[512,128]{1,0:T(8,128)(2,1)S(1)} %get-tuple-element.80), channel_id=1, source_target_pairs={{0,248},{8,0},{16,8},{24,16},{32,24},{40,32},{48,40},{56,48},{64,5... | collective-permute-start | bytes 393224 | tf_op jit(solution)/shard_map/ppermute | solution.py:426
  22.4 3.6 %copy-start.3 = (bf16[128,128]{1,0:T(8,128)(2,1)S(1)}, bf16[128,128]{1,0:T(8,128)(2,1)}, u32[]{:S(2)}) copy-start(bf16[128,128]{1,0:T(8,128)(2,1)} %k_ref.1) | copy-start | bytes 98308
  24.9 6.1 %collective-permute-start.7 = (bf16[512,128]{1,0:T(8,128)(2,1)S(1)}, bf16[512,128]{1,0:T(8,128)(2,1)S(1)}, u32[]{:S(2)}, u32[]{:S(2)}) collective-permute-start(bf16[512,128]{1,0:T(8,128)(2,1)S(1)} %collective-permute-done.6.rest_1_.rest_2_), channel_id=1, source_target_pairs={{0,64},{8,72},{16,80},{24,88},{32,96},{40,104},{48,112},{56,120},{... | collective-permute-start | bytes 393224 | tf_op jit(solution)/shard_map/ppermute | solution.py:426
  26.0 6.3 %collective-permute-start.8 = (bf16[512,128]{1,0:T(8,128)(2,1)S(1)}, bf16[512,128]{1,0:T(8,128)(2,1)S(1)}, u32[]{:S(2)}, u32[]{:S(2)}) collective-permute-start(bf16[512,128]{1,0:T(8,128)(2,1)S(1)} %collective-permute-done.4.rest_2_.rest_3_), channel_id=1, source_target_pairs={{0,64},{8,72},{16,80},{24,88},{32,96},{40,104},{48,112},{56,120},{... | collective-permute-start | bytes 393224 | tf_op jit(solution)/shard_map/ppermute | solution.py:426
  41.4 20.4 %all-to-all-start = ((f32[32,48,128]{2,1,0:T(8,128)}), f32[32,48,128]{2,1,0:T(8,128)S(1)}, u32[]{:S(2)}, u32[]{:S(2)}) async-start(f32[32,48,128]{2,1,0:T(8,128)} %get-tuple-element.70), calls=%async_computation | async-start | bytes 1572864 | tf_op jit(solution)/shard_map/all_to_all | solution.py:464
  81.7 16.2 %all-to-all-start.2 = ((f32[8,8,128]{2,1,0:T(8,128)}), f32[8,8,128]{2,1,0:T(8,128)S(1)}, u32[]{:S(2)}, u32[]{:S(2)}) async-start(f32[8,8,128]{2,1,0:T(8,128)} %head_squares.1), calls=%async_computation.2 | async-start | bytes 65536 | tf_op jit(solution)/shard_map/all_to_all | solution.py:477
  93.1 1.5 %copy-start.4 = (bf16[128,128]{1,0:T(8,128)(2,1)S(1)}, bf16[128,128]{1,0:T(8,128)(2,1)}, u32[]{:S(2)}) copy-start(bf16[128,128]{1,0:T(8,128)(2,1)} %v_ref.1) | copy-start | bytes 98308
